TPU v7x, 256 devices: a whole 4x4x8 slice. The times are simulated.
256 devices in a mesh: ctx: 16 (over z, core), row: 4 (over y), col: 4 (over x).
Axes of the slice: x: 4, y: 4, z: 8, core: 2. Of those that a mesh axis runs over, the one named last changes fastest.
Arguments:
- output_grad: bfloat16 [8192, 8192], P('ctx', ('row', 'col')), may hold values from -6 to 6
- conv_out: bfloat16 [8192, 8192], P('ctx', ('row', 'col')), may hold values from -9 to 9
- input_mix: bfloat16 [8192, 4, 256], P('ctx'), may hold values from -0.15625 to 0.15625
- output_mix: bfloat16 [8192, 4, 256], P('ctx'), may hold values from -1 to 1
- step_size: float32 [128, 8192], P(('row', 'col'), 'ctx'), may hold values from 0.5 to 2
- log_decay: float32 [128, 8192], P(('row', 'col'), 'ctx'), may hold values from -2.1 to 0, as said below
- skip_gain: float32 [128], P(('row', 'col')), may hold values from 0.5 to 2
- conv_weight: float32 [4, 8192], P(None, ('row', 'col')), may hold values from -3 to 3
- later_grad: float32 [128, 64, 256], P(('row', 'col')), may hold values from -32 to 32
- proj_weight: bfloat16 [8192, 8192], P('col', 'row'), may hold values from -0.0625 to 0.0625
Outputs:
- hidden_grad: bfloat16 [8192, 8192], P('ctx', ('col', 'row'))
- x_grad: bfloat16 [8192, 8192], P('ctx', ('row', 'col'))
- state_grad: float32 [16, 128, 64, 256], P('ctx', ('row', 'col'))
Inputs may be any that keep to these rules, and one draw needn't show every extreme that they name: `log_decay`: the forward pass's log decay of each head at each token.
All inputs are finite; a program needn't handle non-finite values.
Results may differ from a plain program's by a relative error of at most 0.022.
Values may be sent and summed in bfloat16 or wider, within the bound.
No kernel may reach another device: no remote copies, remote signals or barrier semaphores. Data moves between devices by JAX's collectives and lax.ppermute only.
A program may use at most 128 MiB of HBM per device.

v0:
```python
import jax
import jax.numpy as jnp
from jax import lax
from jax.sharding import PartitionSpec as P

HD = 64
HPG = 32
KW = 4


def from_behind(value, axis, steps):
    count = lax.axis_size(axis)
    first, last = (max(0, -steps), min(count, count - steps))
    return lax.ppermute(value, axis, [(source, source + steps) for source in range(first, last)])


def on_device(
    output_grad,
    conv_out,
    input_mix,
    output_mix,
    step_size,
    log_decay,
    skip_gain,
    conv_weight,
    later_grad,
    proj_weight,
):
    tokens_dev = output_grad.shape[0]
    heads_dev = step_size.shape[0]
    head_block = lax.axis_index("row") * lax.axis_size("col") + lax.axis_index("col")
    group = head_block * heads_dev // HPG
    write_rows = lax.dynamic_index_in_dim(input_mix, group, 1, keepdims=False)
    read_rows = lax.dynamic_index_in_dim(output_mix, group, 1, keepdims=False)
    cumulative = jnp.cumsum(log_decay, axis=1)
    block_end = cumulative[:, -1]
    decays = jnp.exp(block_end)
    per_head = output_grad.reshape(tokens_dev, heads_dev, HD)
    weighted = (jnp.exp(cumulative).T[:, :, None] * per_head.astype(jnp.float32)).astype(
        jnp.bfloat16
    )
    block_sum = jnp.einsum("shd,sn->hdn", weighted, read_rows, preferred_element_type=jnp.float32)
    is_last = lax.axis_index("ctx") == lax.axis_size("ctx") - 1

    def chain_turn(turn_index, estimate):
        passed = from_behind(
            (block_sum + decays[:, None, None] * estimate).astype(jnp.bfloat16), "ctx", -1
        ).astype(jnp.float32)
        return jnp.where(is_last, later_grad, passed)

    carried = lax.fori_loop(
        0,
        lax.axis_size("ctx") - 1,
        chain_turn,
        jnp.where(is_last, later_grad, jnp.zeros_like(later_grad)),
    )
    state_start = block_sum + decays[:, None, None] * carried
    scores = jnp.dot(write_rows, read_rows.T, preferred_element_type=jnp.float32)
    positions = jnp.arange(tokens_dev)
    causal = positions[None, :] >= positions[:, None]
    offsets = cumulative[:, None, :] - cumulative[:, :, None]
    mixing = (jnp.exp(jnp.where(causal[None], offsets, -jnp.inf)) * scores[None]).astype(
        jnp.bfloat16
    )
    intra = jnp.einsum("hts,shd->thd", mixing, per_head, preferred_element_type=jnp.float32)
    inter = jnp.einsum(
        "hdn,tn->thd", carried, write_rows.astype(jnp.float32), precision=lax.Precision.HIGHEST
    )
    inter = inter * jnp.exp(block_end[:, None] - cumulative).T[:, :, None]
    input_grad = step_size.T[:, :, None] * (intra + inter) + skip_gain[
        None, :, None
    ] * per_head.astype(jnp.float32)
    flat_grad = input_grad.reshape(tokens_dev, heads_dev * HD)
    activated = conv_out.astype(jnp.float32)
    sigma = jax.nn.sigmoid(activated)
    pre_grad = (flat_grad * sigma * (1.0 + activated * (1.0 - sigma))).astype(jnp.bfloat16)
    rim_rows = from_behind(pre_grad[: KW - 1], "ctx", -1)
    extended = jnp.concatenate([pre_grad, rim_rows], axis=0).astype(jnp.float32)
    accum = jnp.zeros(pre_grad.shape, jnp.float32)
    for tap in range(KW):
        accum = accum + conv_weight[tap][None, :] * extended[tap : tap + tokens_dev]
    x_grad = accum.astype(jnp.bfloat16)
    partial_grad = lax.dot_general(
        lax.all_gather(x_grad, "col", axis=1, tiled=True),
        proj_weight,
        (((1,), (1,)), ((), ())),
        preferred_element_type=jnp.float32,
    )
    hidden_grad = lax.psum_scatter(
        partial_grad.astype(jnp.bfloat16), "row", scatter_dimension=1, tiled=True
    )
    return (hidden_grad, x_grad, state_start[None])


def solution(mesh):
    return jax.shard_map(
        on_device,
        mesh=mesh,
        in_specs=(
            P("ctx", ("row", "col")),
            P("ctx", ("row", "col")),
            P("ctx", None, None),
            P("ctx", None, None),
            P(("row", "col"), "ctx"),
            P(("row", "col"), "ctx"),
            P(("row", "col")),
            P(None, ("row", "col")),
            P(("row", "col"), None, None),
            P("col", "row"),
        ),
        out_specs=(
            P("ctx", ("col", "row")),
            P("ctx", ("row", "col")),
            P("ctx", ("row", "col"), None, None),
        ),
        check_vma=False,
    )
```

profile of v0, /device:TPU:1, one launch (start us, length us, event | category | flops | bytes accessed | tf_op | source)
XLA Modules:
  0.0 251.9 jit_solution(11634387616972478772)
XLA Ops:
  7.2 2.3 reduce-window.6
  9.5 0.2 slice_reduce_fusion
  9.8 0.2 slice_reduce_fusion.1
  10.1 1.3 copy.26
  11.5 2.6 %constant_dynamic-slice_fusion = (bf16[512,1,256]{2,1,0:T(2,128)(2,1)S(1)}, bf16[512,1,256]{2,1,0:T(2,128)(2,1)S(1)}) fusion(bf16[512,4,256]{2,1,0:T(4,128)(2,1)} %param.15, s32[]{:T(128)S(6)} %select_n.30, bf16[512,4,256]{2,1,0:T(4,128)(2,1)} %param.14), kind=kLoop, calls=%fused_computation.48 | loop fusion | bytes 1048580 | tf_op jit(solution)/shard_map/jit(dynamic_index_in_dim)/dynamic_slice | solution.py:34
  14.1 0.3 fusion.17
  14.5 1.3 fusion.20
  15.8 4.3 %fusion.2 = f32[512,8,64]{0,2,1:T(8,128)} fusion(bf16[512,8,64]{0,2,1:T(8,128)(2,1)S(1)} %bitcast.41, f32[512,512]{1,0:T(8,128)} %fusion.20, f32[8,512]{1,0:T(8,128)S(1)} %get-tuple-element.49, pred[512,512]{1,0:T(8,128)(4,1)S(1)} %iota_compare_fusion), kind=kOutput, calls=%fused_computation.6 | convolution fusion | flops 276824064 | bytes 2899968 | tf_op jit(solution)/shard_map/hts,shd->thd/dot_general | solution.py:65
  20.1 119.6 %while.10 = (s32[]{:T(128)}, f32[8,64,256]{2,1,0:T(8,128)S(1)}, pred[]{:T(512)}, f32[8]{0:T(128)S(1)}, f32[8,64,256]{2,1,0:T(8,128)S(1)}, /*index=5*/f32[8,64,256]{2,1,0:T(8,128)S(1)}, s32[]{:T(128)}) while((s32[]{:T(128)}, f32[8,64,256]{2,1,0:T(8,128)S(1)}, pred[]{:T(512)}, f32[8]{0:T(128)S(1)}, f32[8,64,256]{2,1,0:T(8,128)S(1)}, ...), condition=%wide.region_3.4_spmd, body=%wide.region_2.3_spmd.sunk | while | flops 655362 | bytes 3670166 | solution.py:51
  20.2 5.2 %collective-permute-start = (bf16[8,64,256]{2,1,0:T(8,128)(2,1)S(1)}, bf16[8,64,256]{2,1,0:T(8,128)(2,1)S(1)}, u32[]{:S(2)}, u32[]{:S(2)}) collective-permute-start(bf16[8,64,256]{2,1,0:T(8,128)(2,1)S(1)} %add_convert_fusion.2), channel_id=1, source_target_pairs={{16,0},{32,16},{48,32},{64,48},{80,64},{96,80},{112,96},{128,112},... | collective-permute-start | bytes 786440 | tf_op jit(solution)/shard_map/while/body/eval_jaxpr/ppermute | solution.py:14
  25.4 3.8 %collective-permute-done = bf16[8,64,256]{2,1,0:T(8,128)(2,1)S(1)} collective-permute-done((bf16[8,64,256]{2,1,0:T(8,128)(2,1)S(1)}, bf16[8,64,256]{2,1,0:T(8,128)(2,1)S(1)}, u32[]{:S(2)}, u32[]{:S(2)}) %collective-permute-start) | collective-permute-done | bytes 262176 | tf_op jit(solution)/shard_map/while/body/eval_jaxpr/ppermute | solution.py:14
  29.3 0.1 add_convert_fusion.2
  29.4 1.9 collective-permute-start
  31.3 5.8 %collective-permute-done = bf16[8,64,256]{2,1,0:T(8,128)(2,1)S(1)} collective-permute-done((bf16[8,64,256]{2,1,0:T(8,128)(2,1)S(1)}, bf16[8,64,256]{2,1,0:T(8,128)(2,1)S(1)}, u32[]{:S(2)}, u32[]{:S(2)}) %collective-permute-start) | collective-permute-done | bytes 262176 | tf_op jit(solution)/shard_map/while/body/eval_jaxpr/ppermute | solution.py:14
  37.2 0.1 add_convert_fusion.2
  37.3 1.9 collective-permute-start
  39.2 5.8 %collective-permute-done = bf16[8,64,256]{2,1,0:T(8,128)(2,1)S(1)} collective-permute-done((bf16[8,64,256]{2,1,0:T(8,128)(2,1)S(1)}, bf16[8,64,256]{2,1,0:T(8,128)(2,1)S(1)}, u32[]{:S(2)}, u32[]{:S(2)}) %collective-permute-start) | collective-permute-done | bytes 262176 | tf_op jit(solution)/shard_map/while/body/eval_jaxpr/ppermute | solution.py:14
  45.0 0.1 add_convert_fusion.2
  45.2 1.9 collective-permute-start
  47.1 5.8 %collective-permute-done = bf16[8,64,256]{2,1,0:T(8,128)(2,1)S(1)} collective-permute-done((bf16[8,64,256]{2,1,0:T(8,128)(2,1)S(1)}, bf16[8,64,256]{2,1,0:T(8,128)(2,1)S(1)}, u32[]{:S(2)}, u32[]{:S(2)}) %collective-permute-start) | collective-permute-done | bytes 262176 | tf_op jit(solution)/shard_map/while/body/eval_jaxpr/ppermute | solution.py:14
  52.9 0.1 add_convert_fusion.2
  53.1 1.9 collective-permute-start
  55.0 5.8 %collective-permute-done = bf16[8,64,256]{2,1,0:T(8,128)(2,1)S(1)} collective-permute-done((bf16[8,64,256]{2,1,0:T(8,128)(2,1)S(1)}, bf16[8,64,256]{2,1,0:T(8,128)(2,1)S(1)}, u32[]{:S(2)}, u32[]{:S(2)}) %collective-permute-start) | collective-permute-done | bytes 262176 | tf_op jit(solution)/shard_map/while/body/eval_jaxpr/ppermute | solution.py:14
  60.8 0.1 add_convert_fusion.2
  60.9 1.9 collective-permute-start
  62.9 5.8 %collective-permute-done = bf16[8,64,256]{2,1,0:T(8,128)(2,1)S(1)} collective-permute-done((bf16[8,64,256]{2,1,0:T(8,128)(2,1)S(1)}, bf16[8,64,256]{2,1,0:T(8,128)(2,1)S(1)}, u32[]{:S(2)}, u32[]{:S(2)}) %collective-permute-start) | collective-permute-done | bytes 262176 | tf_op jit(solution)/shard_map/while/body/eval_jaxpr/ppermute | solution.py:14
  68.7 0.1 add_convert_fusion.2
  68.8 1.9 collective-permute-start
  70.8 5.8 %collective-permute-done = bf16[8,64,256]{2,1,0:T(8,128)(2,1)S(1)} collective-permute-done((bf16[8,64,256]{2,1,0:T(8,128)(2,1)S(1)}, bf16[8,64,256]{2,1,0:T(8,128)(2,1)S(1)}, u32[]{:S(2)}, u32[]{:S(2)}) %collective-permute-start) | collective-permute-done | bytes 262176 | tf_op jit(solution)/shard_map/while/body/eval_jaxpr/ppermute | solution.py:14
  76.6 0.1 add_convert_fusion.2
  76.7 1.9 collective-permute-start
  78.6 5.8 %collective-permute-done = bf16[8,64,256]{2,1,0:T(8,128)(2,1)S(1)} collective-permute-done((bf16[8,64,256]{2,1,0:T(8,128)(2,1)S(1)}, bf16[8,64,256]{2,1,0:T(8,128)(2,1)S(1)}, u32[]{:S(2)}, u32[]{:S(2)}) %collective-permute-start) | collective-permute-done | bytes 262176 | tf_op jit(solution)/shard_map/while/body/eval_jaxpr/ppermute | solution.py:14
  84.5 0.1 add_convert_fusion.2
  84.6 1.9 collective-permute-start
  86.5 5.8 %collective-permute-done = bf16[8,64,256]{2,1,0:T(8,128)(2,1)S(1)} collective-permute-done((bf16[8,64,256]{2,1,0:T(8,128)(2,1)S(1)}, bf16[8,64,256]{2,1,0:T(8,128)(2,1)S(1)}, u32[]{:S(2)}, u32[]{:S(2)}) %collective-permute-start) | collective-permute-done | bytes 262176 | tf_op jit(solution)/shard_map/while/body/eval_jaxpr/ppermute | solution.py:14
  92.4 0.1 add_convert_fusion.2
  92.5 1.9 collective-permute-start
  94.4 5.8 %collective-permute-done = bf16[8,64,256]{2,1,0:T(8,128)(2,1)S(1)} collective-permute-done((bf16[8,64,256]{2,1,0:T(8,128)(2,1)S(1)}, bf16[8,64,256]{2,1,0:T(8,128)(2,1)S(1)}, u32[]{:S(2)}, u32[]{:S(2)}) %collective-permute-start) | collective-permute-done | bytes 262176 | tf_op jit(solution)/shard_map/while/body/eval_jaxpr/ppermute | solution.py:14
  100.3 0.1 add_convert_fusion.2
  100.4 1.9 collective-permute-start
  102.3 5.8 %collective-permute-done = bf16[8,64,256]{2,1,0:T(8,128)(2,1)S(1)} collective-permute-done((bf16[8,64,256]{2,1,0:T(8,128)(2,1)S(1)}, bf16[8,64,256]{2,1,0:T(8,128)(2,1)S(1)}, u32[]{:S(2)}, u32[]{:S(2)}) %collective-permute-start) | collective-permute-done | bytes 262176 | tf_op jit(solution)/shard_map/while/body/eval_jaxpr/ppermute | solution.py:14
  108.1 0.1 add_convert_fusion.2
  108.3 1.9 collective-permute-start
  110.2 5.8 %collective-permute-done = bf16[8,64,256]{2,1,0:T(8,128)(2,1)S(1)} collective-permute-done((bf16[8,64,256]{2,1,0:T(8,128)(2,1)S(1)}, bf16[8,64,256]{2,1,0:T(8,128)(2,1)S(1)}, u32[]{:S(2)}, u32[]{:S(2)}) %collective-permute-start) | collective-permute-done | bytes 262176 | tf_op jit(solution)/shard_map/while/body/eval_jaxpr/ppermute | solution.py:14
  116.0 0.1 add_convert_fusion.2
  116.2 1.9 collective-permute-start
  118.1 5.8 %collective-permute-done = bf16[8,64,256]{2,1,0:T(8,128)(2,1)S(1)} collective-permute-done((bf16[8,64,256]{2,1,0:T(8,128)(2,1)S(1)}, bf16[8,64,256]{2,1,0:T(8,128)(2,1)S(1)}, u32[]{:S(2)}, u32[]{:S(2)}) %collective-permute-start) | collective-permute-done | bytes 262176 | tf_op jit(solution)/shard_map/while/body/eval_jaxpr/ppermute | solution.py:14
  123.9 0.1 add_convert_fusion.2
  124.0 1.9 collective-permute-start
  126.0 5.8 %collective-permute-done = bf16[8,64,256]{2,1,0:T(8,128)(2,1)S(1)} collective-permute-done((bf16[8,64,256]{2,1,0:T(8,128)(2,1)S(1)}, bf16[8,64,256]{2,1,0:T(8,128)(2,1)S(1)}, u32[]{:S(2)}, u32[]{:S(2)}) %collective-permute-start) | collective-permute-done | bytes 262176 | tf_op jit(solution)/shard_map/while/body/eval_jaxpr/ppermute | solution.py:14
  131.8 0.1 add_convert_fusion.2
  131.9 1.9 collective-permute-start
  133.9 5.8 %collective-permute-done = bf16[8,64,256]{2,1,0:T(8,128)(2,1)S(1)} collective-permute-done((bf16[8,64,256]{2,1,0:T(8,128)(2,1)S(1)}, bf16[8,64,256]{2,1,0:T(8,128)(2,1)S(1)}, u32[]{:S(2)}, u32[]{:S(2)}) %collective-permute-start) | collective-permute-done | bytes 262176 | tf_op jit(solution)/shard_map/while/body/eval_jaxpr/ppermute | solution.py:14
  139.7 2.0 fusion.5
  141.7 0.3 copy.28
  142.0 1.4 fusion.11
  143.5 1.9 collective-permute-start.1
  145.5 3.0 %collective-permute-done.1 = bf16[3,512]{1,0:T(4,128)(2,1)S(1)} collective-permute-done((bf16[3,512]{1,0:T(4,128)(2,1)S(1)}, bf16[3,512]{1,0:T(4,128)(2,1)S(1)}, u32[]{:S(2)}, u32[]{:S(2)}) %collective-permute-start.1) | collective-permute-done | bytes 3104 | tf_op jit(solution)/shard_map/ppermute | solution.py:14
  148.4 0.1 maximum_convert_fusion
  148.6 1.3 fusion.13
  149.9 52.7 %all-gather.2.cloned.1.call-done = bf16[512,2048]{1,0:T(8,128)(2,1)} async-done(((bf16[512,512]{1,0:T(8,128)(2,1)}), bf16[512,2048]{1,0:T(8,128)(2,1)}) %all-gather.2.cloned.1.call-update) | async-done | bytes 2097168 | tf_op jit(solution)/shard_map/all_gather | solution.py:84
  202.6 9.9 %convolution_convert_fusion = bf16[512,2048]{1,0:T(8,128)(2,1)} fusion(bf16[512,2048]{1,0:T(8,128)(2,1)} %all-gather.2.cloned.1.call-done, bf16[2048,2048]{1,0:T(8,128)(2,1)} %param.21), kind=kOutput, calls=%fused_computation.5 | convolution fusion | flops 4296015872 | bytes 12582912 | tf_op jit(solution)/shard_map/dot_general | solution.py:83
  212.5 0.9 add_bitcast_fusion
  213.4 31.6 %reduce-scatter.2.cloned.1.call-done = bf16[512,512]{1,0:T(8,128)(2,1)} async-done(((bf16[512,2048]{1,0:T(8,128)(2,1)}), bf16[512,512]{1,0:T(8,128)(2,1)}) %reduce-scatter.2.cloned.1.call-update) | async-done | bytes 524304 | tf_op jit(solution)/shard_map/reduce_scatter | solution.py:89
  (38 shorter events, 1.5 us)
Async XLA Ops:
  7.2 8.6 %copy-start = (f32[8,64,256]{2,1,0:T(8,128)S(1)}, f32[8,64,256]{2,1,0:T(8,128)}, u32[]{:S(2)}) copy-start(f32[8,64,256]{2,1,0:T(8,128)} %param.20) | copy-start | bytes 1572868
  7.2 195.4 %all-gather.2.cloned.1.call-start = ((), (), s32[]{:S(2)}) async-start(), calls=%async_computation.1 | async-start | bytes 2621440 | tf_op jit(solution)/shard_map/all_gather | solution.py:84
  20.1 119.6 %copy-start.1 = (f32[8,512]{1,0:T(8,128)S(1)}, f32[8,512]{1,0:T(8,128)}, u32[]{:S(2)}) copy-start(f32[8,512]{1,0:T(8,128)} %param.16) | copy-start | bytes 49156
  20.1 119.6 %copy-start.3 = (f32[8]{0:T(128)S(1)}, f32[8]{0:T(128)}, u32[]{:S(2)}) copy-start(f32[8]{0:T(128)} %param.18) | copy-start | bytes 100
  20.2 9.0 %collective-permute-start = (bf16[8,64,256]{2,1,0:T(8,128)(2,1)S(1)}, bf16[8,64,256]{2,1,0:T(8,128)(2,1)S(1)}, u32[]{:S(2)}, u32[]{:S(2)}) collective-permute-start(bf16[8,64,256]{2,1,0:T(8,128)(2,1)S(1)} %add_convert_fusion.2), channel_id=1, source_target_pairs={{16,0},{32,16},{48,32},{64,48},{80,64},{96,80},{112,96},{128,112},... | collective-permute-start | bytes 786440 | tf_op jit(solution)/shard_map/while/body/eval_jaxpr/ppermute | solution.py:14
  29.4 7.7 %collective-permute-start = (bf16[8,64,256]{2,1,0:T(8,128)(2,1)S(1)}, bf16[8,64,256]{2,1,0:T(8,128)(2,1)S(1)}, u32[]{:S(2)}, u32[]{:S(2)}) collective-permute-start(bf16[8,64,256]{2,1,0:T(8,128)(2,1)S(1)} %add_convert_fusion.2), channel_id=1, source_target_pairs={{16,0},{32,16},{48,32},{64,48},{80,64},{96,80},{112,96},{128,112},... | collective-permute-start | bytes 786440 | tf_op jit(solution)/shard_map/while/body/eval_jaxpr/ppermute | solution.py:14
  37.3 7.7 %collective-permute-start = (bf16[8,64,256]{2,1,0:T(8,128)(2,1)S(1)}, bf16[8,64,256]{2,1,0:T(8,128)(2,1)S(1)}, u32[]{:S(2)}, u32[]{:S(2)}) collective-permute-start(bf16[8,64,256]{2,1,0:T(8,128)(2,1)S(1)} %add_convert_fusion.2), channel_id=1, source_target_pairs={{16,0},{32,16},{48,32},{64,48},{80,64},{96,80},{112,96},{128,112},... | collective-permute-start | bytes 786440 | tf_op jit(solution)/shard_map/while/body/eval_jaxpr/ppermute | solution.py:14
  45.2 7.7 %collective-permute-start = (bf16[8,64,256]{2,1,0:T(8,128)(2,1)S(1)}, bf16[8,64,256]{2,1,0:T(8,128)(2,1)S(1)}, u32[]{:S(2)}, u32[]{:S(2)}) collective-permute-start(bf16[8,64,256]{2,1,0:T(8,128)(2,1)S(1)} %add_convert_fusion.2), channel_id=1, source_target_pairs={{16,0},{32,16},{48,32},{64,48},{80,64},{96,80},{112,96},{128,112},... | collective-permute-start | bytes 786440 | tf_op jit(solution)/shard_map/while/body/eval_jaxpr/ppermute | solution.py:14
  53.1 7.7 %collective-permute-start = (bf16[8,64,256]{2,1,0:T(8,128)(2,1)S(1)}, bf16[8,64,256]{2,1,0:T(8,128)(2,1)S(1)}, u32[]{:S(2)}, u32[]{:S(2)}) collective-permute-start(bf16[8,64,256]{2,1,0:T(8,128)(2,1)S(1)} %add_convert_fusion.2), channel_id=1, source_target_pairs={{16,0},{32,16},{48,32},{64,48},{80,64},{96,80},{112,96},{128,112},... | collective-permute-start | bytes 786440 | tf_op jit(solution)/shard_map/while/body/eval_jaxpr/ppermute | solution.py:14
  60.9 7.7 %collective-permute-start = (bf16[8,64,256]{2,1,0:T(8,128)(2,1)S(1)}, bf16[8,64,256]{2,1,0:T(8,128)(2,1)S(1)}, u32[]{:S(2)}, u32[]{:S(2)}) collective-permute-start(bf16[8,64,256]{2,1,0:T(8,128)(2,1)S(1)} %add_convert_fusion.2), channel_id=1, source_target_pairs={{16,0},{32,16},{48,32},{64,48},{80,64},{96,80},{112,96},{128,112},... | collective-permute-start | bytes 786440 | tf_op jit(solution)/shard_map/while/body/eval_jaxpr/ppermute | solution.py:14
  68.8 7.7 %collective-permute-start = (bf16[8,64,256]{2,1,0:T(8,128)(2,1)S(1)}, bf16[8,64,256]{2,1,0:T(8,128)(2,1)S(1)}, u32[]{:S(2)}, u32[]{:S(2)}) collective-permute-start(bf16[8,64,256]{2,1,0:T(8,128)(2,1)S(1)} %add_convert_fusion.2), channel_id=1, source_target_pairs={{16,0},{32,16},{48,32},{64,48},{80,64},{96,80},{112,96},{128,112},... | collective-permute-start | bytes 786440 | tf_op jit(solution)/shard_map/while/body/eval_jaxpr/ppermute | solution.py:14
  76.7 7.7 %collective-permute-start = (bf16[8,64,256]{2,1,0:T(8,128)(2,1)S(1)}, bf16[8,64,256]{2,1,0:T(8,128)(2,1)S(1)}, u32[]{:S(2)}, u32[]{:S(2)}) collective-permute-start(bf16[8,64,256]{2,1,0:T(8,128)(2,1)S(1)} %add_convert_fusion.2), channel_id=1, source_target_pairs={{16,0},{32,16},{48,32},{64,48},{80,64},{96,80},{112,96},{128,112},... | collective-permute-start | bytes 786440 | tf_op jit(solution)/shard_map/while/body/eval_jaxpr/ppermute | solution.py:14
  84.6 7.7 %collective-permute-start = (bf16[8,64,256]{2,1,0:T(8,128)(2,1)S(1)}, bf16[8,64,256]{2,1,0:T(8,128)(2,1)S(1)}, u32[]{:S(2)}, u32[]{:S(2)}) collective-permute-start(bf16[8,64,256]{2,1,0:T(8,128)(2,1)S(1)} %add_convert_fusion.2), channel_id=1, source_target_pairs={{16,0},{32,16},{48,32},{64,48},{80,64},{96,80},{112,96},{128,112},... | collective-permute-start | bytes 786440 | tf_op jit(solution)/shard_map/while/body/eval_jaxpr/ppermute | solution.py:14
  92.5 7.7 %collective-permute-start = (bf16[8,64,256]{2,1,0:T(8,128)(2,1)S(1)}, bf16[8,64,256]{2,1,0:T(8,128)(2,1)S(1)}, u32[]{:S(2)}, u32[]{:S(2)}) collective-permute-start(bf16[8,64,256]{2,1,0:T(8,128)(2,1)S(1)} %add_convert_fusion.2), channel_id=1, source_target_pairs={{16,0},{32,16},{48,32},{64,48},{80,64},{96,80},{112,96},{128,112},... | collective-permute-start | bytes 786440 | tf_op jit(solution)/shard_map/while/body/eval_jaxpr/ppermute | solution.py:14
  100.4 7.7 %collective-permute-start = (bf16[8,64,256]{2,1,0:T(8,128)(2,1)S(1)}, bf16[8,64,256]{2,1,0:T(8,128)(2,1)S(1)}, u32[]{:S(2)}, u32[]{:S(2)}) collective-permute-start(bf16[8,64,256]{2,1,0:T(8,128)(2,1)S(1)} %add_convert_fusion.2), channel_id=1, source_target_pairs={{16,0},{32,16},{48,32},{64,48},{80,64},{96,80},{112,96},{128,112},... | collective-permute-start | bytes 786440 | tf_op jit(solution)/shard_map/while/body/eval_jaxpr/ppermute | solution.py:14
  108.3 7.7 %collective-permute-start = (bf16[8,64,256]{2,1,0:T(8,128)(2,1)S(1)}, bf16[8,64,256]{2,1,0:T(8,128)(2,1)S(1)}, u32[]{:S(2)}, u32[]{:S(2)}) collective-permute-start(bf16[8,64,256]{2,1,0:T(8,128)(2,1)S(1)} %add_convert_fusion.2), channel_id=1, source_target_pairs={{16,0},{32,16},{48,32},{64,48},{80,64},{96,80},{112,96},{128,112},... | collective-permute-start | bytes 786440 | tf_op jit(solution)/shard_map/while/body/eval_jaxpr/ppermute | solution.py:14
  116.2 7.7 %collective-permute-start = (bf16[8,64,256]{2,1,0:T(8,128)(2,1)S(1)}, bf16[8,64,256]{2,1,0:T(8,128)(2,1)S(1)}, u32[]{:S(2)}, u32[]{:S(2)}) collective-permute-start(bf16[8,64,256]{2,1,0:T(8,128)(2,1)S(1)} %add_convert_fusion.2), channel_id=1, source_target_pairs={{16,0},{32,16},{48,32},{64,48},{80,64},{96,80},{112,96},{128,112},... | collective-permute-start | bytes 786440 | tf_op jit(solution)/shard_map/while/body/eval_jaxpr/ppermute | solution.py:14
  124.0 7.7 %collective-permute-start = (bf16[8,64,256]{2,1,0:T(8,128)(2,1)S(1)}, bf16[8,64,256]{2,1,0:T(8,128)(2,1)S(1)}, u32[]{:S(2)}, u32[]{:S(2)}) collective-permute-start(bf16[8,64,256]{2,1,0:T(8,128)(2,1)S(1)} %add_convert_fusion.2), channel_id=1, source_target_pairs={{16,0},{32,16},{48,32},{64,48},{80,64},{96,80},{112,96},{128,112},... | collective-permute-start | bytes 786440 | tf_op jit(solution)/shard_map/while/body/eval_jaxpr/ppermute | solution.py:14
  131.9 7.7 %collective-permute-start = (bf16[8,64,256]{2,1,0:T(8,128)(2,1)S(1)}, bf16[8,64,256]{2,1,0:T(8,128)(2,1)S(1)}, u32[]{:S(2)}, u32[]{:S(2)}) collective-permute-start(bf16[8,64,256]{2,1,0:T(8,128)(2,1)S(1)} %add_convert_fusion.2), channel_id=1, source_target_pairs={{16,0},{32,16},{48,32},{64,48},{80,64},{96,80},{112,96},{128,112},... | collective-permute-start | bytes 786440 | tf_op jit(solution)/shard_map/while/body/eval_jaxpr/ppermute | solution.py:14
  139.7 5.7 %copy-start.2 = (f32[4,512]{1,0:T(4,128)S(1)}, f32[4,512]{1,0:T(4,128)}, u32[]{:S(2)}) copy-start(f32[4,512]{1,0:T(4,128)} %param.19) | copy-start | bytes 24580
  143.5 4.9 %collective-permute-start.1 = (bf16[3,512]{1,0:T(4,128)(2,1)S(1)}, bf16[3,512]{1,0:T(4,128)(2,1)S(1)}, u32[]{:S(2)}, u32[]{:S(2)}) collective-permute-start(bf16[3,512]{1,0:T(4,128)(2,1)S(1)} %slice.50), channel_id=1, source_target_pairs={{16,0},{32,16},{48,32},{64,48},{80,64},{96,80},{112,96},{128,112},... | collective-permute-start | bytes 9224 | tf_op jit(solution)/shard_map/ppermute | solution.py:14
  149.8 95.2 %reduce-scatter.2.cloned.1.call-start = ((), (), s32[]{:S(2)}) async-start(), calls=%async_computation.2 | async-start | bytes 2621440 | tf_op jit(solution)/shard_map/reduce_scatter | solution.py:89
Sparse Core Ops, SparseCore 0:
  150.0 52.5 all-gather.1
  212.6 32.3 reduce-scatter.1
where the time goes:
time: 253 us; the launch traced here: 252 us
  waiting for transfers between devices  172 us (68%)
  starting transfers between devices  34 us (13%)
  matrix products  17.7 us (7%)
  between operations  14.2 us (6%)
  other arithmetic  8.98 us (4%)
  local copies, waits for them, and re-layouts  4.6 us (2%)
    ppermute x16, waiting for transfers between devices, from_behind(): lax.ppermute(value, axis, [(source, source + steps) for source in range(f...  87.5 us
    all_gather x1, waiting for transfers between devices, on_device(): lax.all_gather(x_grad, 'col', axis=1, tiled=True)  52.7 us
    ppermute x16, starting transfers between devices, from_behind(): lax.ppermute(value, axis, [(source, source + steps) for source in range(f...  34 us
    reduce_scatter x1, waiting for transfers between devices, on_device(): lax.psum_scatter(partial_grad.astype(jnp.bfloat16), 'row', scatter_dimens...  31.6 us
    dot_general x1, matrix products, on_device(): lax.dot_general(lax.all_gather(x_grad, 'col', axis=1, tiled=True), proj_w...  9.85 us
  transfers between devices with their start and end apart: 18, of which 18 were waited for; matrix products, arithmetic and copies ran while one was open for 0% of the time, Pallas kernels for 0%

commit v1 on v0

v1 whole, which is shorter than its diff:
```python
import jax
import jax.numpy as jnp
from jax import lax
from jax.experimental import pallas as pl
from jax.experimental.pallas import tpu as pltpu
from jax.sharding import PartitionSpec as P

HD = 64
HPG = 32
KW = 4
QUAD = 4
F32 = jnp.float32
BF16 = jnp.bfloat16
VMEM = pl.BlockSpec(memory_space=pltpu.VMEM)
SMEM = pl.BlockSpec(memory_space=pltpu.SMEM)


def struct(shape, dtype):
    return jax.ShapeDtypeStruct(shape, dtype)


def call(kernel, outs, args, scratch=(), flops=0, moved=0, smem=0):
    return pl.pallas_call(
        kernel,
        out_shape=outs,
        in_specs=[SMEM] * smem + [VMEM] * (len(args) - smem),
        out_specs=jax.tree.map(lambda unused: VMEM, outs),
        scratch_shapes=list(scratch),
        cost_estimate=pl.CostEstimate(flops=flops, bytes_accessed=moved, transcendentals=0),
        compiler_params=pltpu.CompilerParams(vmem_limit_bytes=40 << 20),
    )(*args)


def split3(value):
    high = value.astype(BF16)
    rest = value - high.astype(F32)
    middle = rest.astype(BF16)
    low = (rest - middle.astype(F32)).astype(BF16)
    return high, middle, low


def over_columns(per_head):
    heads = per_head.shape[0]
    stacked = jnp.concatenate([part.astype(F32) for part in split3(per_head)], axis=0).astype(BF16)
    row = lax.broadcasted_iota(jnp.int32, (3 * heads, heads * HD), 0)
    column = lax.broadcasted_iota(jnp.int32, (3 * heads, heads * HD), 1)
    picks = (lax.rem(row, heads) == column // HD).astype(F32).astype(BF16)
    return lax.dot_general(stacked, picks, (((0,), (0,)), ((), ())), preferred_element_type=F32)


def decay_rows(per_head):
    wide = jnp.broadcast_to(per_head, (per_head.shape[0], 256))
    high = wide.astype(BF16)
    low = (wide - high.astype(F32)).astype(BF16)
    return jnp.concatenate([high.astype(F32), low.astype(F32)], axis=0).astype(BF16)


def block_kernel(where, grad, reads, log_decay, sums, cumulative, decays, one, two, three):
    heads, tokens = log_decay.shape
    part = HD // QUAD
    total = log_decay[...]
    lane = lax.broadcasted_iota(jnp.int32, (heads, tokens), 1)
    step = 1
    while step < tokens:
        total = total + jnp.where(lane >= step, pltpu.roll(total, step, 1), 0.0)
        step *= 2
    cumulative[...] = total
    last = jnp.exp(total[:, tokens - 1 : tokens])
    decays[...] = jnp.broadcast_to(last, decays.shape)
    weighted = (over_columns(jnp.exp(total)) * grad[...].astype(F32)).astype(BF16)
    sums[...] = lax.dot_general(
        weighted, reads[...], (((0,), (0,)), ((), ())), preferred_element_type=F32
    )
    rows = decay_rows(last)
    me = where[0]
    for flip, sent in ((1, one), (2, two), (3, three)):
        quarter = jnp.bitwise_xor(me, flip)
        for head in range(heads):
            start = pl.multiple_of(head * HD + quarter * part, part)
            sent[head] = sums[pl.ds(start, part), :].astype(BF16)
        sent[heads] = rows


def intra_kernel(
    grad, writes, reads, cumulative, step_size, skip_row, conv_out, fixed, slope, scores, steps
):
    heads, tokens = cumulative.shape
    half = tokens // 2
    scores[...] = lax.dot_general(
        writes[...], reads[...], (((1,), (1,)), ((), ())), preferred_element_type=F32
    )
    total = cumulative[...]
    columns = jnp.transpose(total)
    steps[...] = over_columns(step_size[...])
    slope[...] = over_columns(
        step_size[...] * jnp.exp(total[:, tokens - 1 : tokens] - total)
    )
    causal = lax.broadcasted_iota(jnp.int32, (half, half), 1) >= lax.broadcasted_iota(
        jnp.int32, (half, half), 0
    )
    lane = lax.broadcasted_iota(jnp.int32, (half, 2 * HD), 1)
    for pair in range(heads // 2):
        span = slice(pair * 2 * HD, (pair + 1) * 2 * HD)
        for at in range(2):
            rows = slice(at * half, (at + 1) * half)
            both = []
            for head in (2 * pair, 2 * pair + 1):
                own = columns[rows, head : head + 1]
                offsets = total[head : head + 1, rows] - own
                mixing = (
                    jnp.exp(jnp.where(causal, offsets, -jnp.inf)) * scores[rows, rows]
                ).astype(BF16)
                sums = jnp.dot(mixing, grad[rows, span], preferred_element_type=F32)
                if at == 0:
                    later = slice(half, tokens)
                    mixing = (
                        jnp.exp(total[head : head + 1, later] - own) * scores[rows, later]
                    ).astype(BF16)
                    sums = sums + jnp.dot(mixing, grad[later, span], preferred_element_type=F32)
                both.append(sums)
            intra = jnp.where(lane < HD, both[0], both[1])
            activated = conv_out[rows, span].astype(F32)
            sigma = 1.0 / (1.0 + jnp.exp(-activated))
            gate = sigma * (1.0 + activated * (1.0 - sigma))
            fixed[rows, span] = gate * (
                steps[rows, span] * intra + skip_row[:, span] * grad[rows, span].astype(F32)
            )
            slope[rows, span] = gate * slope[rows, span]


def gather_quad(me, sums, decays, received, values, scales):
    heads = decays.shape[0]
    part = HD // QUAD
    for head in range(heads):
        start = pl.multiple_of(head * HD + me * part, part)
        values[me, head] = sums[pl.ds(start, part), :]
    scales[me] = decays[...]
    for flip, came in enumerate(received, 1):
        other = jnp.bitwise_xor(me, flip)
        for head in range(heads):
            values[other, head] = came[head].astype(F32)
        tail = came[heads].astype(F32)
        scales[other] = tail[:heads] + tail[heads:]


def quad_kernel(where, sums, decays, one, two, three, sent, values, scales):
    heads = decays.shape[0]
    gather_quad(where[0], sums, decays, (one, two, three), values, scales)
    for head in range(heads):
        total = values[3, head]
        for block in (2, 1, 0):
            total = values[block, head] + scales[block][head : head + 1] * total
        sent[head] = total.astype(BF16)
    product = scales[0] * scales[1] * scales[2] * scales[3]
    high = product.astype(BF16).astype(F32)
    sent[heads] = jnp.concatenate([high, product - high], axis=0).astype(BF16)


def carry_kernel(
    where, sums, decays, one, two, three, near, middle, far, later, own, first, second, third,
    values, scales, carries,
):
    heads = decays.shape[0]
    part = HD // QUAD
    me, quad = where[0], where[1]
    gather_quad(me, sums, decays, (one, two, three), values, scales)
    jumps = []
    for ahead, came in ((3, far), (2, middle), (1, near)):
        tail = came[heads].astype(F32)
        present = jnp.full(decays.shape, quad + ahead, jnp.int32) < QUAD
        jumps.append((came, jnp.where(present, tail[:heads] + tail[heads:], 1.0)))
    for head in range(heads):
        start = pl.multiple_of(head * HD + me * part, part)
        carry = later[pl.ds(start, part), :]
        for came, scale in jumps:
            carry = came[head].astype(F32) + scale[head : head + 1] * carry
        carries[3, head] = carry
        for block in (3, 2, 1):
            carry = values[block, head] + scales[block][head : head + 1] * carry
            carries[block - 1, head] = carry
    for head in range(heads):
        own[head] = carries[me, head]
        for flip, sent in ((1, first), (2, second), (3, third)):
            sent[head] = carries[jnp.bitwise_xor(me, flip), head].astype(BF16)


def join_kernel(
    where, sums, decays, own, first, second, third, writes, fixed, slope, taps,
    state, rim, chunk, rest, carried, pre,
):
    heads = decays.shape[0]
    part = HD // QUAD
    tokens = fixed.shape[0]
    half = tokens // 2
    me = where[0]
    for flip, came in ((0, own), (1, first), (2, second), (3, third)):
        quarter = jnp.bitwise_xor(me, flip)
        for head in range(heads):
            spot = pl.ds(pl.multiple_of(head * HD + quarter * part, part), part)
            value = came[head].astype(F32)
            state[spot, :] = sums[spot, :] + decays[head : head + 1] * value
            carried[spot, :] = value.astype(BF16)
    inter = lax.dot_general(
        writes[...], carried[...], (((1,), (1,)), ((), ())), preferred_element_type=F32
    )
    rounded = (fixed[...] + slope[...] * inter).astype(BF16)
    rim[...] = rounded[:16]
    rest[...] = rounded[half:]
    pre[...] = rounded[: half + 16].astype(F32)
    total = taps[0:1] * pre[0:half]
    for tap in range(1, KW):
        total = total + taps[tap : tap + 1] * pre[tap : tap + half]
    chunk[...] = total.astype(BF16)


def tail_kernel(rest, rim, chunk, taps, last, whole, pre):
    half = rest.shape[0]
    pre[:half] = rest[...].astype(F32)
    pre[half:] = rim[...].astype(F32)
    total = taps[0:1] * pre[0:half]
    for tap in range(1, KW):
        total = total + taps[tap : tap + 1] * pre[tap : tap + half]
    rounded = total.astype(BF16)
    last[...] = rounded
    whole[:half] = chunk[...]
    whole[half:] = rounded


def product_kernel(where, own, behind, ahead, across, weight, kept, up, down, over):
    row, column = where[2], where[3]
    width = own.shape[1]
    for place, out in ((2, over), (1, up), (3, down), (0, kept)):
        spot = pl.ds(pl.multiple_of(lax.rem(row + place, 4) * width, width), width)
        total = None
        for source, piece in ((0, own), (3, behind), (1, ahead), (2, across)):
            at = pl.ds(pl.multiple_of(lax.rem(column + source, 4) * width, width), width)
            term = lax.dot_general(
                piece[...], weight[spot, at], (((1,), (1,)), ((), ())), preferred_element_type=F32
            )
            total = term if total is None else total + term
        out[...] = total.astype(out.dtype)


def flipped(value, flip):
    count = lax.axis_size("ctx")
    return lax.ppermute(value, "ctx", [(place, place ^ flip) for place in range(count)])


def earlier(value, steps):
    count = lax.axis_size("ctx")
    return lax.ppermute(value, "ctx", [(place, place - steps) for place in range(steps, count)])


def around(value, axis, steps):
    count = lax.axis_size(axis)
    return lax.ppermute(value, axis, [(place, (place + steps) % count) for place in range(count)])


def on_device(
    output_grad, conv_out, input_mix, output_mix, step_size, log_decay, skip_gain, conv_weight,
    later_grad, proj_weight,
):
    tokens, width = output_grad.shape
    heads = step_size.shape[0]
    states = input_mix.shape[2]
    half = tokens // 2
    part = HD // QUAD
    ctx, row, column = lax.axis_index("ctx"), lax.axis_index("row"), lax.axis_index("col")
    where = jnp.stack([ctx % QUAD, ctx // QUAD, row, column]).astype(jnp.int32)
    group = (row * lax.axis_size("col") + column) * heads // HPG
    reads = lax.dynamic_index_in_dim(output_mix, group, 1, keepdims=False)
    writes = lax.dynamic_index_in_dim(input_mix, group, 1, keepdims=False)
    later = later_grad.reshape(width, states)
    skip_row = jnp.repeat(skip_gain, HD)[None, :]

    message = struct((heads + 1, part, states), BF16)
    piece = struct((heads, part, states), BF16)
    wide = struct((width, states), F32)
    plane = struct((tokens, width), F32)
    sums, cumulative, decays, *out = call(
        block_kernel,
        (wide, struct((heads, tokens), F32), struct((heads, states), F32)) + (message,) * 3,
        (where, output_grad, reads, log_decay),
        flops=2 * tokens * width * states, moved=3 << 20, smem=1,
    )
    near = [flipped(value, flip) for flip, value in enumerate(out, 1)]
    fixed, slope = call(
        intra_kernel,
        (plane, plane),
        (output_grad, writes, reads, cumulative, step_size, skip_row, conv_out),
        scratch=(pltpu.VMEM((tokens, tokens), F32), pltpu.VMEM((tokens, width), F32)),
        flops=6 * tokens * tokens * width, moved=6 << 20,
    )
    quads = (
        pltpu.VMEM((QUAD, heads, part, states), F32),
        pltpu.VMEM((QUAD, heads, states), F32),
    )
    joined = call(
        quad_kernel, message, (where, sums, decays, *near), scratch=quads, moved=1 << 20, smem=1
    )
    beyond = [earlier(joined, QUAD * ahead) for ahead in (1, 2, 3)]
    own, *out = call(
        carry_kernel,
        (struct((heads, part, states), F32),) + (piece,) * 3,
        (where, sums, decays, *near, *beyond, later),
        scratch=quads + (pltpu.VMEM((QUAD, heads, part, states), F32),),
        moved=1 << 20, smem=1,
    )
    parts = [flipped(value, flip) for flip, value in enumerate(out, 1)]
    block = struct((half, width), BF16)
    state, rim, chunk, rest = call(
        join_kernel,
        (wide, struct((16, width), BF16), block, block),
        (where, sums, decays, own, *parts, writes, fixed, slope, conv_weight),
        scratch=(pltpu.VMEM((width, states), BF16), pltpu.VMEM((half + 16, width), F32)),
        flops=2 * tokens * width * states, moved=4 << 20, smem=1,
    )
    rim = earlier(rim, 1)
    gathered = [around(chunk, "col", steps) for steps in (2, 1, -1)]
    last, x_grad = call(
        tail_kernel,
        (block, struct((tokens, width), BF16)),
        (rest, rim, chunk, conv_weight),
        scratch=(pltpu.VMEM((half + 16, width), F32),),
        moved=1 << 20,
    )
    gathered_last = [around(last, "col", steps) for steps in (2, 1, -1)]

    def product(mine, others):
        across, behind, ahead = others
        kept, up, down, over = call(
            product_kernel,
            (struct((half, width), F32), block, block, block),
            (where, mine, behind, ahead, across, proj_weight),
            flops=2 * half * proj_weight.size, moved=10 << 20, smem=1,
        )
        return kept, [around(over, "row", 2), around(up, "row", 1), around(down, "row", -1)]

    def total(kept, others):
        return (kept + sum(value.astype(F32) for value in others)).astype(BF16)

    first_sums = product(chunk, gathered)
    last_sums = product(last, gathered_last)
    hidden_grad = jnp.concatenate([total(*first_sums), total(*last_sums)], axis=0)
    return hidden_grad, x_grad, state.reshape(1, heads, HD, states)


def solution(mesh):
    return jax.shard_map(
        on_device,
        mesh=mesh,
        in_specs=(
            P("ctx", ("row", "col")),
            P("ctx", ("row", "col")),
            P("ctx", None, None),
            P("ctx", None, None),
            P(("row", "col"), "ctx"),
            P(("row", "col"), "ctx"),
            P(("row", "col")),
            P(None, ("row", "col")),
            P(("row", "col"), None, None),
            P("col", "row"),
        ),
        out_specs=(
            P("ctx", ("col", "row")),
            P("ctx", ("row", "col")),
            P("ctx", ("row", "col"), None, None),
        ),
        check_vma=False,
    )
```

time: 253 us -> 85.8 us (0.34)
  waiting for transfers between devices: 172 us -> 27.7 us
  matrix products: 17.7 us -> 0 us
  Pallas kernels: 0 us -> 13.9 us
  between operations: 14.2 us -> 0.86 us
  other arithmetic: 8.98 us -> 1.19 us
  local copies, waits for them, and re-layouts: 4.6 us -> 9.98 us
  starting transfers between devices: 34 us -> 31.3 us
    ppermute x16 -> x22, waiting for transfers between devices: 87.5 us -> 27.7 us  [the longest x12 14.7 us: around(): lax.ppermute(value, axis, [(place, (place + steps) % count) for place in...]
    all_gather x1 -> x0, waiting for transfers between devices: 52.7 us -> none  [on_device(): lax.all_gather(x_grad, 'col', axis=1, tiled=True)]
    reduce_scatter x1 -> x0, waiting for transfers between devices: 31.6 us -> none  [on_device(): lax.psum_scatter(partial_grad.astype(jnp.bfloat16), 'row', scatter_dimens...]
    dot_general x5 -> x0, matrix products: 17.7 us -> none  [the longest x1 9.85 us: on_device(): lax.dot_general(lax.all_gather(x_grad, 'col', axis=1, tiled=True), proj_w...]
    pallas_call x0 -> x8, Pallas kernels: none -> 13.9 us  [call(): pl.pallas_call(kernel, out_shape=outs, in_specs=[SMEM] * smem + [VMEM] *...]
    unnamed x9 -> x20, local copies, waits for them, and re-layouts: 1.27 us -> 6.86 us
    convert_element_type x19 -> x2, other arithmetic: 4.71 us -> 0.28 us  [total(): return (kept + sum((value.astype(F32) for value in others))).astype(BF16)]
    ppermute x16 -> x22, starting transfers between devices: 34 us -> 31.3 us  [the longest x12 17 us: around(): lax.ppermute(value, axis, [(place, (place + steps) % count) for place in...]
  transfers between devices with their start and end apart: 18 -> 22, of which waited for: 18 -> 12; matrix products, arithmetic and copies ran while one was open for 0% -> 3% of each run, Pallas kernels for 0% -> 11%
where the time goes in v1:
time: 85.8 us; the launch traced here: 84.9 us
  starting transfers between devices  31.3 us (36%)
  waiting for transfers between devices  27.7 us (32%)
  Pallas kernels  13.9 us (16%)
  local copies, waits for them, and re-layouts  9.98 us (12%)
  other arithmetic  1.19 us (1%)
  between operations  0.86 us (1%)
    ppermute x12, starting transfers between devices, around(): lax.ppermute(value, axis, [(place, (place + steps) % count) for place in...  17 us
    ppermute x12, waiting for transfers between devices, around(): lax.ppermute(value, axis, [(place, (place + steps) % count) for place in...  14.7 us
    pallas_call x8, Pallas kernels, call(): pl.pallas_call(kernel, out_shape=outs, in_specs=[SMEM] * smem + [VMEM] *...  13.9 us
    ppermute x4, waiting for transfers between devices, earlier(): lax.ppermute(value, 'ctx', [(place, place - steps) for place in range(ste...  9.94 us
    ppermute x6, starting transfers between devices, flipped(): lax.ppermute(value, 'ctx', [(place, place ^ flip) for place in range(coun...  7.34 us
    ppermute x4, starting transfers between devices, earlier(): lax.ppermute(value, 'ctx', [(place, place - steps) for place in range(ste...  6.95 us
    unnamed x20, local copies, waits for them, and re-layouts  6.86 us
    ppermute x6, waiting for transfers between devices, flipped(): lax.ppermute(value, 'ctx', [(place, place ^ flip) for place in range(coun...  3.06 us
  transfers between devices with their start and end apart: 22, of which 12 were waited for; matrix products, arithmetic and copies ran while one was open for 3% of the time, Pallas kernels for 11%

profile of v1, /device:TPU:1, one launch (start us, length us, event | category | flops | bytes accessed | tf_op | source)
XLA Modules:
  0.0 84.9 jit_solution(1889075047173737581)
XLA Ops:
  0.6 0.0 copy-start
  0.7 1.2 %copy-done = bf16[512,4,256]{2,1,0:T(4,128)(2,1)S(1)} copy-done((bf16[512,4,256]{2,1,0:T(4,128)(2,1)S(1)}, bf16[512,4,256]{2,1,0:T(4,128)(2,1)}, u32[]{:S(2)}) %copy-start) | copy-done | bytes 1048600
  1.9 0.5 constant_dynamic-slice_fusion.1
  2.5 0.1 pad_add_fusion.where
  2.6 1.0 %copy-done.3 = bf16[512,512]{1,0:T(8,128)(2,1)S(1)} copy-done((bf16[512,512]{1,0:T(8,128)(2,1)S(1)}, bf16[512,512]{1,0:T(8,128)(2,1)}, u32[]{:S(2)}) %copy-start.3) | copy-done | bytes 524312
  3.6 0.7 copy-done.6
  4.3 1.7 %shard_map.121 = (f32[512,256]{1,0:T(8,128)S(1)}, f32[8,512]{1,0:T(8,128)S(1)}, f32[8,256]{1,0:T(8,128)S(1)}, bf16[9,16,256]{2,1,0:T(8,128)(2,1)S(1)}, bf16[9,16...) custom-call(s32[4]{0:T(128)S(1)} %pad_add_fusion.where, bf16[512,512]{1,0:T(8,128)(2,1)S(1)} %copy-done.3, ...), custom_call_target="tpu_custom_call" | custom-call | flops 134217728 | bytes 3145728 | tf_op jit(solution)/shard_map/pallas_call | solution.py:23
  6.0 3.3 %collective-permute-start = (bf16[9,16,256]{2,1,0:T(8,128)(2,1)S(1)}, bf16[9,16,256]{2,1,0:T(8,128)(2,1)S(1)}, u32[]{:S(2)}, u32[]{:S(2)}) collective-permute-start(bf16[9,16,256]{2,1,0:T(8,128)(2,1)S(1)} %get-tuple-element.31), channel_id=1, source_target_pairs={{0,16},{16,0},{32,48},{48,32},{64,80},{80,64},{96,112},{112,96},{1... | collective-permute-start | bytes 221192 | tf_op jit(solution)/shard_map/ppermute | solution.py:246
  9.3 0.0 collective-permute-start.1
  9.3 1.7 %collective-permute-start.2 = (bf16[9,16,256]{2,1,0:T(8,128)(2,1)S(1)}, bf16[9,16,256]{2,1,0:T(8,128)(2,1)S(1)}, u32[]{:S(2)}, u32[]{:S(2)}) collective-permute-start(bf16[9,16,256]{2,1,0:T(8,128)(2,1)S(1)} %get-tuple-element.33), channel_id=1, source_target_pairs={{0,48},{16,32},{32,16},{48,0},{64,112},{80,96},{96,80},{112,64},{1... | collective-permute-start | bytes 221192 | tf_op jit(solution)/shard_map/ppermute | solution.py:246
  11.1 0.7 broadcast_in_dim.3
  11.8 0.1 broadcast_in_dim_reshape.3.skip_row
  11.9 0.0 collective-permute-done.one
  11.9 1.3 %collective-permute-done.1.two = bf16[9,16,256]{2,1,0:T(8,128)(2,1)S(1)} collective-permute-done((bf16[9,16,256]{2,1,0:T(8,128)(2,1)S(1)}, bf16[9,16,256]{2,1,0:T(8,128)(2,1)S(1)}, u32[]{:S(2)}, u32[]{:S(2)}) %collective-permute-start.1) | collective-permute-done | bytes 73760 | tf_op jit(solution)/shard_map/ppermute | solution.py:246
  13.2 1.8 %collective-permute-done.2.three = bf16[9,16,256]{2,1,0:T(8,128)(2,1)S(1)} collective-permute-done((bf16[9,16,256]{2,1,0:T(8,128)(2,1)S(1)}, bf16[9,16,256]{2,1,0:T(8,128)(2,1)S(1)}, u32[]{:S(2)}, u32[]{:S(2)}) %collective-permute-start.2) | collective-permute-done | bytes 73760 | tf_op jit(solution)/shard_map/ppermute | solution.py:246
  14.9 0.6 shard_map.122
  15.6 1.3 %collective-permute-start.5 = (bf16[9,16,256]{2,1,0:T(8,128)(2,1)S(1)}, bf16[9,16,256]{2,1,0:T(8,128)(2,1)S(1)}, u32[]{:S(2)}, u32[]{:S(2)}) collective-permute-start(bf16[9,16,256]{2,1,0:T(8,128)(2,1)S(1)} %shard_map.122), channel_id=1, source_target_pairs={{192,0},{208,16},{224,32},{240,48},{193,1},{209,17},{225,33},{241,... | collective-permute-start | bytes 221192 | tf_op jit(solution)/shard_map/ppermute | solution.py:251
  16.9 1.3 %collective-permute-start.4 = (bf16[9,16,256]{2,1,0:T(8,128)(2,1)S(1)}, bf16[9,16,256]{2,1,0:T(8,128)(2,1)S(1)}, u32[]{:S(2)}, u32[]{:S(2)}) collective-permute-start(bf16[9,16,256]{2,1,0:T(8,128)(2,1)S(1)} %shard_map.122), channel_id=1, source_target_pairs={{128,0},{144,16},{160,32},{176,48},{192,64},{208,80},{224,96},{240... | collective-permute-start | bytes 221192 | tf_op jit(solution)/shard_map/ppermute | solution.py:251
  18.2 1.3 %collective-permute-start.3 = (bf16[9,16,256]{2,1,0:T(8,128)(2,1)S(1)}, bf16[9,16,256]{2,1,0:T(8,128)(2,1)S(1)}, u32[]{:S(2)}, u32[]{:S(2)}) collective-permute-start(bf16[9,16,256]{2,1,0:T(8,128)(2,1)S(1)} %shard_map.122), channel_id=1, source_target_pairs={{64,0},{80,16},{96,32},{112,48},{128,64},{144,80},{160,96},{176,11... | collective-permute-start | bytes 221192 | tf_op jit(solution)/shard_map/ppermute | solution.py:251
  19.5 1.8 %constant_dynamic-slice_fusion = bf16[512,1,256]{2,1,0:T(2,128)(2,1)S(1)} fusion(bf16[512,4,256]{2,1,0:T(4,128)(2,1)} %param.12, s32[]{:T(128)S(6)} %select_n.22), kind=kLoop, calls=%fused_computation.6 | loop fusion | bytes 524292 | tf_op jit(solution)/shard_map/jit(dynamic_index_in_dim)/dynamic_slice | solution.py:272
  21.3 2.2 %collective-permute-done.5.far = bf16[9,16,256]{2,1,0:T(8,128)(2,1)S(1)} collective-permute-done((bf16[9,16,256]{2,1,0:T(8,128)(2,1)S(1)}, bf16[9,16,256]{2,1,0:T(8,128)(2,1)S(1)}, u32[]{:S(2)}, u32[]{:S(2)}) %collective-permute-start.5) | collective-permute-done | bytes 73760 | tf_op jit(solution)/shard_map/ppermute | solution.py:251
  23.5 2.9 %collective-permute-done.4.middle = bf16[9,16,256]{2,1,0:T(8,128)(2,1)S(1)} collective-permute-done((bf16[9,16,256]{2,1,0:T(8,128)(2,1)S(1)}, bf16[9,16,256]{2,1,0:T(8,128)(2,1)S(1)}, u32[]{:S(2)}, u32[]{:S(2)}) %collective-permute-start.4) | collective-permute-done | bytes 73760 | tf_op jit(solution)/shard_map/ppermute | solution.py:251
  26.3 1.9 %collective-permute-done.3.near = bf16[9,16,256]{2,1,0:T(8,128)(2,1)S(1)} collective-permute-done((bf16[9,16,256]{2,1,0:T(8,128)(2,1)S(1)}, bf16[9,16,256]{2,1,0:T(8,128)(2,1)S(1)}, u32[]{:S(2)}, u32[]{:S(2)}) %collective-permute-start.3) | collective-permute-done | bytes 73760 | tf_op jit(solution)/shard_map/ppermute | solution.py:251
  28.2 1.0 %copy-done.2 = f32[8,64,256]{2,1,0:T(8,128)S(1)} copy-done((f32[8,64,256]{2,1,0:T(8,128)S(1)}, f32[8,64,256]{2,1,0:T(8,128)}, u32[]{:S(2)}) %copy-start.2) | copy-done | bytes 524312
  29.2 0.7 shard_map.123
  29.9 0.5 collective-permute-start.6
  30.5 1.2 %collective-permute-start.7 = (bf16[8,16,256]{2,1,0:T(8,128)(2,1)S(1)}, bf16[8,16,256]{2,1,0:T(8,128)(2,1)S(1)}, u32[]{:S(2)}, u32[]{:S(2)}) collective-permute-start(bf16[8,16,256]{2,1,0:T(8,128)(2,1)S(1)} %get-tuple-element.36), channel_id=1, source_target_pairs={{0,32},{16,48},{32,0},{48,16},{64,96},{80,112},{96,64},{112,80},{1... | collective-permute-start | bytes 196616 | tf_op jit(solution)/shard_map/ppermute | solution.py:246
  31.7 0.5 collective-permute-start.8
  32.2 1.0 %copy-done.4 = bf16[512,512]{1,0:T(8,128)(2,1)S(1)} copy-done((bf16[512,512]{1,0:T(8,128)(2,1)S(1)}, bf16[512,512]{1,0:T(8,128)(2,1)}, u32[]{:S(2)}) %copy-start.4) | copy-done | bytes 524312
  33.3 1.0 %copy-done.7 = bf16[512,512]{1,0:T(8,128)(2,1)S(1)} copy-done((bf16[512,512]{1,0:T(8,128)(2,1)S(1)}, bf16[512,512]{1,0:T(8,128)(2,1)}, u32[]{:S(2)}) %copy-start.7) | copy-done | bytes 524312
  34.3 0.7 copy-done.8
  35.0 2.4 %shard_map.124 = (f32[512,512]{1,0:T(8,128)S(1)}, f32[512,512]{1,0:T(8,128)S(1)}) custom-call(bf16[512,512]{1,0:T(8,128)(2,1)S(1)} %copy-done.4, bf16[512,256]{1,0:T(8,128)(2,1)S(1)} %bitcast.14, bf16[512,256]{1,0:T(8,128)(2,1)S(1)} %bitcast.13, f32[8,512]{1,0:T(8,128)S(1)} %get-tuple-element.38.cumulative, f32[8,512]{1,0:T(8,128)S(1)} %copy-done.8, ...), custom_call_target="tpu_custom_call" | custom-call | flops 805306368 | bytes 6291456 | tf_op jit(solution)/shard_map/pallas_call | solution.py:23
  37.4 0.0 collective-permute-done.6.first
  37.4 0.0 collective-permute-done.7.second
  37.5 0.0 collective-permute-done.8.third
  37.5 1.4 %shard_map.125 = (f32[512,256]{1,0:T(8,128)}, bf16[16,512]{1,0:T(8,128)(2,1)S(1)}, bf16[256,512]{1,0:T(8,128)(2,1)S(1)}, bf16[256,512]{1,0:T(8,128)(2,1)S(1)}) custom-call(s32[4]{0:T(128)S(1)} %pad_add_fusion.where, f32[512,256]{1,0:T(8,128)S(1)} %get-tuple-element.29.sums, f32[8,256]{1,0:T(8,128)S(1)} %get-tuple-element.30.decays, ...), custom_call_target="tpu_custom_call" | custom-call | flops 134217728 | bytes 4194304 | tf_op jit(solution)/shard_map/pallas_call | solution.py:23
  38.9 2.3 %collective-permute-start.11 = (bf16[256,512]{1,0:T(8,128)(2,1)S(1)}, bf16[256,512]{1,0:T(8,128)(2,1)S(1)}, u32[]{:S(2)}, u32[]{:S(2)}) collective-permute-start(bf16[256,512]{1,0:T(8,128)(2,1)S(1)} %get-tuple-element.41.own.chunk), channel_id=1, source_target_pairs={{0,2},{1,3},{2,0},{3,1},{4,6},{5,7},{6,4},{7,5},{8,10},{9,11},{10,... | collective-permute-start | bytes 786440 | tf_op jit(solution)/shard_map/ppermute | solution.py:256
  41.2 0.9 %collective-permute-start.10 = (bf16[256,512]{1,0:T(8,128)(2,1)S(1)}, bf16[256,512]{1,0:T(8,128)(2,1)S(1)}, u32[]{:S(2)}, u32[]{:S(2)}) collective-permute-start(bf16[256,512]{1,0:T(8,128)(2,1)S(1)} %get-tuple-element.41.own.chunk), channel_id=1, source_target_pairs={{0,3},{1,0},{2,1},{3,2},{4,7},{5,4},{6,5},{7,6},{8,11},{9,8},{10,9... | collective-permute-start | bytes 786440 | tf_op jit(solution)/shard_map/ppermute | solution.py:256
  42.0 0.6 collective-permute-start.9
  42.6 3.1 %collective-permute-start.15 = (bf16[16,512]{1,0:T(8,128)(2,1)S(1)}, bf16[16,512]{1,0:T(8,128)(2,1)S(1)}, u32[]{:S(2)}, u32[]{:S(2)}) collective-permute-start(bf16[16,512]{1,0:T(8,128)(2,1)S(1)} %get-tuple-element.47), channel_id=1, source_target_pairs={{16,0},{32,16},{48,32},{64,48},{80,64},{96,80},{112,96},{128,112},... | collective-permute-start | bytes 49160 | tf_op jit(solution)/shard_map/ppermute | solution.py:251
  45.7 3.0 %collective-permute-done.15.rim = bf16[16,512]{1,0:T(8,128)(2,1)S(1)} collective-permute-done((bf16[16,512]{1,0:T(8,128)(2,1)S(1)}, bf16[16,512]{1,0:T(8,128)(2,1)S(1)}, u32[]{:S(2)}, u32[]{:S(2)}) %collective-permute-start.15) | collective-permute-done | bytes 16416 | tf_op jit(solution)/shard_map/ppermute | solution.py:251
  48.8 1.3 %shard_map.127 = (bf16[256,512]{1,0:T(8,128)(2,1)S(1)}, bf16[512,512]{1,0:T(8,128)(2,1)}) custom-call(bf16[256,512]{1,0:T(8,128)(2,1)S(1)} %get-tuple-element.46.rest, bf16[16,512]{1,0:T(8,128)(2,1)S(1)} %collective-permute-done.15.rim, bf16[256,512]{1,0:T(8,128)(2,1)S(1)} %get-tuple-element.41.own.chunk, f32[4,512]{1,0:T(4,128)S(1)} %copy-done.5), custom_call_target="tpu_custom_call" | custom-call | bytes 1048576 | tf_op jit(solution)/shard_map/pallas_call | solution.py:23
  50.0 0.4 collective-permute-start.18
  50.4 2.3 %collective-permute-start.17 = (bf16[256,512]{1,0:T(8,128)(2,1)S(1)}, bf16[256,512]{1,0:T(8,128)(2,1)S(1)}, u32[]{:S(2)}, u32[]{:S(2)}) collective-permute-start(bf16[256,512]{1,0:T(8,128)(2,1)S(1)} %get-tuple-element.48.own), channel_id=1, source_target_pairs={{0,3},{1,0},{2,1},{3,2},{4,7},{5,4},{6,5},{7,6},{8,11},{9,8},{10,9... | collective-permute-start | bytes 786440 | tf_op jit(solution)/shard_map/ppermute | solution.py:256
  52.7 0.0 collective-permute-done.11.across
  52.7 0.0 collective-permute-start.16
  52.7 0.5 collective-permute-done.10.ahead
  53.2 1.0 %collective-permute-done.9.behind = bf16[256,512]{1,0:T(8,128)(2,1)S(1)} collective-permute-done((bf16[256,512]{1,0:T(8,128)(2,1)S(1)}, bf16[256,512]{1,0:T(8,128)(2,1)S(1)}, u32[]{:S(2)}, u32[]{:S(2)}) %collective-permute-start.9) | collective-permute-done | bytes 262176 | tf_op jit(solution)/shard_map/ppermute | solution.py:256
  54.2 2.9 %shard_map.126 = (f32[256,512]{1,0:T(8,128)S(1)}, bf16[256,512]{1,0:T(8,128)(2,1)S(1)}, bf16[256,512]{1,0:T(8,128)(2,1)S(1)}, bf16[256,512]{1,0:T(8,128)(2,1)S(1)}) custom-call(s32[4]{0:T(128)S(1)} %pad_add_fusion.where, bf16[256,512]{1,0:T(8,128)(2,1)S(1)} %get-tuple-element.41.own.chunk, bf16[256,512]{1,0:T(8,128)(2,1)S(1)} %collective-permute-done.9.behind, ...), custom_call_target="tpu_custom_call" | custom-call | flops 2147483648 | bytes 10485760 | tf_op jit(solution)/shard_map/pallas_call | solution.py:23
  57.2 2.5 %collective-permute-start.12 = (bf16[256,512]{1,0:T(8,128)(2,1)S(1)}, bf16[256,512]{1,0:T(8,128)(2,1)S(1)}, u32[]{:S(2)}, u32[]{:S(2)}) collective-permute-start(bf16[256,512]{1,0:T(8,128)(2,1)S(1)} %get-tuple-element.43), channel_id=1, source_target_pairs={{0,8},{4,12},{8,0},{12,4},{1,9},{5,13},{9,1},{13,5},{2,10},{6,14},... | collective-permute-start | bytes 786440 | tf_op jit(solution)/shard_map/ppermute | solution.py:256
  59.7 0.4 collective-permute-start.13
  60.1 0.0 collective-permute-done.18.across
  60.1 2.3 %collective-permute-start.14 = (bf16[256,512]{1,0:T(8,128)(2,1)S(1)}, bf16[256,512]{1,0:T(8,128)(2,1)S(1)}, u32[]{:S(2)}, u32[]{:S(2)}) collective-permute-start(bf16[256,512]{1,0:T(8,128)(2,1)S(1)} %get-tuple-element.45), channel_id=1, source_target_pairs={{0,12},{4,0},{8,4},{12,8},{1,13},{5,1},{9,5},{13,9},{2,14},{6,2},{... | collective-permute-start | bytes 786440 | tf_op jit(solution)/shard_map/ppermute | solution.py:256
  62.4 2.9 %collective-permute-done.17.ahead = bf16[256,512]{1,0:T(8,128)(2,1)S(1)} collective-permute-done((bf16[256,512]{1,0:T(8,128)(2,1)S(1)}, bf16[256,512]{1,0:T(8,128)(2,1)S(1)}, u32[]{:S(2)}, u32[]{:S(2)}) %collective-permute-start.17) | collective-permute-done | bytes 262176 | tf_op jit(solution)/shard_map/ppermute | solution.py:256
  65.2 0.4 collective-permute-done.16.behind
  65.6 2.9 %shard_map.128 = (f32[256,512]{1,0:T(8,128)S(1)}, bf16[256,512]{1,0:T(8,128)(2,1)S(1)}, bf16[256,512]{1,0:T(8,128)(2,1)S(1)}, bf16[256,512]{1,0:T(8,128)(2,1)S(1)}) custom-call(s32[4]{0:T(128)S(1)} %pad_add_fusion.where, bf16[256,512]{1,0:T(8,128)(2,1)S(1)} %get-tuple-element.48.own, bf16[256,512]{1,0:T(8,128)(2,1)S(1)} %collective-permute-done.16.behind, ...), custom_call_target="tpu_custom_call" | custom-call | flops 2147483648 | bytes 10485760 | tf_op jit(solution)/shard_map/pallas_call | solution.py:23
  68.5 2.6 %collective-permute-start.19 = (bf16[256,512]{1,0:T(8,128)(2,1)S(1)}, bf16[256,512]{1,0:T(8,128)(2,1)S(1)}, u32[]{:S(2)}, u32[]{:S(2)}) collective-permute-start(bf16[256,512]{1,0:T(8,128)(2,1)S(1)} %get-tuple-element.50), channel_id=1, source_target_pairs={{0,8},{4,12},{8,0},{12,4},{1,9},{5,13},{9,1},{13,5},{2,10},{6,14},... | collective-permute-start | bytes 786440 | tf_op jit(solution)/shard_map/ppermute | solution.py:256
  71.2 0.4 collective-permute-start.20
  71.6 2.3 %collective-permute-start.21 = (bf16[256,512]{1,0:T(8,128)(2,1)S(1)}, bf16[256,512]{1,0:T(8,128)(2,1)S(1)}, u32[]{:S(2)}, u32[]{:S(2)}) collective-permute-start(bf16[256,512]{1,0:T(8,128)(2,1)S(1)} %get-tuple-element.52), channel_id=1, source_target_pairs={{0,12},{4,0},{8,4},{12,8},{1,13},{5,1},{9,5},{13,9},{2,14},{6,2},{... | collective-permute-start | bytes 786440 | tf_op jit(solution)/shard_map/ppermute | solution.py:256
  73.9 0.1 add_convert_fusion.1
  74.0 3.7 %collective-permute-done.19 = bf16[256,512]{1,0:T(8,128)(2,1)S(1)} collective-permute-done((bf16[256,512]{1,0:T(8,128)(2,1)S(1)}, bf16[256,512]{1,0:T(8,128)(2,1)S(1)}, u32[]{:S(2)}, u32[]{:S(2)}) %collective-permute-start.19) | collective-permute-done | bytes 262176 | tf_op jit(solution)/shard_map/ppermute | solution.py:256
  77.7 6.2 %collective-permute-done.20 = bf16[256,512]{1,0:T(8,128)(2,1)S(1)} collective-permute-done((bf16[256,512]{1,0:T(8,128)(2,1)S(1)}, bf16[256,512]{1,0:T(8,128)(2,1)S(1)}, u32[]{:S(2)}, u32[]{:S(2)}) %collective-permute-start.20) | collective-permute-done | bytes 262176 | tf_op jit(solution)/shard_map/ppermute | solution.py:256
  84.0 0.1 add_convert_fusion
  84.1 0.8 pad_maximum_fusion
  (16 shorter events, 0.1 us)
Async XLA Ops:
  0.6 1.2 %copy-start = (bf16[512,4,256]{2,1,0:T(4,128)(2,1)S(1)}, bf16[512,4,256]{2,1,0:T(4,128)(2,1)}, u32[]{:S(2)}) copy-start(bf16[512,4,256]{2,1,0:T(4,128)(2,1)} %param.13) | copy-start | bytes 3145732
  0.6 36.8 %copy-start.5 = (f32[4,512]{1,0:T(4,128)S(1)}, f32[4,512]{1,0:T(4,128)}, u32[]{:S(2)}) copy-start(f32[4,512]{1,0:T(4,128)} %taps.3) | copy-start | bytes 24580
  2.5 1.0 %copy-start.3 = (bf16[512,512]{1,0:T(8,128)(2,1)S(1)}, bf16[512,512]{1,0:T(8,128)(2,1)}, u32[]{:S(2)}) copy-start(bf16[512,512]{1,0:T(8,128)(2,1)} %grad.3) | copy-start | bytes 1572868
  3.6 0.7 copy-start.6
  6.0 5.9 %collective-permute-start = (bf16[9,16,256]{2,1,0:T(8,128)(2,1)S(1)}, bf16[9,16,256]{2,1,0:T(8,128)(2,1)S(1)}, u32[]{:S(2)}, u32[]{:S(2)}) collective-permute-start(bf16[9,16,256]{2,1,0:T(8,128)(2,1)S(1)} %get-tuple-element.31), channel_id=1, source_target_pairs={{0,16},{16,0},{32,48},{48,32},{64,80},{80,64},{96,112},{112,96},{1... | collective-permute-start | bytes 221192 | tf_op jit(solution)/shard_map/ppermute | solution.py:246
  9.3 3.8 %collective-permute-start.1 = (bf16[9,16,256]{2,1,0:T(8,128)(2,1)S(1)}, bf16[9,16,256]{2,1,0:T(8,128)(2,1)S(1)}, u32[]{:S(2)}, u32[]{:S(2)}) collective-permute-start(bf16[9,16,256]{2,1,0:T(8,128)(2,1)S(1)} %get-tuple-element.32), channel_id=1, source_target_pairs={{0,32},{16,48},{32,0},{48,16},{64,96},{80,112},{96,64},{112,80},{1... | collective-permute-start | bytes 221192 | tf_op jit(solution)/shard_map/ppermute | solution.py:246
  9.3 5.6 %collective-permute-start.2 = (bf16[9,16,256]{2,1,0:T(8,128)(2,1)S(1)}, bf16[9,16,256]{2,1,0:T(8,128)(2,1)S(1)}, u32[]{:S(2)}, u32[]{:S(2)}) collective-permute-start(bf16[9,16,256]{2,1,0:T(8,128)(2,1)S(1)} %get-tuple-element.33), channel_id=1, source_target_pairs={{0,48},{16,32},{32,16},{48,0},{64,112},{80,96},{96,80},{112,64},{1... | collective-permute-start | bytes 221192 | tf_op jit(solution)/shard_map/ppermute | solution.py:246
  11.9 42.4 %copy-start.1 = (bf16[2048,2048]{1,0:T(8,128)(2,1)S(1)}, bf16[2048,2048]{1,0:T(8,128)(2,1)}, u32[]{:S(2)}) copy-start(bf16[2048,2048]{1,0:T(8,128)(2,1)} %weight.3) | copy-start | bytes 25165828
  15.6 7.9 %collective-permute-start.5 = (bf16[9,16,256]{2,1,0:T(8,128)(2,1)S(1)}, bf16[9,16,256]{2,1,0:T(8,128)(2,1)S(1)}, u32[]{:S(2)}, u32[]{:S(2)}) collective-permute-start(bf16[9,16,256]{2,1,0:T(8,128)(2,1)S(1)} %shard_map.122), channel_id=1, source_target_pairs={{192,0},{208,16},{224,32},{240,48},{193,1},{209,17},{225,33},{241,... | collective-permute-start | bytes 221192 | tf_op jit(solution)/shard_map/ppermute | solution.py:251
  16.9 9.5 %collective-permute-start.4 = (bf16[9,16,256]{2,1,0:T(8,128)(2,1)S(1)}, bf16[9,16,256]{2,1,0:T(8,128)(2,1)S(1)}, u32[]{:S(2)}, u32[]{:S(2)}) collective-permute-start(bf16[9,16,256]{2,1,0:T(8,128)(2,1)S(1)} %shard_map.122), channel_id=1, source_target_pairs={{128,0},{144,16},{160,32},{176,48},{192,64},{208,80},{224,96},{240... | collective-permute-start | bytes 221192 | tf_op jit(solution)/shard_map/ppermute | solution.py:251
  18.2 10.0 %collective-permute-start.3 = (bf16[9,16,256]{2,1,0:T(8,128)(2,1)S(1)}, bf16[9,16,256]{2,1,0:T(8,128)(2,1)S(1)}, u32[]{:S(2)}, u32[]{:S(2)}) collective-permute-start(bf16[9,16,256]{2,1,0:T(8,128)(2,1)S(1)} %shard_map.122), channel_id=1, source_target_pairs={{64,0},{80,16},{96,32},{112,48},{128,64},{144,80},{160,96},{176,11... | collective-permute-start | bytes 221192 | tf_op jit(solution)/shard_map/ppermute | solution.py:251
  28.2 1.0 %copy-start.2 = (f32[8,64,256]{2,1,0:T(8,128)S(1)}, f32[8,64,256]{2,1,0:T(8,128)}, u32[]{:S(2)}) copy-start(f32[8,64,256]{2,1,0:T(8,128)} %param.18) | copy-start | bytes 1572868
  29.9 7.5 %collective-permute-start.6 = (bf16[8,16,256]{2,1,0:T(8,128)(2,1)S(1)}, bf16[8,16,256]{2,1,0:T(8,128)(2,1)S(1)}, u32[]{:S(2)}, u32[]{:S(2)}) collective-permute-start(bf16[8,16,256]{2,1,0:T(8,128)(2,1)S(1)} %get-tuple-element.35), channel_id=1, source_target_pairs={{0,16},{16,0},{32,48},{48,32},{64,80},{80,64},{96,112},{112,96},{1... | collective-permute-start | bytes 196616 | tf_op jit(solution)/shard_map/ppermute | solution.py:246
  30.5 7.0 %collective-permute-start.7 = (bf16[8,16,256]{2,1,0:T(8,128)(2,1)S(1)}, bf16[8,16,256]{2,1,0:T(8,128)(2,1)S(1)}, u32[]{:S(2)}, u32[]{:S(2)}) collective-permute-start(bf16[8,16,256]{2,1,0:T(8,128)(2,1)S(1)} %get-tuple-element.36), channel_id=1, source_target_pairs={{0,32},{16,48},{32,0},{48,16},{64,96},{80,112},{96,64},{112,80},{1... | collective-permute-start | bytes 196616 | tf_op jit(solution)/shard_map/ppermute | solution.py:246
  31.7 5.8 %collective-permute-start.8 = (bf16[8,16,256]{2,1,0:T(8,128)(2,1)S(1)}, bf16[8,16,256]{2,1,0:T(8,128)(2,1)S(1)}, u32[]{:S(2)}, u32[]{:S(2)}) collective-permute-start(bf16[8,16,256]{2,1,0:T(8,128)(2,1)S(1)} %get-tuple-element.37), channel_id=1, source_target_pairs={{0,48},{16,32},{32,16},{48,0},{64,112},{80,96},{96,80},{112,64},{1... | collective-permute-start | bytes 196616 | tf_op jit(solution)/shard_map/ppermute | solution.py:246
  32.2 1.0 %copy-start.4 = (bf16[512,512]{1,0:T(8,128)(2,1)S(1)}, bf16[512,512]{1,0:T(8,128)(2,1)}, u32[]{:S(2)}) copy-start(bf16[512,512]{1,0:T(8,128)(2,1)} %grad.3) | copy-start | bytes 1572868
  33.3 1.0 %copy-start.7 = (bf16[512,512]{1,0:T(8,128)(2,1)S(1)}, bf16[512,512]{1,0:T(8,128)(2,1)}, u32[]{:S(2)}) copy-start(bf16[512,512]{1,0:T(8,128)(2,1)} %conv_out.1) | copy-start | bytes 1572868
  34.3 0.7 copy-start.8
  38.9 13.8 %collective-permute-start.11 = (bf16[256,512]{1,0:T(8,128)(2,1)S(1)}, bf16[256,512]{1,0:T(8,128)(2,1)S(1)}, u32[]{:S(2)}, u32[]{:S(2)}) collective-permute-start(bf16[256,512]{1,0:T(8,128)(2,1)S(1)} %get-tuple-element.41.own.chunk), channel_id=1, source_target_pairs={{0,2},{1,3},{2,0},{3,1},{4,6},{5,7},{6,4},{7,5},{8,10},{9,11},{10,... | collective-permute-start | bytes 786440 | tf_op jit(solution)/shard_map/ppermute | solution.py:256
  41.2 12.0 %collective-permute-start.10 = (bf16[256,512]{1,0:T(8,128)(2,1)S(1)}, bf16[256,512]{1,0:T(8,128)(2,1)S(1)}, u32[]{:S(2)}, u32[]{:S(2)}) collective-permute-start(bf16[256,512]{1,0:T(8,128)(2,1)S(1)} %get-tuple-element.41.own.chunk), channel_id=1, source_target_pairs={{0,3},{1,0},{2,1},{3,2},{4,7},{5,4},{6,5},{7,6},{8,11},{9,8},{10,9... | collective-permute-start | bytes 786440 | tf_op jit(solution)/shard_map/ppermute | solution.py:256
  42.0 12.2 %collective-permute-start.9 = (bf16[256,512]{1,0:T(8,128)(2,1)S(1)}, bf16[256,512]{1,0:T(8,128)(2,1)S(1)}, u32[]{:S(2)}, u32[]{:S(2)}) collective-permute-start(bf16[256,512]{1,0:T(8,128)(2,1)S(1)} %get-tuple-element.41.own.chunk), channel_id=1, source_target_pairs={{0,1},{1,2},{2,3},{3,0},{4,5},{5,6},{6,7},{7,4},{8,9},{9,10},{10,1... | collective-permute-start | bytes 786440 | tf_op jit(solution)/shard_map/ppermute | solution.py:256
  42.6 6.1 %collective-permute-start.15 = (bf16[16,512]{1,0:T(8,128)(2,1)S(1)}, bf16[16,512]{1,0:T(8,128)(2,1)S(1)}, u32[]{:S(2)}, u32[]{:S(2)}) collective-permute-start(bf16[16,512]{1,0:T(8,128)(2,1)S(1)} %get-tuple-element.47), channel_id=1, source_target_pairs={{16,0},{32,16},{48,32},{64,48},{80,64},{96,80},{112,96},{128,112},... | collective-permute-start | bytes 49160 | tf_op jit(solution)/shard_map/ppermute | solution.py:251
  50.0 10.1 %collective-permute-start.18 = (bf16[256,512]{1,0:T(8,128)(2,1)S(1)}, bf16[256,512]{1,0:T(8,128)(2,1)S(1)}, u32[]{:S(2)}, u32[]{:S(2)}) collective-permute-start(bf16[256,512]{1,0:T(8,128)(2,1)S(1)} %get-tuple-element.48.own), channel_id=1, source_target_pairs={{0,2},{1,3},{2,0},{3,1},{4,6},{5,7},{6,4},{7,5},{8,10},{9,11},{10,... | collective-permute-start | bytes 786440 | tf_op jit(solution)/shard_map/ppermute | solution.py:256
  50.4 14.9 %collective-permute-start.17 = (bf16[256,512]{1,0:T(8,128)(2,1)S(1)}, bf16[256,512]{1,0:T(8,128)(2,1)S(1)}, u32[]{:S(2)}, u32[]{:S(2)}) collective-permute-start(bf16[256,512]{1,0:T(8,128)(2,1)S(1)} %get-tuple-element.48.own), channel_id=1, source_target_pairs={{0,3},{1,0},{2,1},{3,2},{4,7},{5,4},{6,5},{7,6},{8,11},{9,8},{10,9... | collective-permute-start | bytes 786440 | tf_op jit(solution)/shard_map/ppermute | solution.py:256
  52.7 12.9 %collective-permute-start.16 = (bf16[256,512]{1,0:T(8,128)(2,1)S(1)}, bf16[256,512]{1,0:T(8,128)(2,1)S(1)}, u32[]{:S(2)}, u32[]{:S(2)}) collective-permute-start(bf16[256,512]{1,0:T(8,128)(2,1)S(1)} %get-tuple-element.48.own), channel_id=1, source_target_pairs={{0,1},{1,2},{2,3},{3,0},{4,5},{5,6},{6,7},{7,4},{8,9},{9,10},{10,1... | collective-permute-start | bytes 786440 | tf_op jit(solution)/shard_map/ppermute | solution.py:256
  57.2 14.4 %collective-permute-start.12 = (bf16[256,512]{1,0:T(8,128)(2,1)S(1)}, bf16[256,512]{1,0:T(8,128)(2,1)S(1)}, u32[]{:S(2)}, u32[]{:S(2)}) collective-permute-start(bf16[256,512]{1,0:T(8,128)(2,1)S(1)} %get-tuple-element.43), channel_id=1, source_target_pairs={{0,8},{4,12},{8,0},{12,4},{1,9},{5,13},{9,1},{13,5},{2,10},{6,14},... | collective-permute-start | bytes 786440 | tf_op jit(solution)/shard_map/ppermute | solution.py:256
  59.7 14.2 %collective-permute-start.13 = (bf16[256,512]{1,0:T(8,128)(2,1)S(1)}, bf16[256,512]{1,0:T(8,128)(2,1)S(1)}, u32[]{:S(2)}, u32[]{:S(2)}) collective-permute-start(bf16[256,512]{1,0:T(8,128)(2,1)S(1)} %get-tuple-element.44), channel_id=1, source_target_pairs={{0,4},{4,8},{8,12},{12,0},{1,5},{5,9},{9,13},{13,1},{2,6},{6,10},{... | collective-permute-start | bytes 786440 | tf_op jit(solution)/shard_map/ppermute | solution.py:256
  60.1 13.8 %collective-permute-start.14 = (bf16[256,512]{1,0:T(8,128)(2,1)S(1)}, bf16[256,512]{1,0:T(8,128)(2,1)S(1)}, u32[]{:S(2)}, u32[]{:S(2)}) collective-permute-start(bf16[256,512]{1,0:T(8,128)(2,1)S(1)} %get-tuple-element.45), channel_id=1, source_target_pairs={{0,12},{4,0},{8,4},{12,8},{1,13},{5,1},{9,5},{13,9},{2,14},{6,2},{... | collective-permute-start | bytes 786440 | tf_op jit(solution)/shard_map/ppermute | solution.py:256
  68.5 9.2 %collective-permute-start.19 = (bf16[256,512]{1,0:T(8,128)(2,1)S(1)}, bf16[256,512]{1,0:T(8,128)(2,1)S(1)}, u32[]{:S(2)}, u32[]{:S(2)}) collective-permute-start(bf16[256,512]{1,0:T(8,128)(2,1)S(1)} %get-tuple-element.50), channel_id=1, source_target_pairs={{0,8},{4,12},{8,0},{12,4},{1,9},{5,13},{9,1},{13,5},{2,10},{6,14},... | collective-permute-start | bytes 786440 | tf_op jit(solution)/shard_map/ppermute | solution.py:256
  71.2 12.8 %collective-permute-start.20 = (bf16[256,512]{1,0:T(8,128)(2,1)S(1)}, bf16[256,512]{1,0:T(8,128)(2,1)S(1)}, u32[]{:S(2)}, u32[]{:S(2)}) collective-permute-start(bf16[256,512]{1,0:T(8,128)(2,1)S(1)} %get-tuple-element.51), channel_id=1, source_target_pairs={{0,4},{4,8},{8,12},{12,0},{1,5},{5,9},{9,13},{13,1},{2,6},{6,10},{... | collective-permute-start | bytes 786440 | tf_op jit(solution)/shard_map/ppermute | solution.py:256
  71.6 12.4 %collective-permute-start.21 = (bf16[256,512]{1,0:T(8,128)(2,1)S(1)}, bf16[256,512]{1,0:T(8,128)(2,1)S(1)}, u32[]{:S(2)}, u32[]{:S(2)}) collective-permute-start(bf16[256,512]{1,0:T(8,128)(2,1)S(1)} %get-tuple-element.52), channel_id=1, source_target_pairs={{0,12},{4,0},{8,4},{12,8},{1,13},{5,1},{9,5},{13,9},{2,14},{6,2},{... | collective-permute-start | bytes 786440 | tf_op jit(solution)/shard_map/ppermute | solution.py:256

commit v2 on v1

v2 whole, which is shorter than its diff:
```python
import jax
import jax.numpy as jnp
from jax import lax
from jax.experimental import pallas as pl
from jax.experimental.pallas import tpu as pltpu
from jax.sharding import PartitionSpec as P

HD = 64
HPG = 32
KW = 4
QUAD = 4
F32 = jnp.float32
BF16 = jnp.bfloat16
VMEM = pl.BlockSpec(memory_space=pltpu.VMEM)
SMEM = pl.BlockSpec(memory_space=pltpu.SMEM)
HBM = pl.BlockSpec(memory_space=pltpu.HBM)
FIRST = 256


def struct(shape, dtype):
    return jax.ShapeDtypeStruct(shape, dtype)


def call(kernel, outs, args, specs=(), scratch=()):
    return pl.pallas_call(
        kernel,
        out_shape=outs,
        in_specs=list(specs) + [VMEM] * (len(args) - len(specs)),
        out_specs=jax.tree.map(lambda unused: VMEM, outs),
        scratch_shapes=list(scratch),
        cost_estimate=pl.CostEstimate(flops=0, bytes_accessed=0, transcendentals=0),
        compiler_params=pltpu.CompilerParams(vmem_limit_bytes=40 << 20),
    )(*args)


def split3(value):
    high = value.astype(BF16)
    rest = value - high.astype(F32)
    middle = rest.astype(BF16)
    low = (rest - middle.astype(F32)).astype(BF16)
    return high, middle, low


def over_columns(per_head):
    heads = per_head.shape[0]
    stacked = jnp.concatenate([part.astype(F32) for part in split3(per_head)], axis=0).astype(BF16)
    row = lax.broadcasted_iota(jnp.int32, (3 * heads, heads * HD), 0)
    column = lax.broadcasted_iota(jnp.int32, (3 * heads, heads * HD), 1)
    picks = (lax.rem(row, heads) == column // HD).astype(F32).astype(BF16)
    return lax.dot_general(stacked, picks, (((0,), (0,)), ((), ())), preferred_element_type=F32)


def decay_rows(per_head):
    wide = jnp.broadcast_to(per_head, (per_head.shape[0], 256))
    high = wide.astype(BF16)
    low = (wide - high.astype(F32)).astype(BF16)
    return jnp.concatenate([high.astype(F32), low.astype(F32)], axis=0).astype(BF16)


def block_kernel(
    where, grad_hbm, reads, log_decay, sums, cumulative, decays, one, two, three, grad, total, arrived
):
    fetches = (
        pltpu.make_async_copy(log_decay, total, arrived.at[0]),
        pltpu.make_async_copy(grad_hbm, grad, arrived.at[1]),
    )
    for fetch in fetches:
        fetch.start()
    heads, tokens = total.shape
    part = HD // QUAD
    fetches[0].wait()
    running = total[...]
    lane = lax.broadcasted_iota(jnp.int32, (heads, tokens), 1)
    step = 1
    while step < tokens:
        running = running + jnp.where(lane >= step, pltpu.roll(running, step, 1), 0.0)
        step *= 2
    cumulative[...] = running
    last = jnp.exp(running[:, tokens - 1 : tokens])
    decays[...] = jnp.broadcast_to(last, decays.shape)
    spread = over_columns(jnp.exp(running))
    fetches[1].wait()
    weighted = (spread * grad[...].astype(F32)).astype(BF16)
    sums[...] = lax.dot_general(
        weighted, reads[...], (((0,), (0,)), ((), ())), preferred_element_type=F32
    )
    rows = decay_rows(last)
    me = where[0]
    for flip, sent in ((1, one), (2, two), (3, three)):
        quarter = jnp.bitwise_xor(me, flip)
        for head in range(heads):
            start = pl.multiple_of(head * HD + quarter * part, part)
            sent[head] = sums[pl.ds(start, part), :].astype(BF16)
        sent[heads] = rows


def intra_kernel(
    where, skips, grad_hbm, conv_hbm, step_hbm, later_hbm, writes, reads, cumulative, after,
    fixed, slope, quarter, scores, steps, grad, conv_out, step_size, later, arrived,
):
    fetches = [
        pltpu.make_async_copy(source, target, arrived.at[place])
        for place, (source, target) in enumerate(
            ((step_hbm, step_size), (grad_hbm, grad), (conv_hbm, conv_out), (later_hbm, later))
        )
    ]
    for fetch in fetches:
        fetch.start()
    heads, tokens = cumulative.shape
    part = HD // QUAD
    half = tokens // 2
    scores[...] = lax.dot_general(
        writes[...], reads[...], (((1,), (1,)), ((), ())), preferred_element_type=F32
    )
    total = cumulative[...]
    columns = jnp.transpose(total)
    fetches[0].wait()
    steps[...] = over_columns(step_size[...])
    slope[...] = over_columns(
        step_size[...] * jnp.exp(total[:, tokens - 1 : tokens] - total)
    )
    causal = lax.broadcasted_iota(jnp.int32, (half, half), 1) >= lax.broadcasted_iota(
        jnp.int32, (half, half), 0
    )
    lane = lax.broadcasted_iota(jnp.int32, (half, 2 * HD), 1)
    for fetch in fetches[1:]:
        fetch.wait()
    for head in range(heads):
        start = pl.multiple_of(head * HD + where[0] * part, part)
        quarter[head] = later[pl.ds(start, part), :]
    for pair in range(heads // 2):
        span = slice(pair * 2 * HD, (pair + 1) * 2 * HD)
        skip = jnp.where(lane < HD, skips[2 * pair], skips[2 * pair + 1])
        for at in range(2):
            rows = slice(at * half, (at + 1) * half)
            both = []
            for head in (2 * pair, 2 * pair + 1):
                own = columns[rows, head : head + 1]
                offsets = total[head : head + 1, rows] - own
                mixing = (
                    jnp.exp(jnp.where(causal, offsets, -jnp.inf)) * scores[rows, rows]
                ).astype(BF16)
                sums = jnp.dot(mixing, grad[rows, span], preferred_element_type=F32)
                if at == 0:
                    rest = slice(half, tokens)
                    mixing = (
                        jnp.exp(total[head : head + 1, rest] - own) * scores[rows, rest]
                    ).astype(BF16)
                    sums = sums + jnp.dot(mixing, grad[rest, span], preferred_element_type=F32)
                both.append(sums)
            intra = jnp.where(lane < HD, both[0], both[1])
            activated = conv_out[rows, span].astype(F32)
            sigma = 1.0 / (1.0 + jnp.exp(-activated))
            gate = sigma * (1.0 + activated * (1.0 - sigma))
            fixed[rows, span] = gate * (
                steps[rows, span] * intra + skip * grad[rows, span].astype(F32)
            )
            slope[rows, span] = gate * slope[rows, span]


def gather_quad(me, sums, decays, received, values, scales):
    heads = decays.shape[0]
    part = HD // QUAD
    for head in range(heads):
        start = pl.multiple_of(head * HD + me * part, part)
        values[me, head] = sums[pl.ds(start, part), :]
    scales[me] = decays[...]
    for flip, came in enumerate(received, 1):
        other = jnp.bitwise_xor(me, flip)
        for head in range(heads):
            values[other, head] = came[head].astype(F32)
        tail = came[heads].astype(F32)
        scales[other] = tail[:heads] + tail[heads:]


def quad_kernel(where, sums, decays, one, two, three, after, sent, values, scales):
    heads = decays.shape[0]
    gather_quad(where[0], sums, decays, (one, two, three), values, scales)
    for head in range(heads):
        total = values[3, head]
        for block in (2, 1, 0):
            total = values[block, head] + scales[block][head : head + 1] * total
        sent[head] = total.astype(BF16)
    product = scales[0] * scales[1] * scales[2] * scales[3]
    high = product.astype(BF16).astype(F32)
    sent[heads] = jnp.concatenate([high, product - high], axis=0).astype(BF16)


def carry_kernel(
    where, sums, decays, one, two, three, far, near, middle, later, own, first, second, third,
    values, scales, carries,
):
    heads = decays.shape[0]
    me, quad = where[0], where[1]
    gather_quad(me, sums, decays, (one, two, three), values, scales)
    jumps = []
    for ahead, came in ((3, far), (2, middle), (1, near)):
        tail = came[heads].astype(F32)
        present = jnp.full(decays.shape, quad + ahead, jnp.int32) < QUAD
        jumps.append((came, jnp.where(present, tail[:heads] + tail[heads:], 1.0)))
    for head in range(heads):
        carry = later[head]
        for came, scale in jumps:
            carry = came[head].astype(F32) + scale[head : head + 1] * carry
        carries[3, head] = carry.astype(BF16)
        for block in (3, 2, 1):
            carry = values[block, head] + scales[block][head : head + 1] * carry
            carries[block - 1, head] = carry.astype(BF16)
    for flip, sent in ((0, own), (1, first), (2, second), (3, third)):
        sent[...] = carries[jnp.bitwise_xor(me, flip)]


def taps_sum(pre, taps, start, count):
    total = taps[0:1] * pre[start : start + count]
    for tap in range(1, KW):
        total = total + taps[tap : tap + 1] * pre[start + tap : start + tap + count]
    return total.astype(BF16)


def join_kernel(
    where, own, first, second, third, writes, fixed, slope, taps, chunk, rim, rest, carried, pre
):
    heads = own.shape[0]
    part = HD // QUAD
    me = where[0]
    for flip, came in ((0, own), (1, first), (2, second), (3, third)):
        quarter = jnp.bitwise_xor(me, flip)
        for head in range(heads):
            spot = pl.ds(pl.multiple_of(head * HD + quarter * part, part), part)
            carried[spot, :] = came[head]
    count = chunk.shape[0]
    inter = lax.dot_general(
        writes[...], carried[...], (((1,), (1,)), ((), ())), preferred_element_type=F32
    )
    rounded = (fixed[...] + slope[...] * inter).astype(BF16)
    rim[...] = rounded[:16]
    rest[...] = rounded[count:]
    pre[...] = rounded[: count + 16].astype(F32)
    chunk[...] = taps_sum(pre, taps, 0, count)


def tail_kernel(rest, rim, taps, chunk, pre):
    count = rest.shape[0]
    pre[:count] = rest[...].astype(F32)
    pre[count:] = rim[...].astype(F32)
    chunk[...] = taps_sum(pre, taps, 0, count)


def output_kernel(sums, decays, carried, head, last, after, state, x_grad):
    for at in range(decays.shape[0]):
        spot = slice(at * HD, (at + 1) * HD)
        state[spot] = sums[spot] + decays[at : at + 1] * carried[spot].astype(F32)
    x_grad[: head.shape[0]] = head[...]
    x_grad[head.shape[0] :] = last[...]


def product_kernel(where, own, near, far, weight, after, total):
    column = where[3]
    width = own.shape[1]
    for place in range(4):
        spot = slice(place * width, (place + 1) * width)
        sums = None
        for flip, piece in ((0, own), (1, near), (3, far)):
            source = jnp.bitwise_xor(column, flip)
            at = pl.ds(pl.multiple_of(source * width, width), width)
            term = lax.dot_general(
                piece[...], weight[spot, at], (((1,), (1,)), ((), ())), preferred_element_type=F32
            )
            sums = term if sums is None else sums + term
        total[:, spot] = sums


def finish_kernel(where, across, weight, total, kept, near, far, over):
    row, column = where[2], where[3]
    width = across.shape[1]
    at = pl.ds(pl.multiple_of(jnp.bitwise_xor(column, 2) * width, width), width)
    for flip, out in ((2, over), (1, near), (3, far), (0, kept)):
        target = jnp.bitwise_xor(row, flip)
        spot = pl.ds(pl.multiple_of(target * width, width), width)
        term = lax.dot_general(
            across[...], weight[spot, at], (((1,), (1,)), ((), ())), preferred_element_type=F32
        )
        out[...] = (total[:, spot] + term).astype(out.dtype)


def earlier(value, steps):
    count = lax.axis_size("ctx")
    return lax.ppermute(value, "ctx", [(place, place - steps) for place in range(steps, count)])


def swapped(value, axis, flip):
    count = lax.axis_size(axis)
    return lax.ppermute(value, axis, [(place, place ^ flip) for place in range(count)])


def on_device(
    output_grad, conv_out, input_mix, output_mix, step_size, log_decay, skip_gain, conv_weight,
    later_grad, proj_weight,
):
    tokens, width = output_grad.shape
    heads = step_size.shape[0]
    states = input_mix.shape[2]
    part = HD // QUAD
    ctx, row, column = lax.axis_index("ctx"), lax.axis_index("row"), lax.axis_index("col")
    where = jnp.stack([ctx % QUAD, ctx // QUAD, row, column]).astype(jnp.int32)
    group = (row * lax.axis_size("col") + column) * heads // HPG
    reads = lax.dynamic_index_in_dim(output_mix, group, 1, keepdims=False)
    writes = lax.dynamic_index_in_dim(input_mix, group, 1, keepdims=False)
    later = later_grad.reshape(width, states)

    message = struct((heads + 1, part, states), BF16)
    piece = struct((heads, part, states), BF16)
    wide = struct((width, states), F32)
    plane = struct((tokens, width), F32)
    sums, cumulative, decays, *out = call(
        block_kernel,
        (wide, struct((heads, tokens), F32), struct((heads, states), F32)) + (message,) * 3,
        (where, output_grad, reads, log_decay),
        specs=(SMEM, HBM, VMEM, HBM),
        scratch=(
            pltpu.VMEM((tokens, width), BF16),
            pltpu.VMEM((heads, tokens), F32),
            pltpu.SemaphoreType.DMA((2,)),
        ),
    )
    near = [swapped(value, "ctx", flip) for flip, value in enumerate(out, 1)]
    quads = (
        pltpu.VMEM((QUAD, heads, part, states), F32),
        pltpu.VMEM((QUAD, heads, states), F32),
    )
    joined = call(
        quad_kernel, message, (where, sums, decays, *near, writes), specs=(SMEM,), scratch=quads,
    )
    far, middle, close = (earlier(joined, QUAD * ahead) for ahead in (3, 2, 1))
    fixed, slope, quarter = call(
        intra_kernel,
        (plane, plane, struct((heads, part, states), F32)),
        (where, skip_gain, output_grad, conv_out, step_size, later, writes, reads, cumulative)
        + (joined,),
        specs=(SMEM, SMEM, HBM, HBM, HBM, HBM),
        scratch=(
            pltpu.VMEM((tokens, tokens), F32),
            pltpu.VMEM((tokens, width), F32),
            pltpu.VMEM((tokens, width), BF16),
            pltpu.VMEM((tokens, width), BF16),
            pltpu.VMEM((heads, tokens), F32),
            pltpu.VMEM((width, states), F32),
            pltpu.SemaphoreType.DMA((4,)),
        ),
    )
    own, *out = call(
        carry_kernel,
        (piece,) * 4,
        (where, sums, decays, *near, far, close, middle, quarter),
        specs=(SMEM,),
        scratch=quads + (pltpu.VMEM((QUAD, heads, part, states), BF16),),
    )
    parts = [swapped(value, "ctx", flip) for flip, value in enumerate(out, 1)]
    blocks = [struct((count, width), BF16) for count in (FIRST, tokens - FIRST)]
    head, rim, rest, carried = call(
        join_kernel,
        (blocks[0], struct((16, width), BF16), blocks[1], struct((width, states), BF16)),
        (where, own, *parts, writes, fixed, slope, conv_weight),
        specs=(SMEM,),
        scratch=(pltpu.VMEM((FIRST + 16, width), F32),),
    )
    last = call(
        tail_kernel,
        blocks[1],
        (rest, earlier(rim, 1), conv_weight),
        scratch=(pltpu.VMEM((tokens - FIRST + 16, width), F32),),
    )
    sums_of, after = [], head
    for chunk in (head, last):
        near, far, across = (swapped(chunk, "col", flip) for flip in (1, 3, 2))
        block, held = struct(chunk.shape, BF16), struct(chunk.shape, F32)
        partial = call(
            product_kernel,
            struct((chunk.shape[0], proj_weight.shape[0]), F32),
            (where, chunk, near, far, proj_weight, after),
            specs=(SMEM,),
        )
        kept, near, far, over = call(
            finish_kernel,
            (held, block, block, block),
            (where, across, proj_weight, partial),
            specs=(SMEM,),
        )
        came = [swapped(value, "row", flip) for value, flip in ((near, 1), (far, 3), (over, 2))]
        sums_of.append(kept + sum(value.astype(F32) for value in came))
        after = kept
    state, x_grad = call(
        output_kernel,
        (wide, struct((tokens, width), BF16)),
        (sums, decays, carried, head, last, after),
    )
    hidden_grad = jnp.concatenate(sums_of, axis=0).astype(BF16)
    return hidden_grad, x_grad, state.reshape(1, heads, HD, states)


def solution(mesh):
    return jax.shard_map(
        on_device,
        mesh=mesh,
        in_specs=(
            P("ctx", ("row", "col")),
            P("ctx", ("row", "col")),
            P("ctx", None, None),
            P("ctx", None, None),
            P(("row", "col"), "ctx"),
            P(("row", "col"), "ctx"),
            P(("row", "col")),
            P(None, ("row", "col")),
            P(("row", "col"), None, None),
            P("col", "row"),
        ),
        out_specs=(
            P("ctx", ("col", "row")),
            P("ctx", ("row", "col")),
            P("ctx", ("row", "col"), None, None),
        ),
        check_vma=False,
    )
```

time: 85.8 us -> 84.4 us (0.984)
  local copies, waits for them, and re-layouts: 9.98 us -> 4.42 us
  Pallas kernels: 13.9 us -> 16.7 us
  waiting for transfers between devices: 27.7 us -> 29.7 us
    ppermute x18, waiting for transfers between devices: 17.8 us -> 24.6 us  [swapped(): lax.ppermute(value, axis, [(place, place ^ flip) for place in range(count)])]
    ppermute x4, waiting for transfers between devices: 9.94 us -> 5.1 us  [earlier(): lax.ppermute(value, 'ctx', [(place, place - steps) for place in range(ste...]
    unnamed x20, local copies, waits for them, and re-layouts: 6.86 us -> 2.1 us
    pallas_call x8 -> x11, Pallas kernels: 13.9 us -> 16.7 us  [call(): pl.pallas_call(kernel, out_shape=outs, in_specs=list(specs) + [VMEM] * (l...]
  transfers between devices with their start and end apart: 22 -> 22, of which waited for: 12 -> 13; matrix products, arithmetic and copies ran while one was open for 3% -> 2% of each run, Pallas kernels for 11% -> 15%
where the time goes in v2:
time: 84.4 us; the launch traced here: 84.2 us
  starting transfers between devices  31.2 us (37%)
  waiting for transfers between devices  29.7 us (35%)
  Pallas kernels  16.7 us (20%)
  local copies, waits for them, and re-layouts  4.42 us (5%)
  other arithmetic  1.18 us (1%)
  between operations  0.92 us (1%)
    ppermute x18, starting transfers between devices, swapped(): lax.ppermute(value, axis, [(place, place ^ flip) for place in range(count)])  25.1 us
    ppermute x18, waiting for transfers between devices, swapped(): lax.ppermute(value, axis, [(place, place ^ flip) for place in range(count)])  24.6 us
    pallas_call x11, Pallas kernels, call(): pl.pallas_call(kernel, out_shape=outs, in_specs=list(specs) + [VMEM] * (l...  16.7 us
    ppermute x4, starting transfers between devices, earlier(): lax.ppermute(value, 'ctx', [(place, place - steps) for place in range(ste...  6.15 us
    ppermute x4, waiting for transfers between devices, earlier(): lax.ppermute(value, 'ctx', [(place, place - steps) for place in range(ste...  5.1 us
    unnamed x20, local copies, waits for them, and re-layouts  2.1 us
    dynamic_slice x1, local copies, waits for them, and re-layouts, on_device(): writes = lax.dynamic_index_in_dim(input_mix, group, 1, keepdims=False)  1.78 us
  transfers between devices with their start and end apart: 22, of which 13 were waited for; matrix products, arithmetic and copies ran while one was open for 2% of the time, Pallas kernels for 15%

profile of v2, /device:TPU:1, one launch (start us, length us, event | category | flops | bytes accessed | tf_op | source)
XLA Modules:
  0.0 84.2 jit_solution(865674672137112250)
XLA Ops:
  0.6 0.0 copy-start
  0.7 1.2 %copy-done = bf16[512,4,256]{2,1,0:T(4,128)(2,1)S(1)} copy-done((bf16[512,4,256]{2,1,0:T(4,128)(2,1)S(1)}, bf16[512,4,256]{2,1,0:T(4,128)(2,1)}, u32[]{:S(2)}) %copy-start) | copy-done | bytes 1048600
  1.9 0.5 constant_dynamic-slice_fusion.1
  2.4 0.0 copy-start.3
  2.4 0.0 copy-start.4
  2.4 0.0 copy-start.6
  2.5 0.1 pad_add_fusion.where
  2.6 0.8 copy-done.7
  3.4 1.9 %shard_map.121 = (f32[512,256]{1,0:T(8,128)S(1)}, f32[8,512]{1,0:T(8,128)S(1)}, f32[8,256]{1,0:T(8,128)S(1)}, bf16[9,16,256]{2,1,0:T(8,128)(2,1)S(1)}, bf16[9,16...) custom-call(s32[4]{0:T(128)S(1)} %pad_add_fusion.where, bf16[512,512]{1,0:T(8,128)(2,1)S(1)} %copy-done.2, ...), custom_call_target="tpu_custom_call" | custom-call | tf_op jit(solution)/shard_map/pallas_call | solution.py:25
  5.3 3.3 %collective-permute-start = (bf16[9,16,256]{2,1,0:T(8,128)(2,1)S(1)}, bf16[9,16,256]{2,1,0:T(8,128)(2,1)S(1)}, u32[]{:S(2)}, u32[]{:S(2)}) collective-permute-start(bf16[9,16,256]{2,1,0:T(8,128)(2,1)S(1)} %get-tuple-element.32), channel_id=1, source_target_pairs={{0,16},{16,0},{32,48},{48,32},{64,80},{80,64},{96,112},{112,96},{1... | collective-permute-start | bytes 221192 | tf_op jit(solution)/shard_map/ppermute | solution.py:293
  8.6 0.0 collective-permute-start.1
  8.6 1.7 %collective-permute-start.2 = (bf16[9,16,256]{2,1,0:T(8,128)(2,1)S(1)}, bf16[9,16,256]{2,1,0:T(8,128)(2,1)S(1)}, u32[]{:S(2)}, u32[]{:S(2)}) collective-permute-start(bf16[9,16,256]{2,1,0:T(8,128)(2,1)S(1)} %get-tuple-element.34), channel_id=1, source_target_pairs={{0,48},{16,32},{32,16},{48,0},{64,112},{80,96},{96,80},{112,64},{1... | collective-permute-start | bytes 221192 | tf_op jit(solution)/shard_map/ppermute | solution.py:293
  10.3 1.8 %constant_dynamic-slice_fusion = bf16[512,1,256]{2,1,0:T(2,128)(2,1)S(1)} fusion(bf16[512,4,256]{2,1,0:T(4,128)(2,1)} %param.12, s32[]{:T(128)S(6)} %select_n.22), kind=kLoop, calls=%fused_computation.6 | loop fusion | bytes 524292 | tf_op jit(solution)/shard_map/jit(dynamic_index_in_dim)/dynamic_slice | solution.py:308
  12.1 0.0 copy-start.1
  12.2 0.0 collective-permute-done.one
  12.2 0.2 collective-permute-done.1.two
  12.4 1.8 %collective-permute-done.2.three = bf16[9,16,256]{2,1,0:T(8,128)(2,1)S(1)} collective-permute-done((bf16[9,16,256]{2,1,0:T(8,128)(2,1)S(1)}, bf16[9,16,256]{2,1,0:T(8,128)(2,1)S(1)}, u32[]{:S(2)}, u32[]{:S(2)}) %collective-permute-start.2) | collective-permute-done | bytes 73760 | tf_op jit(solution)/shard_map/ppermute | solution.py:293
  14.2 0.6 shard_map.122.after
  14.8 1.3 %collective-permute-start.5 = (bf16[9,16,256]{2,1,0:T(8,128)(2,1)S(1)}, bf16[9,16,256]{2,1,0:T(8,128)(2,1)S(1)}, u32[]{:S(2)}, u32[]{:S(2)}) collective-permute-start(bf16[9,16,256]{2,1,0:T(8,128)(2,1)S(1)} %shard_map.122.after), channel_id=1, source_target_pairs={{128,0},{144,16},{160,32},{176,48},{192,64},{208,80},{224,96},{240... | collective-permute-start | bytes 221192 | tf_op jit(solution)/shard_map/ppermute | solution.py:288
  16.1 1.3 %collective-permute-start.4 = (bf16[9,16,256]{2,1,0:T(8,128)(2,1)S(1)}, bf16[9,16,256]{2,1,0:T(8,128)(2,1)S(1)}, u32[]{:S(2)}, u32[]{:S(2)}) collective-permute-start(bf16[9,16,256]{2,1,0:T(8,128)(2,1)S(1)} %shard_map.122.after), channel_id=1, source_target_pairs={{64,0},{80,16},{96,32},{112,48},{128,64},{144,80},{160,96},{176,11... | collective-permute-start | bytes 221192 | tf_op jit(solution)/shard_map/ppermute | solution.py:288
  17.4 1.3 %collective-permute-start.3 = (bf16[9,16,256]{2,1,0:T(8,128)(2,1)S(1)}, bf16[9,16,256]{2,1,0:T(8,128)(2,1)S(1)}, u32[]{:S(2)}, u32[]{:S(2)}) collective-permute-start(bf16[9,16,256]{2,1,0:T(8,128)(2,1)S(1)} %shard_map.122.after), channel_id=1, source_target_pairs={{192,0},{208,16},{224,32},{240,48},{193,1},{209,17},{225,33},{241,... | collective-permute-start | bytes 221192 | tf_op jit(solution)/shard_map/ppermute | solution.py:288
  18.8 3.5 %shard_map.123 = (f32[512,512]{1,0:T(8,128)S(1)}, f32[512,512]{1,0:T(8,128)S(1)}, f32[8,16,256]{2,1,0:T(8,128)S(1)}) custom-call(s32[4]{0:T(128)S(1)} %pad_add_fusion.where, f32[8]{0:T(128)S(1)} %copy-done.8, bf16[512,512]{1,0:T(8,128)(2,1)S(1)} %copy-done.2, bf16[512,512]{1,0:T(8,128)(2,1)S(1)} %copy-done.3, f32[8,512]{1,0:T(8,128)S(1)} %copy-done.6, ...), custom_call_target="tpu_custom_call" | custom-call | tf_op jit(solution)/shard_map/pallas_call | solution.py:25
  22.2 2.1 %collective-permute-done.5.middle = bf16[9,16,256]{2,1,0:T(8,128)(2,1)S(1)} collective-permute-done((bf16[9,16,256]{2,1,0:T(8,128)(2,1)S(1)}, bf16[9,16,256]{2,1,0:T(8,128)(2,1)S(1)}, u32[]{:S(2)}, u32[]{:S(2)}) %collective-permute-start.5) | collective-permute-done | bytes 73760 | tf_op jit(solution)/shard_map/ppermute | solution.py:288
  24.3 1.8 %collective-permute-done.4.near = bf16[9,16,256]{2,1,0:T(8,128)(2,1)S(1)} collective-permute-done((bf16[9,16,256]{2,1,0:T(8,128)(2,1)S(1)}, bf16[9,16,256]{2,1,0:T(8,128)(2,1)S(1)}, u32[]{:S(2)}, u32[]{:S(2)}) %collective-permute-start.4) | collective-permute-done | bytes 73760 | tf_op jit(solution)/shard_map/ppermute | solution.py:288
  26.1 1.3 %collective-permute-done.3.far = bf16[9,16,256]{2,1,0:T(8,128)(2,1)S(1)} collective-permute-done((bf16[9,16,256]{2,1,0:T(8,128)(2,1)S(1)}, bf16[9,16,256]{2,1,0:T(8,128)(2,1)S(1)}, u32[]{:S(2)}, u32[]{:S(2)}) %collective-permute-start.3) | collective-permute-done | bytes 73760 | tf_op jit(solution)/shard_map/ppermute | solution.py:288
  27.3 0.7 shard_map.124
  28.0 1.7 %collective-permute-start.6 = (bf16[8,16,256]{2,1,0:T(8,128)(2,1)S(1)}, bf16[8,16,256]{2,1,0:T(8,128)(2,1)S(1)}, u32[]{:S(2)}, u32[]{:S(2)}) collective-permute-start(bf16[8,16,256]{2,1,0:T(8,128)(2,1)S(1)} %get-tuple-element.38), channel_id=1, source_target_pairs={{0,16},{16,0},{32,48},{48,32},{64,80},{80,64},{96,112},{112,96},{1... | collective-permute-start | bytes 196616 | tf_op jit(solution)/shard_map/ppermute | solution.py:293
  29.8 1.8 %collective-permute-start.7 = (bf16[8,16,256]{2,1,0:T(8,128)(2,1)S(1)}, bf16[8,16,256]{2,1,0:T(8,128)(2,1)S(1)}, u32[]{:S(2)}, u32[]{:S(2)}) collective-permute-start(bf16[8,16,256]{2,1,0:T(8,128)(2,1)S(1)} %get-tuple-element.39), channel_id=1, source_target_pairs={{0,32},{16,48},{32,0},{48,16},{64,96},{80,112},{96,64},{112,80},{1... | collective-permute-start | bytes 196616 | tf_op jit(solution)/shard_map/ppermute | solution.py:293
  31.6 0.1 collective-permute-start.8
  31.6 0.0 collective-permute-done.6.first
  31.7 2.3 %collective-permute-done.7.second = bf16[8,16,256]{2,1,0:T(8,128)(2,1)S(1)} collective-permute-done((bf16[8,16,256]{2,1,0:T(8,128)(2,1)S(1)}, bf16[8,16,256]{2,1,0:T(8,128)(2,1)S(1)}, u32[]{:S(2)}, u32[]{:S(2)}) %collective-permute-start.7) | collective-permute-done | bytes 65568 | tf_op jit(solution)/shard_map/ppermute | solution.py:293
  33.9 1.7 %collective-permute-done.8.third = bf16[8,16,256]{2,1,0:T(8,128)(2,1)S(1)} collective-permute-done((bf16[8,16,256]{2,1,0:T(8,128)(2,1)S(1)}, bf16[8,16,256]{2,1,0:T(8,128)(2,1)S(1)}, u32[]{:S(2)}, u32[]{:S(2)}) %collective-permute-start.8) | collective-permute-done | bytes 65568 | tf_op jit(solution)/shard_map/ppermute | solution.py:293
  35.6 1.2 %shard_map.125 = (bf16[256,512]{1,0:T(8,128)(2,1)S(1)}, bf16[16,512]{1,0:T(8,128)(2,1)S(1)}, bf16[256,512]{1,0:T(8,128)(2,1)S(1)}, bf16[512,256]{1,0:T(8,128)(2,1)S(1)}) custom-call(s32[4]{0:T(128)S(1)} %pad_add_fusion.where, bf16[8,16,256]{2,1,0:T(8,128)(2,1)S(1)} %get-tuple-element.37.own, bf16[8,16,256]{2,1,0:T(8,128)(2,1)S(1)} %collective-permute-done.6.first, ...), custom_call_target="tpu_custom_call" | custom-call | tf_op jit(solution)/shard_map/pallas_call | solution.py:25
  36.9 2.3 %collective-permute-start.15 = (bf16[16,512]{1,0:T(8,128)(2,1)S(1)}, bf16[16,512]{1,0:T(8,128)(2,1)S(1)}, u32[]{:S(2)}, u32[]{:S(2)}) collective-permute-start(bf16[16,512]{1,0:T(8,128)(2,1)S(1)} %get-tuple-element.49), channel_id=1, source_target_pairs={{16,0},{32,16},{48,32},{64,48},{80,64},{96,80},{112,96},{128,112},... | collective-permute-start | bytes 49160 | tf_op jit(solution)/shard_map/ppermute | solution.py:288
  39.1 2.2 %collective-permute-start.11 = (bf16[256,512]{1,0:T(8,128)(2,1)S(1)}, bf16[256,512]{1,0:T(8,128)(2,1)S(1)}, u32[]{:S(2)}, u32[]{:S(2)}) collective-permute-start(bf16[256,512]{1,0:T(8,128)(2,1)S(1)} %get-tuple-element.43.own.after.head), channel_id=1, source_target_pairs={{0,3},{1,2},{2,1},{3,0},{4,7},{5,6},{6,5},{7,4},{8,11},{9,10},{10,... | collective-permute-start | bytes 786440 | tf_op jit(solution)/shard_map/ppermute | solution.py:293
  41.3 0.0 collective-permute-start.10
  41.4 1.7 %collective-permute-start.9 = (bf16[256,512]{1,0:T(8,128)(2,1)S(1)}, bf16[256,512]{1,0:T(8,128)(2,1)S(1)}, u32[]{:S(2)}, u32[]{:S(2)}) collective-permute-start(bf16[256,512]{1,0:T(8,128)(2,1)S(1)} %get-tuple-element.43.own.after.head), channel_id=1, source_target_pairs={{0,2},{1,3},{2,0},{3,1},{4,6},{5,7},{6,4},{7,5},{8,10},{9,11},{10,... | collective-permute-start | bytes 786440 | tf_op jit(solution)/shard_map/ppermute | solution.py:293
  43.1 0.0 collective-permute-done.15.rim
  43.1 0.4 shard_map.128.own.last
  43.5 2.2 %collective-permute-start.18 = (bf16[256,512]{1,0:T(8,128)(2,1)S(1)}, bf16[256,512]{1,0:T(8,128)(2,1)S(1)}, u32[]{:S(2)}, u32[]{:S(2)}) collective-permute-start(bf16[256,512]{1,0:T(8,128)(2,1)S(1)} %shard_map.128.own.last), channel_id=1, source_target_pairs={{0,3},{1,2},{2,1},{3,0},{4,7},{5,6},{6,5},{7,4},{8,11},{9,10},{10,... | collective-permute-start | bytes 786440 | tf_op jit(solution)/shard_map/ppermute | solution.py:293
  45.7 0.0 collective-permute-start.17
  45.7 3.0 %collective-permute-done.11.far = bf16[256,512]{1,0:T(8,128)(2,1)S(1)} collective-permute-done((bf16[256,512]{1,0:T(8,128)(2,1)S(1)}, bf16[256,512]{1,0:T(8,128)(2,1)S(1)}, u32[]{:S(2)}, u32[]{:S(2)}) %collective-permute-start.11) | collective-permute-done | bytes 262176 | tf_op jit(solution)/shard_map/ppermute | solution.py:293
  48.8 1.2 %collective-permute-start.16 = (bf16[256,512]{1,0:T(8,128)(2,1)S(1)}, bf16[256,512]{1,0:T(8,128)(2,1)S(1)}, u32[]{:S(2)}, u32[]{:S(2)}) collective-permute-start(bf16[256,512]{1,0:T(8,128)(2,1)S(1)} %shard_map.128.own.last), channel_id=1, source_target_pairs={{0,2},{1,3},{2,0},{3,1},{4,6},{5,7},{6,4},{7,5},{8,10},{9,11},{10,... | collective-permute-start | bytes 786440 | tf_op jit(solution)/shard_map/ppermute | solution.py:293
  49.9 0.0 collective-permute-done.10.near
  50.0 2.4 %shard_map.126.total = f32[256,2048]{1,0:T(8,128)S(1)} custom-call(s32[4]{0:T(128)S(1)} %pad_add_fusion.where, bf16[256,512]{1,0:T(8,128)(2,1)S(1)} %get-tuple-element.43.own.after.head, bf16[256,512]{1,0:T(8,128)(2,1)S(1)} %collective-permute-done.10.near, bf16[256,512]{1,0:T(8,128)(2,1)S(1)} %collective-permute-done.11.far, ...), custom_call_target="tpu_custom_call" | custom-call | tf_op jit(solution)/shard_map/pallas_call | solution.py:25
  52.3 3.2 %collective-permute-done.9.across = bf16[256,512]{1,0:T(8,128)(2,1)S(1)} collective-permute-done((bf16[256,512]{1,0:T(8,128)(2,1)S(1)}, bf16[256,512]{1,0:T(8,128)(2,1)S(1)}, u32[]{:S(2)}, u32[]{:S(2)}) %collective-permute-start.9) | collective-permute-done | bytes 262176 | tf_op jit(solution)/shard_map/ppermute | solution.py:293
  55.5 1.3 %shard_map.127 = (f32[256,512]{1,0:T(8,128)S(1)}, bf16[256,512]{1,0:T(8,128)(2,1)S(1)}, bf16[256,512]{1,0:T(8,128)(2,1)S(1)}, bf16[256,512]{1,0:T(8,128)(2,1)S(1)}) custom-call(s32[4]{0:T(128)S(1)} %pad_add_fusion.where, bf16[256,512]{1,0:T(8,128)(2,1)S(1)} %collective-permute-done.9.across, bf16[2048,2048]{1,0:T(8,128)(2,1)S(1)} %copy-done.1, ...), custom_call_target="tpu_custom_call" | custom-call | tf_op jit(solution)/shard_map/pallas_call | solution.py:25
  56.8 1.0 %collective-permute-start.12 = (bf16[256,512]{1,0:T(8,128)(2,1)S(1)}, bf16[256,512]{1,0:T(8,128)(2,1)S(1)}, u32[]{:S(2)}, u32[]{:S(2)}) collective-permute-start(bf16[256,512]{1,0:T(8,128)(2,1)S(1)} %get-tuple-element.45), channel_id=1, source_target_pairs={{0,4},{4,0},{8,12},{12,8},{1,5},{5,1},{9,13},{13,9},{2,6},{6,2},{1... | collective-permute-start | bytes 786440 | tf_op jit(solution)/shard_map/ppermute | solution.py:293
  57.8 1.9 %collective-permute-start.13 = (bf16[256,512]{1,0:T(8,128)(2,1)S(1)}, bf16[256,512]{1,0:T(8,128)(2,1)S(1)}, u32[]{:S(2)}, u32[]{:S(2)}) collective-permute-start(bf16[256,512]{1,0:T(8,128)(2,1)S(1)} %get-tuple-element.46), channel_id=1, source_target_pairs={{0,12},{4,8},{8,4},{12,0},{1,13},{5,9},{9,5},{13,1},{2,14},{6,10},... | collective-permute-start | bytes 786440 | tf_op jit(solution)/shard_map/ppermute | solution.py:293
  59.7 0.0 collective-permute-done.18.far
  59.7 2.5 %collective-permute-start.14 = (bf16[256,512]{1,0:T(8,128)(2,1)S(1)}, bf16[256,512]{1,0:T(8,128)(2,1)S(1)}, u32[]{:S(2)}, u32[]{:S(2)}) collective-permute-start(bf16[256,512]{1,0:T(8,128)(2,1)S(1)} %get-tuple-element.47), channel_id=1, source_target_pairs={{0,8},{4,12},{8,0},{12,4},{1,9},{5,13},{9,1},{13,5},{2,10},{6,14},... | collective-permute-start | bytes 786440 | tf_op jit(solution)/shard_map/ppermute | solution.py:293
  62.2 2.4 %shard_map.129.total = f32[256,2048]{1,0:T(8,128)S(1)} custom-call(s32[4]{0:T(128)S(1)} %pad_add_fusion.where, bf16[256,512]{1,0:T(8,128)(2,1)S(1)} %shard_map.128.own.last, bf16[256,512]{1,0:T(8,128)(2,1)S(1)} %collective-permute-done.17.near, bf16[256,512]{1,0:T(8,128)(2,1)S(1)} %collective-permute-done.18.far, bf16[2048,2048]{1,0:T(8,128)(2,1)S(1)} %copy-done.1, ...), custom_call_target="tpu_custom_call" | custom-call | tf_op jit(solution)/shard_map/pallas_call | solution.py:25
  64.6 2.1 %collective-permute-done.16.across = bf16[256,512]{1,0:T(8,128)(2,1)S(1)} collective-permute-done((bf16[256,512]{1,0:T(8,128)(2,1)S(1)}, bf16[256,512]{1,0:T(8,128)(2,1)S(1)}, u32[]{:S(2)}, u32[]{:S(2)}) %collective-permute-start.16) | collective-permute-done | bytes 262176 | tf_op jit(solution)/shard_map/ppermute | solution.py:293
  66.7 1.3 %shard_map.130 = (f32[256,512]{1,0:T(8,128)S(1)}, bf16[256,512]{1,0:T(8,128)(2,1)S(1)}, bf16[256,512]{1,0:T(8,128)(2,1)S(1)}, bf16[256,512]{1,0:T(8,128)(2,1)S(1)}) custom-call(s32[4]{0:T(128)S(1)} %pad_add_fusion.where, bf16[256,512]{1,0:T(8,128)(2,1)S(1)} %collective-permute-done.16.across, bf16[2048,2048]{1,0:T(8,128)(2,1)S(1)} %copy-done.1, ...), custom_call_target="tpu_custom_call" | custom-call | tf_op jit(solution)/shard_map/pallas_call | solution.py:25
  68.0 1.0 %collective-permute-start.19 = (bf16[256,512]{1,0:T(8,128)(2,1)S(1)}, bf16[256,512]{1,0:T(8,128)(2,1)S(1)}, u32[]{:S(2)}, u32[]{:S(2)}) collective-permute-start(bf16[256,512]{1,0:T(8,128)(2,1)S(1)} %get-tuple-element.51), channel_id=1, source_target_pairs={{0,4},{4,0},{8,12},{12,8},{1,5},{5,1},{9,13},{13,9},{2,6},{6,2},{1... | collective-permute-start | bytes 786440 | tf_op jit(solution)/shard_map/ppermute | solution.py:293
  69.1 1.9 %collective-permute-start.20 = (bf16[256,512]{1,0:T(8,128)(2,1)S(1)}, bf16[256,512]{1,0:T(8,128)(2,1)S(1)}, u32[]{:S(2)}, u32[]{:S(2)}) collective-permute-start(bf16[256,512]{1,0:T(8,128)(2,1)S(1)} %get-tuple-element.52), channel_id=1, source_target_pairs={{0,12},{4,8},{8,4},{12,0},{1,13},{5,9},{9,5},{13,1},{2,14},{6,10},... | collective-permute-start | bytes 786440 | tf_op jit(solution)/shard_map/ppermute | solution.py:293
  71.0 1.1 %shard_map.131 = (f32[512,256]{1,0:T(8,128)}, bf16[512,512]{1,0:T(8,128)(2,1)}) custom-call(f32[512,256]{1,0:T(8,128)S(1)} %get-tuple-element.30.sums, f32[8,256]{1,0:T(8,128)S(1)} %get-tuple-element.31.decays, bf16[512,256]{1,0:T(8,128)(2,1)S(1)} %get-tuple-element.54.carried, bf16[256,512]{1,0:T(8,128)(2,1)S(1)} %get-tuple-element.43.own.after.head, ...), custom_call_target="tpu_custom_call" | custom-call | tf_op jit(solution)/shard_map/pallas_call | solution.py:25
  72.0 0.7 collective-permute-start.21
  72.8 0.1 add_convert_fusion.1
  72.9 2.7 %collective-permute-done.19 = bf16[256,512]{1,0:T(8,128)(2,1)S(1)} collective-permute-done((bf16[256,512]{1,0:T(8,128)(2,1)S(1)}, bf16[256,512]{1,0:T(8,128)(2,1)S(1)}, u32[]{:S(2)}, u32[]{:S(2)}) %collective-permute-start.19) | collective-permute-done | bytes 262176 | tf_op jit(solution)/shard_map/ppermute | solution.py:293
  75.6 1.7 %collective-permute-done.20 = bf16[256,512]{1,0:T(8,128)(2,1)S(1)} collective-permute-done((bf16[256,512]{1,0:T(8,128)(2,1)S(1)}, bf16[256,512]{1,0:T(8,128)(2,1)S(1)}, u32[]{:S(2)}, u32[]{:S(2)}) %collective-permute-start.20) | collective-permute-done | bytes 262176 | tf_op jit(solution)/shard_map/ppermute | solution.py:293
  77.3 5.9 %collective-permute-done.21 = bf16[256,512]{1,0:T(8,128)(2,1)S(1)} collective-permute-done((bf16[256,512]{1,0:T(8,128)(2,1)S(1)}, bf16[256,512]{1,0:T(8,128)(2,1)S(1)}, u32[]{:S(2)}, u32[]{:S(2)}) %collective-permute-start.21) | collective-permute-done | bytes 262176 | tf_op jit(solution)/shard_map/ppermute | solution.py:293
  83.2 0.1 add_convert_fusion
  83.3 0.8 pad_maximum_fusion
  (17 shorter events, 0.1 us)
Async XLA Ops:
  0.6 1.2 %copy-start = (bf16[512,4,256]{2,1,0:T(4,128)(2,1)S(1)}, bf16[512,4,256]{2,1,0:T(4,128)(2,1)}, u32[]{:S(2)}) copy-start(bf16[512,4,256]{2,1,0:T(4,128)(2,1)} %param.13) | copy-start | bytes 3145732
  0.6 1.9 %copy-start.2 = (bf16[512,512]{1,0:T(8,128)(2,1)S(1)}, bf16[512,512]{1,0:T(8,128)(2,1)}, u32[]{:S(2)}) copy-start(bf16[512,512]{1,0:T(8,128)(2,1)} %grad_hbm.3) | copy-start | bytes 1572868
  1.9 16.9 %copy-start.8 = (f32[8]{0:T(128)S(1)}, f32[8]{0:T(128)}, u32[]{:S(2)}) copy-start(f32[8]{0:T(128)} %skips.1) | copy-start | bytes 100
  2.4 16.3 %copy-start.3 = (bf16[512,512]{1,0:T(8,128)(2,1)S(1)}, bf16[512,512]{1,0:T(8,128)(2,1)}, u32[]{:S(2)}) copy-start(bf16[512,512]{1,0:T(8,128)(2,1)} %conv_hbm.1) | copy-start | bytes 1572868
  2.4 16.3 %copy-start.4 = (f32[8,64,256]{2,1,0:T(8,128)S(1)}, f32[8,64,256]{2,1,0:T(8,128)}, u32[]{:S(2)}) copy-start(f32[8,64,256]{2,1,0:T(8,128)} %param.18) | copy-start | bytes 1572868
  2.4 16.3 %copy-start.6 = (f32[8,512]{1,0:T(8,128)S(1)}, f32[8,512]{1,0:T(8,128)}, u32[]{:S(2)}) copy-start(f32[8,512]{1,0:T(8,128)} %step_hbm.1) | copy-start | bytes 49156
  2.6 0.8 copy-start.7
  5.3 6.9 %collective-permute-start = (bf16[9,16,256]{2,1,0:T(8,128)(2,1)S(1)}, bf16[9,16,256]{2,1,0:T(8,128)(2,1)S(1)}, u32[]{:S(2)}, u32[]{:S(2)}) collective-permute-start(bf16[9,16,256]{2,1,0:T(8,128)(2,1)S(1)} %get-tuple-element.32), channel_id=1, source_target_pairs={{0,16},{16,0},{32,48},{48,32},{64,80},{80,64},{96,112},{112,96},{1... | collective-permute-start | bytes 221192 | tf_op jit(solution)/shard_map/ppermute | solution.py:293
  8.6 3.8 %collective-permute-start.1 = (bf16[9,16,256]{2,1,0:T(8,128)(2,1)S(1)}, bf16[9,16,256]{2,1,0:T(8,128)(2,1)S(1)}, u32[]{:S(2)}, u32[]{:S(2)}) collective-permute-start(bf16[9,16,256]{2,1,0:T(8,128)(2,1)S(1)} %get-tuple-element.33), channel_id=1, source_target_pairs={{0,32},{16,48},{32,0},{48,16},{64,96},{80,112},{96,64},{112,80},{1... | collective-permute-start | bytes 221192 | tf_op jit(solution)/shard_map/ppermute | solution.py:293
  8.6 5.6 %collective-permute-start.2 = (bf16[9,16,256]{2,1,0:T(8,128)(2,1)S(1)}, bf16[9,16,256]{2,1,0:T(8,128)(2,1)S(1)}, u32[]{:S(2)}, u32[]{:S(2)}) collective-permute-start(bf16[9,16,256]{2,1,0:T(8,128)(2,1)S(1)} %get-tuple-element.34), channel_id=1, source_target_pairs={{0,48},{16,32},{32,16},{48,0},{64,112},{80,96},{96,80},{112,64},{1... | collective-permute-start | bytes 221192 | tf_op jit(solution)/shard_map/ppermute | solution.py:293
  10.3 25.3 %copy-start.5 = (f32[4,512]{1,0:T(4,128)S(1)}, f32[4,512]{1,0:T(4,128)}, u32[]{:S(2)}) copy-start(f32[4,512]{1,0:T(4,128)} %taps.3) | copy-start | bytes 24580
  12.1 37.8 %copy-start.1 = (bf16[2048,2048]{1,0:T(8,128)(2,1)S(1)}, bf16[2048,2048]{1,0:T(8,128)(2,1)}, u32[]{:S(2)}) copy-start(bf16[2048,2048]{1,0:T(8,128)(2,1)} %weight.7) | copy-start | bytes 25165828
  14.8 9.5 %collective-permute-start.5 = (bf16[9,16,256]{2,1,0:T(8,128)(2,1)S(1)}, bf16[9,16,256]{2,1,0:T(8,128)(2,1)S(1)}, u32[]{:S(2)}, u32[]{:S(2)}) collective-permute-start(bf16[9,16,256]{2,1,0:T(8,128)(2,1)S(1)} %shard_map.122.after), channel_id=1, source_target_pairs={{128,0},{144,16},{160,32},{176,48},{192,64},{208,80},{224,96},{240... | collective-permute-start | bytes 221192 | tf_op jit(solution)/shard_map/ppermute | solution.py:288
  16.1 9.9 %collective-permute-start.4 = (bf16[9,16,256]{2,1,0:T(8,128)(2,1)S(1)}, bf16[9,16,256]{2,1,0:T(8,128)(2,1)S(1)}, u32[]{:S(2)}, u32[]{:S(2)}) collective-permute-start(bf16[9,16,256]{2,1,0:T(8,128)(2,1)S(1)} %shard_map.122.after), channel_id=1, source_target_pairs={{64,0},{80,16},{96,32},{112,48},{128,64},{144,80},{160,96},{176,11... | collective-permute-start | bytes 221192 | tf_op jit(solution)/shard_map/ppermute | solution.py:288
  17.4 9.9 %collective-permute-start.3 = (bf16[9,16,256]{2,1,0:T(8,128)(2,1)S(1)}, bf16[9,16,256]{2,1,0:T(8,128)(2,1)S(1)}, u32[]{:S(2)}, u32[]{:S(2)}) collective-permute-start(bf16[9,16,256]{2,1,0:T(8,128)(2,1)S(1)} %shard_map.122.after), channel_id=1, source_target_pairs={{192,0},{208,16},{224,32},{240,48},{193,1},{209,17},{225,33},{241,... | collective-permute-start | bytes 221192 | tf_op jit(solution)/shard_map/ppermute | solution.py:288
  28.0 3.6 %collective-permute-start.6 = (bf16[8,16,256]{2,1,0:T(8,128)(2,1)S(1)}, bf16[8,16,256]{2,1,0:T(8,128)(2,1)S(1)}, u32[]{:S(2)}, u32[]{:S(2)}) collective-permute-start(bf16[8,16,256]{2,1,0:T(8,128)(2,1)S(1)} %get-tuple-element.38), channel_id=1, source_target_pairs={{0,16},{16,0},{32,48},{48,32},{64,80},{80,64},{96,112},{112,96},{1... | collective-permute-start | bytes 196616 | tf_op jit(solution)/shard_map/ppermute | solution.py:293
  29.8 4.2 %collective-permute-start.7 = (bf16[8,16,256]{2,1,0:T(8,128)(2,1)S(1)}, bf16[8,16,256]{2,1,0:T(8,128)(2,1)S(1)}, u32[]{:S(2)}, u32[]{:S(2)}) collective-permute-start(bf16[8,16,256]{2,1,0:T(8,128)(2,1)S(1)} %get-tuple-element.39), channel_id=1, source_target_pairs={{0,32},{16,48},{32,0},{48,16},{64,96},{80,112},{96,64},{112,80},{1... | collective-permute-start | bytes 196616 | tf_op jit(solution)/shard_map/ppermute | solution.py:293
  31.6 4.1 %collective-permute-start.8 = (bf16[8,16,256]{2,1,0:T(8,128)(2,1)S(1)}, bf16[8,16,256]{2,1,0:T(8,128)(2,1)S(1)}, u32[]{:S(2)}, u32[]{:S(2)}) collective-permute-start(bf16[8,16,256]{2,1,0:T(8,128)(2,1)S(1)} %get-tuple-element.40), channel_id=1, source_target_pairs={{0,48},{16,32},{32,16},{48,0},{64,112},{80,96},{96,80},{112,64},{1... | collective-permute-start | bytes 196616 | tf_op jit(solution)/shard_map/ppermute | solution.py:293
  36.9 6.2 %collective-permute-start.15 = (bf16[16,512]{1,0:T(8,128)(2,1)S(1)}, bf16[16,512]{1,0:T(8,128)(2,1)S(1)}, u32[]{:S(2)}, u32[]{:S(2)}) collective-permute-start(bf16[16,512]{1,0:T(8,128)(2,1)S(1)} %get-tuple-element.49), channel_id=1, source_target_pairs={{16,0},{32,16},{48,32},{64,48},{80,64},{96,80},{112,96},{128,112},... | collective-permute-start | bytes 49160 | tf_op jit(solution)/shard_map/ppermute | solution.py:288
  39.1 9.6 %collective-permute-start.11 = (bf16[256,512]{1,0:T(8,128)(2,1)S(1)}, bf16[256,512]{1,0:T(8,128)(2,1)S(1)}, u32[]{:S(2)}, u32[]{:S(2)}) collective-permute-start(bf16[256,512]{1,0:T(8,128)(2,1)S(1)} %get-tuple-element.43.own.after.head), channel_id=1, source_target_pairs={{0,3},{1,2},{2,1},{3,0},{4,7},{5,6},{6,5},{7,4},{8,11},{9,10},{10,... | collective-permute-start | bytes 786440 | tf_op jit(solution)/shard_map/ppermute | solution.py:293
  41.3 8.6 %collective-permute-start.10 = (bf16[256,512]{1,0:T(8,128)(2,1)S(1)}, bf16[256,512]{1,0:T(8,128)(2,1)S(1)}, u32[]{:S(2)}, u32[]{:S(2)}) collective-permute-start(bf16[256,512]{1,0:T(8,128)(2,1)S(1)} %get-tuple-element.43.own.after.head), channel_id=1, source_target_pairs={{0,1},{1,0},{2,3},{3,2},{4,5},{5,4},{6,7},{7,6},{8,9},{9,8},{10,11... | collective-permute-start | bytes 786440 | tf_op jit(solution)/shard_map/ppermute | solution.py:293
  41.4 14.1 %collective-permute-start.9 = (bf16[256,512]{1,0:T(8,128)(2,1)S(1)}, bf16[256,512]{1,0:T(8,128)(2,1)S(1)}, u32[]{:S(2)}, u32[]{:S(2)}) collective-permute-start(bf16[256,512]{1,0:T(8,128)(2,1)S(1)} %get-tuple-element.43.own.after.head), channel_id=1, source_target_pairs={{0,2},{1,3},{2,0},{3,1},{4,6},{5,7},{6,4},{7,5},{8,10},{9,11},{10,... | collective-permute-start | bytes 786440 | tf_op jit(solution)/shard_map/ppermute | solution.py:293
  43.5 16.2 %collective-permute-start.18 = (bf16[256,512]{1,0:T(8,128)(2,1)S(1)}, bf16[256,512]{1,0:T(8,128)(2,1)S(1)}, u32[]{:S(2)}, u32[]{:S(2)}) collective-permute-start(bf16[256,512]{1,0:T(8,128)(2,1)S(1)} %shard_map.128.own.last), channel_id=1, source_target_pairs={{0,3},{1,2},{2,1},{3,0},{4,7},{5,6},{6,5},{7,4},{8,11},{9,10},{10,... | collective-permute-start | bytes 786440 | tf_op jit(solution)/shard_map/ppermute | solution.py:293
  45.7 16.5 %collective-permute-start.17 = (bf16[256,512]{1,0:T(8,128)(2,1)S(1)}, bf16[256,512]{1,0:T(8,128)(2,1)S(1)}, u32[]{:S(2)}, u32[]{:S(2)}) collective-permute-start(bf16[256,512]{1,0:T(8,128)(2,1)S(1)} %shard_map.128.own.last), channel_id=1, source_target_pairs={{0,1},{1,0},{2,3},{3,2},{4,5},{5,4},{6,7},{7,6},{8,9},{9,8},{10,11... | collective-permute-start | bytes 786440 | tf_op jit(solution)/shard_map/ppermute | solution.py:293
  48.8 18.0 %collective-permute-start.16 = (bf16[256,512]{1,0:T(8,128)(2,1)S(1)}, bf16[256,512]{1,0:T(8,128)(2,1)S(1)}, u32[]{:S(2)}, u32[]{:S(2)}) collective-permute-start(bf16[256,512]{1,0:T(8,128)(2,1)S(1)} %shard_map.128.own.last), channel_id=1, source_target_pairs={{0,2},{1,3},{2,0},{3,1},{4,6},{5,7},{6,4},{7,5},{8,10},{9,11},{10,... | collective-permute-start | bytes 786440 | tf_op jit(solution)/shard_map/ppermute | solution.py:293
  56.8 15.2 %collective-permute-start.12 = (bf16[256,512]{1,0:T(8,128)(2,1)S(1)}, bf16[256,512]{1,0:T(8,128)(2,1)S(1)}, u32[]{:S(2)}, u32[]{:S(2)}) collective-permute-start(bf16[256,512]{1,0:T(8,128)(2,1)S(1)} %get-tuple-element.45), channel_id=1, source_target_pairs={{0,4},{4,0},{8,12},{12,8},{1,5},{5,1},{9,13},{13,9},{2,6},{6,2},{1... | collective-permute-start | bytes 786440 | tf_op jit(solution)/shard_map/ppermute | solution.py:293
  57.8 14.9 %collective-permute-start.13 = (bf16[256,512]{1,0:T(8,128)(2,1)S(1)}, bf16[256,512]{1,0:T(8,128)(2,1)S(1)}, u32[]{:S(2)}, u32[]{:S(2)}) collective-permute-start(bf16[256,512]{1,0:T(8,128)(2,1)S(1)} %get-tuple-element.46), channel_id=1, source_target_pairs={{0,12},{4,8},{8,4},{12,0},{1,13},{5,9},{9,5},{13,1},{2,14},{6,10},... | collective-permute-start | bytes 786440 | tf_op jit(solution)/shard_map/ppermute | solution.py:293
  59.7 13.0 %collective-permute-start.14 = (bf16[256,512]{1,0:T(8,128)(2,1)S(1)}, bf16[256,512]{1,0:T(8,128)(2,1)S(1)}, u32[]{:S(2)}, u32[]{:S(2)}) collective-permute-start(bf16[256,512]{1,0:T(8,128)(2,1)S(1)} %get-tuple-element.47), channel_id=1, source_target_pairs={{0,8},{4,12},{8,0},{12,4},{1,9},{5,13},{9,1},{13,5},{2,10},{6,14},... | collective-permute-start | bytes 786440 | tf_op jit(solution)/shard_map/ppermute | solution.py:293
  68.0 7.5 %collective-permute-start.19 = (bf16[256,512]{1,0:T(8,128)(2,1)S(1)}, bf16[256,512]{1,0:T(8,128)(2,1)S(1)}, u32[]{:S(2)}, u32[]{:S(2)}) collective-permute-start(bf16[256,512]{1,0:T(8,128)(2,1)S(1)} %get-tuple-element.51), channel_id=1, source_target_pairs={{0,4},{4,0},{8,12},{12,8},{1,5},{5,1},{9,13},{13,9},{2,6},{6,2},{1... | collective-permute-start | bytes 786440 | tf_op jit(solution)/shard_map/ppermute | solution.py:293
  69.1 8.2 %collective-permute-start.20 = (bf16[256,512]{1,0:T(8,128)(2,1)S(1)}, bf16[256,512]{1,0:T(8,128)(2,1)S(1)}, u32[]{:S(2)}, u32[]{:S(2)}) collective-permute-start(bf16[256,512]{1,0:T(8,128)(2,1)S(1)} %get-tuple-element.52), channel_id=1, source_target_pairs={{0,12},{4,8},{8,4},{12,0},{1,13},{5,9},{9,5},{13,1},{2,14},{6,10},... | collective-permute-start | bytes 786440 | tf_op jit(solution)/shard_map/ppermute | solution.py:293
  72.0 11.2 %collective-permute-start.21 = (bf16[256,512]{1,0:T(8,128)(2,1)S(1)}, bf16[256,512]{1,0:T(8,128)(2,1)S(1)}, u32[]{:S(2)}, u32[]{:S(2)}) collective-permute-start(bf16[256,512]{1,0:T(8,128)(2,1)S(1)} %get-tuple-element.53), channel_id=1, source_target_pairs={{0,8},{4,12},{8,0},{12,4},{1,9},{5,13},{9,1},{13,5},{2,10},{6,14},... | collective-permute-start | bytes 786440 | tf_op jit(solution)/shard_map/ppermute | solution.py:293

commit v3 on v2

--- a/solution.py
+++ b/solution.py
@@ -51,10 +51,16 @@
 
 
 def decay_rows(per_head):
-    wide = jnp.broadcast_to(per_head, (per_head.shape[0], 256))
-    high = wide.astype(BF16)
-    low = (wide - high.astype(F32)).astype(BF16)
-    return jnp.concatenate([high.astype(F32), low.astype(F32)], axis=0).astype(BF16)
+    wide = per_head
+    high = wide.astype(BF16).astype(F32)
+    return jnp.concatenate([high, wide - high], axis=1).astype(BF16)
+
+
+def decays_of(rows):
+    parts = rows.astype(F32)
+    half = parts.shape[1] // 2
+    total = parts[:, :half] + parts[:, half:]
+    return jnp.concatenate([total, total], axis=1)
 
 
 def block_kernel(
@@ -84,14 +90,14 @@
     sums[...] = lax.dot_general(
         weighted, reads[...], (((0,), (0,)), ((), ())), preferred_element_type=F32
     )
-    rows = decay_rows(last)
+    rows = decay_rows(jnp.broadcast_to(last, (heads, decays.shape[1] // 2)))
     me = where[0]
     for flip, sent in ((1, one), (2, two), (3, three)):
         quarter = jnp.bitwise_xor(me, flip)
         for head in range(heads):
             start = pl.multiple_of(head * HD + quarter * part, part)
-            sent[head] = sums[pl.ds(start, part), :].astype(BF16)
-        sent[heads] = rows
+            sent[head * part : (head + 1) * part] = sums[pl.ds(start, part), :].astype(BF16)
+        sent[heads * part :] = rows
 
 
 def intra_kernel(
@@ -168,22 +174,21 @@
     for flip, came in enumerate(received, 1):
         other = jnp.bitwise_xor(me, flip)
         for head in range(heads):
-            values[other, head] = came[head].astype(F32)
-        tail = came[heads].astype(F32)
-        scales[other] = tail[:heads] + tail[heads:]
+            values[other, head] = came[head * part : (head + 1) * part].astype(F32)
+        scales[other] = decays_of(came[heads * part :])
 
 
 def quad_kernel(where, sums, decays, one, two, three, after, sent, values, scales):
     heads = decays.shape[0]
+    part = HD // QUAD
     gather_quad(where[0], sums, decays, (one, two, three), values, scales)
     for head in range(heads):
         total = values[3, head]
         for block in (2, 1, 0):
             total = values[block, head] + scales[block][head : head + 1] * total
-        sent[head] = total.astype(BF16)
+        sent[head * part : (head + 1) * part] = total.astype(BF16)
     product = scales[0] * scales[1] * scales[2] * scales[3]
-    high = product.astype(BF16).astype(F32)
-    sent[heads] = jnp.concatenate([high, product - high], axis=0).astype(BF16)
+    sent[heads * part :] = decay_rows(product[:, : product.shape[1] // 2])
 
 
 def carry_kernel(
@@ -191,17 +196,18 @@
     values, scales, carries,
 ):
     heads = decays.shape[0]
+    part = HD // QUAD
     me, quad = where[0], where[1]
     gather_quad(me, sums, decays, (one, two, three), values, scales)
     jumps = []
     for ahead, came in ((3, far), (2, middle), (1, near)):
-        tail = came[heads].astype(F32)
         present = jnp.full(decays.shape, quad + ahead, jnp.int32) < QUAD
-        jumps.append((came, jnp.where(present, tail[:heads] + tail[heads:], 1.0)))
+        jumps.append((came, jnp.where(present, decays_of(came[heads * part :]), 1.0)))
     for head in range(heads):
         carry = later[head]
         for came, scale in jumps:
-            carry = came[head].astype(F32) + scale[head : head + 1] * carry
+            sent = came[head * part : (head + 1) * part].astype(F32)
+            carry = sent + scale[head : head + 1] * carry
         carries[3, head] = carry.astype(BF16)
         for block in (3, 2, 1):
             carry = values[block, head] + scales[block][head : head + 1] * carry
@@ -254,7 +260,7 @@
     x_grad[head.shape[0] :] = last[...]
 
 
-def product_kernel(where, own, near, far, weight, after, total):
+def product_kernel(where, own, far, near, weight, after, total):
     column = where[3]
     width = own.shape[1]
     for place in range(4):
@@ -308,7 +314,7 @@
     writes = lax.dynamic_index_in_dim(input_mix, group, 1, keepdims=False)
     later = later_grad.reshape(width, states)
 
-    message = struct((heads + 1, part, states), BF16)
+    message = struct((heads * part + heads, states), BF16)
     piece = struct((heads, part, states), BF16)
     wide = struct((width, states), F32)
     plane = struct((tokens, width), F32)
@@ -377,7 +383,7 @@
         partial = call(
             product_kernel,
             struct((chunk.shape[0], proj_weight.shape[0]), F32),
-            (where, chunk, near, far, proj_weight, after),
+            (where, chunk, far, near, proj_weight, after),
             specs=(SMEM,),
         )
         kept, near, far, over = call(
@@ -387,13 +393,16 @@
             specs=(SMEM,),
         )
         came = [swapped(value, "row", flip) for value, flip in ((near, 1), (far, 3), (over, 2))]
-        sums_of.append(kept + sum(value.astype(F32) for value in came))
+        sums_of.append((kept, *came))
         after = kept
     state, x_grad = call(
         output_kernel,
         (wide, struct((tokens, width), BF16)),
-        (sums, decays, carried, head, last, after),
-    )
+        (sums, decays, carried, head, last, came[0]),
+    )
+    kept, *came = sums_of[-1]
+    sums_of[-1] = lax.optimization_barrier((kept, *came, state))[:-1]
+    sums_of = [kept + sum(value.astype(F32) for value in came) for kept, *came in sums_of]
     hidden_grad = jnp.concatenate(sums_of, axis=0).astype(BF16)
     return hidden_grad, x_grad, state.reshape(1, heads, HD, states)
 

time: 84.4 us -> 85 us (level)
  starting transfers between devices: 31.2 us -> 33.7 us
  waiting for transfers between devices: 29.7 us -> 27.8 us
    ppermute x18, starting transfers between devices: 25.1 us -> 27.5 us  [swapped(): lax.ppermute(value, axis, [(place, place ^ flip) for place in range(count)])]
    ppermute x18, waiting for transfers between devices: 24.6 us -> 23.2 us  [swapped(): lax.ppermute(value, axis, [(place, place ^ flip) for place in range(count)])]
  transfers between devices with their start and end apart: 22 -> 22, of which waited for: 13 -> 13; matrix products, arithmetic and copies ran while one was open for 2% -> 2% of each run, Pallas kernels for 15% -> 14%
where the time goes in v3:
time: 85 us; the launch traced here: 84.8 us
  starting transfers between devices  33.7 us (40%)
  waiting for transfers between devices  27.8 us (33%)
  Pallas kernels  16.7 us (20%)
  local copies, waits for them, and re-layouts  4.57 us (5%)
  other arithmetic  1.19 us (1%)
  between operations  0.92 us (1%)
    ppermute x18, starting transfers between devices, swapped(): lax.ppermute(value, axis, [(place, place ^ flip) for place in range(count)])  27.5 us
    ppermute x18, waiting for transfers between devices, swapped(): lax.ppermute(value, axis, [(place, place ^ flip) for place in range(count)])  23.2 us
    pallas_call x11, Pallas kernels, call(): pl.pallas_call(kernel, out_shape=outs, in_specs=list(specs) + [VMEM] * (l...  16.7 us
    ppermute x4, starting transfers between devices, earlier(): lax.ppermute(value, 'ctx', [(place, place - steps) for place in range(ste...  6.14 us
    ppermute x4, waiting for transfers between devices, earlier(): lax.ppermute(value, 'ctx', [(place, place - steps) for place in range(ste...  4.57 us
    unnamed x20, local copies, waits for them, and re-layouts  2.11 us
    dynamic_slice x1, local copies, waits for them, and re-layouts, on_device(): writes = lax.dynamic_index_in_dim(input_mix, group, 1, keepdims=False)  1.92 us
  transfers between devices with their start and end apart: 22, of which 13 were waited for; matrix products, arithmetic and copies ran while one was open for 2% of the time, Pallas kernels for 14%

profile of v3, /device:TPU:1, one launch (start us, length us, event | category | flops | bytes accessed | tf_op | source)
XLA Modules:
  0.0 84.8 jit_solution(7627770677092576256)
XLA Ops:
  0.6 0.0 copy-start
  0.7 1.2 %copy-done = bf16[512,4,256]{2,1,0:T(4,128)(2,1)S(1)} copy-done((bf16[512,4,256]{2,1,0:T(4,128)(2,1)S(1)}, bf16[512,4,256]{2,1,0:T(4,128)(2,1)}, u32[]{:S(2)}) %copy-start) | copy-done | bytes 1048600
  1.9 0.5 constant_dynamic-slice_fusion.1
  2.4 0.0 copy-start.3
  2.4 0.0 copy-start.4
  2.4 0.0 copy-start.6
  2.5 0.1 pad_add_fusion.where
  2.6 0.8 copy-done.7
  3.4 1.9 %shard_map.121 = (f32[512,256]{1,0:T(8,128)S(1)}, f32[8,512]{1,0:T(8,128)S(1)}, f32[8,256]{1,0:T(8,128)S(1)}, bf16[136,256]{1,0:T(8,128)(2,1)S(1)}, bf16[136,256...) custom-call(s32[4]{0:T(128)S(1)} %pad_add_fusion.where, bf16[512,512]{1,0:T(8,128)(2,1)S(1)} %copy-done.2, ...), custom_call_target="tpu_custom_call" | custom-call | tf_op jit(solution)/shard_map/pallas_call | solution.py:25
  5.3 3.3 %collective-permute-start = (bf16[136,256]{1,0:T(8,128)(2,1)S(1)}, bf16[136,256]{1,0:T(8,128)(2,1)S(1)}, u32[]{:S(2)}, u32[]{:S(2)}) collective-permute-start(bf16[136,256]{1,0:T(8,128)(2,1)S(1)} %get-tuple-element.36), channel_id=1, source_target_pairs={{0,16},{16,0},{32,48},{48,32},{64,80},{80,64},{96,112},{112,96},{1... | collective-permute-start | bytes 208904 | tf_op jit(solution)/shard_map/ppermute | solution.py:299
  8.6 0.0 collective-permute-start.1
  8.6 1.7 %collective-permute-start.2 = (bf16[136,256]{1,0:T(8,128)(2,1)S(1)}, bf16[136,256]{1,0:T(8,128)(2,1)S(1)}, u32[]{:S(2)}, u32[]{:S(2)}) collective-permute-start(bf16[136,256]{1,0:T(8,128)(2,1)S(1)} %get-tuple-element.38), channel_id=1, source_target_pairs={{0,48},{16,32},{32,16},{48,0},{64,112},{80,96},{96,80},{112,64},{1... | collective-permute-start | bytes 208904 | tf_op jit(solution)/shard_map/ppermute | solution.py:299
  10.3 1.9 %constant_dynamic-slice_fusion = bf16[512,1,256]{2,1,0:T(2,128)(2,1)S(1)} fusion(bf16[512,4,256]{2,1,0:T(4,128)(2,1)} %param.12, s32[]{:T(128)S(6)} %select_n.22), kind=kLoop, calls=%fused_computation.6 | loop fusion | bytes 524292 | tf_op jit(solution)/shard_map/jit(dynamic_index_in_dim)/dynamic_slice | solution.py:314
  12.3 0.0 collective-permute-done.one
  12.3 0.0 collective-permute-done.1.two
  12.4 1.7 %collective-permute-done.2.three = bf16[136,256]{1,0:T(8,128)(2,1)S(1)} collective-permute-done((bf16[136,256]{1,0:T(8,128)(2,1)S(1)}, bf16[136,256]{1,0:T(8,128)(2,1)S(1)}, u32[]{:S(2)}, u32[]{:S(2)}) %collective-permute-start.2) | collective-permute-done | bytes 69664 | tf_op jit(solution)/shard_map/ppermute | solution.py:299
  14.0 0.6 shard_map.122.after
  14.7 1.3 %collective-permute-start.3 = (bf16[136,256]{1,0:T(8,128)(2,1)S(1)}, bf16[136,256]{1,0:T(8,128)(2,1)S(1)}, u32[]{:S(2)}, u32[]{:S(2)}) collective-permute-start(bf16[136,256]{1,0:T(8,128)(2,1)S(1)} %shard_map.122.after), channel_id=1, source_target_pairs={{192,0},{208,16},{224,32},{240,48},{193,1},{209,17},{225,33},{241,... | collective-permute-start | bytes 208904 | tf_op jit(solution)/shard_map/ppermute | solution.py:294
  16.0 1.3 %collective-permute-start.4 = (bf16[136,256]{1,0:T(8,128)(2,1)S(1)}, bf16[136,256]{1,0:T(8,128)(2,1)S(1)}, u32[]{:S(2)}, u32[]{:S(2)}) collective-permute-start(bf16[136,256]{1,0:T(8,128)(2,1)S(1)} %shard_map.122.after), channel_id=1, source_target_pairs={{64,0},{80,16},{96,32},{112,48},{128,64},{144,80},{160,96},{176,11... | collective-permute-start | bytes 208904 | tf_op jit(solution)/shard_map/ppermute | solution.py:294
  17.3 1.3 %collective-permute-start.5 = (bf16[136,256]{1,0:T(8,128)(2,1)S(1)}, bf16[136,256]{1,0:T(8,128)(2,1)S(1)}, u32[]{:S(2)}, u32[]{:S(2)}) collective-permute-start(bf16[136,256]{1,0:T(8,128)(2,1)S(1)} %shard_map.122.after), channel_id=1, source_target_pairs={{128,0},{144,16},{160,32},{176,48},{192,64},{208,80},{224,96},{240... | collective-permute-start | bytes 208904 | tf_op jit(solution)/shard_map/ppermute | solution.py:294
  18.6 3.5 %shard_map.123 = (f32[512,512]{1,0:T(8,128)S(1)}, f32[512,512]{1,0:T(8,128)S(1)}, f32[8,16,256]{2,1,0:T(8,128)S(1)}) custom-call(s32[4]{0:T(128)S(1)} %pad_add_fusion.where, f32[8]{0:T(128)S(1)} %copy-done.8, bf16[512,512]{1,0:T(8,128)(2,1)S(1)} %copy-done.2, bf16[512,512]{1,0:T(8,128)(2,1)S(1)} %copy-done.3, f32[8,512]{1,0:T(8,128)S(1)} %copy-done.6, ...), custom_call_target="tpu_custom_call" | custom-call | tf_op jit(solution)/shard_map/pallas_call | solution.py:25
  22.1 0.4 collective-permute-done.3.far
  22.5 1.8 %collective-permute-done.4.near = bf16[136,256]{1,0:T(8,128)(2,1)S(1)} collective-permute-done((bf16[136,256]{1,0:T(8,128)(2,1)S(1)}, bf16[136,256]{1,0:T(8,128)(2,1)S(1)}, u32[]{:S(2)}, u32[]{:S(2)}) %collective-permute-start.4) | collective-permute-done | bytes 69664 | tf_op jit(solution)/shard_map/ppermute | solution.py:294
  24.3 2.3 %collective-permute-done.5.middle = bf16[136,256]{1,0:T(8,128)(2,1)S(1)} collective-permute-done((bf16[136,256]{1,0:T(8,128)(2,1)S(1)}, bf16[136,256]{1,0:T(8,128)(2,1)S(1)}, u32[]{:S(2)}, u32[]{:S(2)}) %collective-permute-start.5) | collective-permute-done | bytes 69664 | tf_op jit(solution)/shard_map/ppermute | solution.py:294
  26.6 0.7 shard_map.124
  27.3 1.2 %collective-permute-start.6 = (bf16[8,16,256]{2,1,0:T(8,128)(2,1)S(1)}, bf16[8,16,256]{2,1,0:T(8,128)(2,1)S(1)}, u32[]{:S(2)}, u32[]{:S(2)}) collective-permute-start(bf16[8,16,256]{2,1,0:T(8,128)(2,1)S(1)} %get-tuple-element.42), channel_id=1, source_target_pairs={{0,16},{16,0},{32,48},{48,32},{64,80},{80,64},{96,112},{112,96},{1... | collective-permute-start | bytes 196616 | tf_op jit(solution)/shard_map/ppermute | solution.py:299
  28.5 3.4 %collective-permute-start.7 = (bf16[8,16,256]{2,1,0:T(8,128)(2,1)S(1)}, bf16[8,16,256]{2,1,0:T(8,128)(2,1)S(1)}, u32[]{:S(2)}, u32[]{:S(2)}) collective-permute-start(bf16[8,16,256]{2,1,0:T(8,128)(2,1)S(1)} %get-tuple-element.43), channel_id=1, source_target_pairs={{0,32},{16,48},{32,0},{48,16},{64,96},{80,112},{96,64},{112,80},{1... | collective-permute-start | bytes 196616 | tf_op jit(solution)/shard_map/ppermute | solution.py:299
  31.9 0.1 collective-permute-start.8
  31.9 0.0 collective-permute-done.6.first
  31.9 2.3 %collective-permute-done.7.second = bf16[8,16,256]{2,1,0:T(8,128)(2,1)S(1)} collective-permute-done((bf16[8,16,256]{2,1,0:T(8,128)(2,1)S(1)}, bf16[8,16,256]{2,1,0:T(8,128)(2,1)S(1)}, u32[]{:S(2)}, u32[]{:S(2)}) %collective-permute-start.7) | collective-permute-done | bytes 65568 | tf_op jit(solution)/shard_map/ppermute | solution.py:299
  34.2 1.7 %collective-permute-done.8.third = bf16[8,16,256]{2,1,0:T(8,128)(2,1)S(1)} collective-permute-done((bf16[8,16,256]{2,1,0:T(8,128)(2,1)S(1)}, bf16[8,16,256]{2,1,0:T(8,128)(2,1)S(1)}, u32[]{:S(2)}, u32[]{:S(2)}) %collective-permute-start.8) | collective-permute-done | bytes 65568 | tf_op jit(solution)/shard_map/ppermute | solution.py:299
  35.9 1.2 %shard_map.125 = (bf16[256,512]{1,0:T(8,128)(2,1)S(1)}, bf16[16,512]{1,0:T(8,128)(2,1)S(1)}, bf16[256,512]{1,0:T(8,128)(2,1)S(1)}, bf16[512,256]{1,0:T(8,128)(2,1)S(1)}) custom-call(s32[4]{0:T(128)S(1)} %pad_add_fusion.where, bf16[8,16,256]{2,1,0:T(8,128)(2,1)S(1)} %get-tuple-element.41.own, bf16[8,16,256]{2,1,0:T(8,128)(2,1)S(1)} %collective-permute-done.6.first, ...), custom_call_target="tpu_custom_call" | custom-call | tf_op jit(solution)/shard_map/pallas_call | solution.py:25
  37.1 2.3 %collective-permute-start.15 = (bf16[16,512]{1,0:T(8,128)(2,1)S(1)}, bf16[16,512]{1,0:T(8,128)(2,1)S(1)}, u32[]{:S(2)}, u32[]{:S(2)}) collective-permute-start(bf16[16,512]{1,0:T(8,128)(2,1)S(1)} %get-tuple-element.53), channel_id=1, source_target_pairs={{16,0},{32,16},{48,32},{64,48},{80,64},{96,80},{112,96},{128,112},... | collective-permute-start | bytes 49160 | tf_op jit(solution)/shard_map/ppermute | solution.py:294
  39.4 2.6 %collective-permute-start.10 = (bf16[256,512]{1,0:T(8,128)(2,1)S(1)}, bf16[256,512]{1,0:T(8,128)(2,1)S(1)}, u32[]{:S(2)}, u32[]{:S(2)}) collective-permute-start(bf16[256,512]{1,0:T(8,128)(2,1)S(1)} %get-tuple-element.47.own.after.head), channel_id=1, source_target_pairs={{0,3},{1,2},{2,1},{3,0},{4,7},{5,6},{6,5},{7,4},{8,11},{9,10},{10,... | collective-permute-start | bytes 786440 | tf_op jit(solution)/shard_map/ppermute | solution.py:299
  42.0 0.0 collective-permute-start.11
  42.0 1.4 %collective-permute-start.9 = (bf16[256,512]{1,0:T(8,128)(2,1)S(1)}, bf16[256,512]{1,0:T(8,128)(2,1)S(1)}, u32[]{:S(2)}, u32[]{:S(2)}) collective-permute-start(bf16[256,512]{1,0:T(8,128)(2,1)S(1)} %get-tuple-element.47.own.after.head), channel_id=1, source_target_pairs={{0,2},{1,3},{2,0},{3,1},{4,6},{5,7},{6,4},{7,5},{8,10},{9,11},{10,... | collective-permute-start | bytes 786440 | tf_op jit(solution)/shard_map/ppermute | solution.py:299
  43.4 0.0 collective-permute-done.15.rim
  43.4 0.4 shard_map.128.own.last
  43.8 2.6 %collective-permute-start.17 = (bf16[256,512]{1,0:T(8,128)(2,1)S(1)}, bf16[256,512]{1,0:T(8,128)(2,1)S(1)}, u32[]{:S(2)}, u32[]{:S(2)}) collective-permute-start(bf16[256,512]{1,0:T(8,128)(2,1)S(1)} %shard_map.128.own.last), channel_id=1, source_target_pairs={{0,3},{1,2},{2,1},{3,0},{4,7},{5,6},{6,5},{7,4},{8,11},{9,10},{10,... | collective-permute-start | bytes 786440 | tf_op jit(solution)/shard_map/ppermute | solution.py:299
  46.4 0.0 collective-permute-start.18
  46.4 2.7 %collective-permute-done.10.far = bf16[256,512]{1,0:T(8,128)(2,1)S(1)} collective-permute-done((bf16[256,512]{1,0:T(8,128)(2,1)S(1)}, bf16[256,512]{1,0:T(8,128)(2,1)S(1)}, u32[]{:S(2)}, u32[]{:S(2)}) %collective-permute-start.10) | collective-permute-done | bytes 262176 | tf_op jit(solution)/shard_map/ppermute | solution.py:299
  49.0 1.6 %collective-permute-start.16 = (bf16[256,512]{1,0:T(8,128)(2,1)S(1)}, bf16[256,512]{1,0:T(8,128)(2,1)S(1)}, u32[]{:S(2)}, u32[]{:S(2)}) collective-permute-start(bf16[256,512]{1,0:T(8,128)(2,1)S(1)} %shard_map.128.own.last), channel_id=1, source_target_pairs={{0,2},{1,3},{2,0},{3,1},{4,6},{5,7},{6,4},{7,5},{8,10},{9,11},{10,... | collective-permute-start | bytes 786440 | tf_op jit(solution)/shard_map/ppermute | solution.py:299
  50.6 0.0 collective-permute-done.11.near
  50.6 2.4 %shard_map.126.total = f32[256,2048]{1,0:T(8,128)S(1)} custom-call(s32[4]{0:T(128)S(1)} %pad_add_fusion.where, bf16[256,512]{1,0:T(8,128)(2,1)S(1)} %get-tuple-element.47.own.after.head, bf16[256,512]{1,0:T(8,128)(2,1)S(1)} %collective-permute-done.10.far, bf16[256,512]{1,0:T(8,128)(2,1)S(1)} %collective-permute-done.11.near, ...), custom_call_target="tpu_custom_call" | custom-call | tf_op jit(solution)/shard_map/pallas_call | solution.py:25
  53.0 2.8 %collective-permute-done.9.across = bf16[256,512]{1,0:T(8,128)(2,1)S(1)} collective-permute-done((bf16[256,512]{1,0:T(8,128)(2,1)S(1)}, bf16[256,512]{1,0:T(8,128)(2,1)S(1)}, u32[]{:S(2)}, u32[]{:S(2)}) %collective-permute-start.9) | collective-permute-done | bytes 262176 | tf_op jit(solution)/shard_map/ppermute | solution.py:299
  55.8 1.3 %shard_map.127 = (f32[256,512]{1,0:T(8,128)S(1)}, bf16[256,512]{1,0:T(8,128)(2,1)S(1)}, bf16[256,512]{1,0:T(8,128)(2,1)S(1)}, bf16[256,512]{1,0:T(8,128)(2,1)S(1)}) custom-call(s32[4]{0:T(128)S(1)} %pad_add_fusion.where, bf16[256,512]{1,0:T(8,128)(2,1)S(1)} %collective-permute-done.9.across, bf16[2048,2048]{1,0:T(8,128)(2,1)S(1)} %copy-done.1, ...), custom_call_target="tpu_custom_call" | custom-call | tf_op jit(solution)/shard_map/pallas_call | solution.py:25
  57.1 1.4 %collective-permute-start.12 = (bf16[256,512]{1,0:T(8,128)(2,1)S(1)}, bf16[256,512]{1,0:T(8,128)(2,1)S(1)}, u32[]{:S(2)}, u32[]{:S(2)}) collective-permute-start(bf16[256,512]{1,0:T(8,128)(2,1)S(1)} %get-tuple-element.49), channel_id=1, source_target_pairs={{0,4},{4,0},{8,12},{12,8},{1,5},{5,1},{9,13},{13,9},{2,6},{6,2},{1... | collective-permute-start | bytes 786440 | tf_op jit(solution)/shard_map/ppermute | solution.py:299
  58.5 1.9 %collective-permute-start.13 = (bf16[256,512]{1,0:T(8,128)(2,1)S(1)}, bf16[256,512]{1,0:T(8,128)(2,1)S(1)}, u32[]{:S(2)}, u32[]{:S(2)}) collective-permute-start(bf16[256,512]{1,0:T(8,128)(2,1)S(1)} %get-tuple-element.50), channel_id=1, source_target_pairs={{0,12},{4,8},{8,4},{12,0},{1,13},{5,9},{9,5},{13,1},{2,14},{6,10},... | collective-permute-start | bytes 786440 | tf_op jit(solution)/shard_map/ppermute | solution.py:299
  60.4 0.0 collective-permute-done.17.far
  60.4 2.5 %collective-permute-start.14 = (bf16[256,512]{1,0:T(8,128)(2,1)S(1)}, bf16[256,512]{1,0:T(8,128)(2,1)S(1)}, u32[]{:S(2)}, u32[]{:S(2)}) collective-permute-start(bf16[256,512]{1,0:T(8,128)(2,1)S(1)} %get-tuple-element.51), channel_id=1, source_target_pairs={{0,8},{4,12},{8,0},{12,4},{1,9},{5,13},{9,1},{13,5},{2,10},{6,14},... | collective-permute-start | bytes 786440 | tf_op jit(solution)/shard_map/ppermute | solution.py:299
  62.9 2.4 %shard_map.129.total = f32[256,2048]{1,0:T(8,128)S(1)} custom-call(s32[4]{0:T(128)S(1)} %pad_add_fusion.where, bf16[256,512]{1,0:T(8,128)(2,1)S(1)} %shard_map.128.own.last, bf16[256,512]{1,0:T(8,128)(2,1)S(1)} %collective-permute-done.17.far, bf16[256,512]{1,0:T(8,128)(2,1)S(1)} %collective-permute-done.18.near, bf16[2048,2048]{1,0:T(8,128)(2,1)S(1)} %copy-done.1, ...), custom_call_target="tpu_custom_call" | custom-call | tf_op jit(solution)/shard_map/pallas_call | solution.py:25
  65.3 1.7 %collective-permute-done.16.across = bf16[256,512]{1,0:T(8,128)(2,1)S(1)} collective-permute-done((bf16[256,512]{1,0:T(8,128)(2,1)S(1)}, bf16[256,512]{1,0:T(8,128)(2,1)S(1)}, u32[]{:S(2)}, u32[]{:S(2)}) %collective-permute-start.16) | collective-permute-done | bytes 262176 | tf_op jit(solution)/shard_map/ppermute | solution.py:299
  67.0 1.3 %shard_map.130 = (f32[256,512]{1,0:T(8,128)S(1)}, bf16[256,512]{1,0:T(8,128)(2,1)S(1)}, bf16[256,512]{1,0:T(8,128)(2,1)S(1)}, bf16[256,512]{1,0:T(8,128)(2,1)S(1)}) custom-call(s32[4]{0:T(128)S(1)} %pad_add_fusion.where, bf16[256,512]{1,0:T(8,128)(2,1)S(1)} %collective-permute-done.16.across, bf16[2048,2048]{1,0:T(8,128)(2,1)S(1)} %copy-done.1, ...), custom_call_target="tpu_custom_call" | custom-call | tf_op jit(solution)/shard_map/pallas_call | solution.py:25
  68.3 1.4 %collective-permute-start.19 = (bf16[256,512]{1,0:T(8,128)(2,1)S(1)}, bf16[256,512]{1,0:T(8,128)(2,1)S(1)}, u32[]{:S(2)}, u32[]{:S(2)}) collective-permute-start(bf16[256,512]{1,0:T(8,128)(2,1)S(1)} %get-tuple-element.55), channel_id=1, source_target_pairs={{0,4},{4,0},{8,12},{12,8},{1,5},{5,1},{9,13},{13,9},{2,6},{6,2},{1... | collective-permute-start | bytes 786440 | tf_op jit(solution)/shard_map/ppermute | solution.py:299
  69.7 1.9 %collective-permute-start.20 = (bf16[256,512]{1,0:T(8,128)(2,1)S(1)}, bf16[256,512]{1,0:T(8,128)(2,1)S(1)}, u32[]{:S(2)}, u32[]{:S(2)}) collective-permute-start(bf16[256,512]{1,0:T(8,128)(2,1)S(1)} %get-tuple-element.56), channel_id=1, source_target_pairs={{0,12},{4,8},{8,4},{12,0},{1,13},{5,9},{9,5},{13,1},{2,14},{6,10},... | collective-permute-start | bytes 786440 | tf_op jit(solution)/shard_map/ppermute | solution.py:299
  71.6 0.7 collective-permute-start.21
  72.3 0.1 collective-permute-done.14
  72.4 0.1 add_convert_fusion.1
  72.6 3.3 %collective-permute-done.19.after = bf16[256,512]{1,0:T(8,128)(2,1)S(1)} collective-permute-done((bf16[256,512]{1,0:T(8,128)(2,1)S(1)}, bf16[256,512]{1,0:T(8,128)(2,1)S(1)}, u32[]{:S(2)}, u32[]{:S(2)}) %collective-permute-start.19) | collective-permute-done | bytes 262176 | tf_op jit(solution)/shard_map/ppermute | solution.py:299
  75.8 1.1 %shard_map.131 = (f32[512,256]{1,0:T(8,128)}, bf16[512,512]{1,0:T(8,128)(2,1)}) custom-call(f32[512,256]{1,0:T(8,128)S(1)} %get-tuple-element.34.sums, f32[8,256]{1,0:T(8,128)S(1)} %get-tuple-element.35.decays, bf16[512,256]{1,0:T(8,128)(2,1)S(1)} %get-tuple-element.58.carried, bf16[256,512]{1,0:T(8,128)(2,1)S(1)} %get-tuple-element.47.own.after.head, ...), custom_call_target="tpu_custom_call" | custom-call | tf_op jit(solution)/shard_map/pallas_call | solution.py:25
  76.9 5.0 %collective-permute-done.20 = bf16[256,512]{1,0:T(8,128)(2,1)S(1)} collective-permute-done((bf16[256,512]{1,0:T(8,128)(2,1)S(1)}, bf16[256,512]{1,0:T(8,128)(2,1)S(1)}, u32[]{:S(2)}, u32[]{:S(2)}) %collective-permute-start.20) | collective-permute-done | bytes 262176 | tf_op jit(solution)/shard_map/ppermute | solution.py:299
  81.9 1.9 %collective-permute-done.21 = bf16[256,512]{1,0:T(8,128)(2,1)S(1)} collective-permute-done((bf16[256,512]{1,0:T(8,128)(2,1)S(1)}, bf16[256,512]{1,0:T(8,128)(2,1)S(1)}, u32[]{:S(2)}, u32[]{:S(2)}) %collective-permute-start.21) | collective-permute-done | bytes 262176 | tf_op jit(solution)/shard_map/ppermute | solution.py:299
  83.8 0.1 add_convert_fusion
  84.0 0.8 pad_maximum_fusion
  (17 shorter events, 0.1 us)
Async XLA Ops:
  0.6 1.2 %copy-start = (bf16[512,4,256]{2,1,0:T(4,128)(2,1)S(1)}, bf16[512,4,256]{2,1,0:T(4,128)(2,1)}, u32[]{:S(2)}) copy-start(bf16[512,4,256]{2,1,0:T(4,128)(2,1)} %param.13) | copy-start | bytes 3145732
  0.6 2.0 %copy-start.2 = (bf16[512,512]{1,0:T(8,128)(2,1)S(1)}, bf16[512,512]{1,0:T(8,128)(2,1)}, u32[]{:S(2)}) copy-start(bf16[512,512]{1,0:T(8,128)(2,1)} %grad_hbm.3) | copy-start | bytes 1572868
  1.9 16.7 %copy-start.8 = (f32[8]{0:T(128)S(1)}, f32[8]{0:T(128)}, u32[]{:S(2)}) copy-start(f32[8]{0:T(128)} %skips.1) | copy-start | bytes 100
  2.4 16.2 %copy-start.3 = (bf16[512,512]{1,0:T(8,128)(2,1)S(1)}, bf16[512,512]{1,0:T(8,128)(2,1)}, u32[]{:S(2)}) copy-start(bf16[512,512]{1,0:T(8,128)(2,1)} %conv_hbm.1) | copy-start | bytes 1572868
  2.4 16.2 %copy-start.4 = (f32[8,64,256]{2,1,0:T(8,128)S(1)}, f32[8,64,256]{2,1,0:T(8,128)}, u32[]{:S(2)}) copy-start(f32[8,64,256]{2,1,0:T(8,128)} %param.18) | copy-start | bytes 1572868
  2.4 16.2 %copy-start.6 = (f32[8,512]{1,0:T(8,128)S(1)}, f32[8,512]{1,0:T(8,128)}, u32[]{:S(2)}) copy-start(f32[8,512]{1,0:T(8,128)} %step_hbm.1) | copy-start | bytes 49156
  2.6 0.8 copy-start.7
  3.4 32.5 %copy-start.5 = (f32[4,512]{1,0:T(4,128)S(1)}, f32[4,512]{1,0:T(4,128)}, u32[]{:S(2)}) copy-start(f32[4,512]{1,0:T(4,128)} %taps.3) | copy-start | bytes 24580
  5.3 7.0 %collective-permute-start = (bf16[136,256]{1,0:T(8,128)(2,1)S(1)}, bf16[136,256]{1,0:T(8,128)(2,1)S(1)}, u32[]{:S(2)}, u32[]{:S(2)}) collective-permute-start(bf16[136,256]{1,0:T(8,128)(2,1)S(1)} %get-tuple-element.36), channel_id=1, source_target_pairs={{0,16},{16,0},{32,48},{48,32},{64,80},{80,64},{96,112},{112,96},{1... | collective-permute-start | bytes 208904 | tf_op jit(solution)/shard_map/ppermute | solution.py:299
  8.6 3.7 %collective-permute-start.1 = (bf16[136,256]{1,0:T(8,128)(2,1)S(1)}, bf16[136,256]{1,0:T(8,128)(2,1)S(1)}, u32[]{:S(2)}, u32[]{:S(2)}) collective-permute-start(bf16[136,256]{1,0:T(8,128)(2,1)S(1)} %get-tuple-element.37), channel_id=1, source_target_pairs={{0,32},{16,48},{32,0},{48,16},{64,96},{80,112},{96,64},{112,80},{1... | collective-permute-start | bytes 208904 | tf_op jit(solution)/shard_map/ppermute | solution.py:299
  8.6 5.4 %collective-permute-start.2 = (bf16[136,256]{1,0:T(8,128)(2,1)S(1)}, bf16[136,256]{1,0:T(8,128)(2,1)S(1)}, u32[]{:S(2)}, u32[]{:S(2)}) collective-permute-start(bf16[136,256]{1,0:T(8,128)(2,1)S(1)} %get-tuple-element.38), channel_id=1, source_target_pairs={{0,48},{16,32},{32,16},{48,0},{64,112},{80,96},{96,80},{112,64},{1... | collective-permute-start | bytes 208904 | tf_op jit(solution)/shard_map/ppermute | solution.py:299
  10.3 40.3 %copy-start.1 = (bf16[2048,2048]{1,0:T(8,128)(2,1)S(1)}, bf16[2048,2048]{1,0:T(8,128)(2,1)}, u32[]{:S(2)}) copy-start(bf16[2048,2048]{1,0:T(8,128)(2,1)} %weight.7) | copy-start | bytes 25165828
  14.7 7.8 %collective-permute-start.3 = (bf16[136,256]{1,0:T(8,128)(2,1)S(1)}, bf16[136,256]{1,0:T(8,128)(2,1)S(1)}, u32[]{:S(2)}, u32[]{:S(2)}) collective-permute-start(bf16[136,256]{1,0:T(8,128)(2,1)S(1)} %shard_map.122.after), channel_id=1, source_target_pairs={{192,0},{208,16},{224,32},{240,48},{193,1},{209,17},{225,33},{241,... | collective-permute-start | bytes 208904 | tf_op jit(solution)/shard_map/ppermute | solution.py:294
  16.0 8.4 %collective-permute-start.4 = (bf16[136,256]{1,0:T(8,128)(2,1)S(1)}, bf16[136,256]{1,0:T(8,128)(2,1)S(1)}, u32[]{:S(2)}, u32[]{:S(2)}) collective-permute-start(bf16[136,256]{1,0:T(8,128)(2,1)S(1)} %shard_map.122.after), channel_id=1, source_target_pairs={{64,0},{80,16},{96,32},{112,48},{128,64},{144,80},{160,96},{176,11... | collective-permute-start | bytes 208904 | tf_op jit(solution)/shard_map/ppermute | solution.py:294
  17.3 9.4 %collective-permute-start.5 = (bf16[136,256]{1,0:T(8,128)(2,1)S(1)}, bf16[136,256]{1,0:T(8,128)(2,1)S(1)}, u32[]{:S(2)}, u32[]{:S(2)}) collective-permute-start(bf16[136,256]{1,0:T(8,128)(2,1)S(1)} %shard_map.122.after), channel_id=1, source_target_pairs={{128,0},{144,16},{160,32},{176,48},{192,64},{208,80},{224,96},{240... | collective-permute-start | bytes 208904 | tf_op jit(solution)/shard_map/ppermute | solution.py:294
  27.3 4.6 %collective-permute-start.6 = (bf16[8,16,256]{2,1,0:T(8,128)(2,1)S(1)}, bf16[8,16,256]{2,1,0:T(8,128)(2,1)S(1)}, u32[]{:S(2)}, u32[]{:S(2)}) collective-permute-start(bf16[8,16,256]{2,1,0:T(8,128)(2,1)S(1)} %get-tuple-element.42), channel_id=1, source_target_pairs={{0,16},{16,0},{32,48},{48,32},{64,80},{80,64},{96,112},{112,96},{1... | collective-permute-start | bytes 196616 | tf_op jit(solution)/shard_map/ppermute | solution.py:299
  28.5 5.7 %collective-permute-start.7 = (bf16[8,16,256]{2,1,0:T(8,128)(2,1)S(1)}, bf16[8,16,256]{2,1,0:T(8,128)(2,1)S(1)}, u32[]{:S(2)}, u32[]{:S(2)}) collective-permute-start(bf16[8,16,256]{2,1,0:T(8,128)(2,1)S(1)} %get-tuple-element.43), channel_id=1, source_target_pairs={{0,32},{16,48},{32,0},{48,16},{64,96},{80,112},{96,64},{112,80},{1... | collective-permute-start | bytes 196616 | tf_op jit(solution)/shard_map/ppermute | solution.py:299
  31.9 4.1 %collective-permute-start.8 = (bf16[8,16,256]{2,1,0:T(8,128)(2,1)S(1)}, bf16[8,16,256]{2,1,0:T(8,128)(2,1)S(1)}, u32[]{:S(2)}, u32[]{:S(2)}) collective-permute-start(bf16[8,16,256]{2,1,0:T(8,128)(2,1)S(1)} %get-tuple-element.44), channel_id=1, source_target_pairs={{0,48},{16,32},{32,16},{48,0},{64,112},{80,96},{96,80},{112,64},{1... | collective-permute-start | bytes 196616 | tf_op jit(solution)/shard_map/ppermute | solution.py:299
  37.1 6.2 %collective-permute-start.15 = (bf16[16,512]{1,0:T(8,128)(2,1)S(1)}, bf16[16,512]{1,0:T(8,128)(2,1)S(1)}, u32[]{:S(2)}, u32[]{:S(2)}) collective-permute-start(bf16[16,512]{1,0:T(8,128)(2,1)S(1)} %get-tuple-element.53), channel_id=1, source_target_pairs={{16,0},{32,16},{48,32},{64,48},{80,64},{96,80},{112,96},{128,112},... | collective-permute-start | bytes 49160 | tf_op jit(solution)/shard_map/ppermute | solution.py:294
  39.4 9.6 %collective-permute-start.10 = (bf16[256,512]{1,0:T(8,128)(2,1)S(1)}, bf16[256,512]{1,0:T(8,128)(2,1)S(1)}, u32[]{:S(2)}, u32[]{:S(2)}) collective-permute-start(bf16[256,512]{1,0:T(8,128)(2,1)S(1)} %get-tuple-element.47.own.after.head), channel_id=1, source_target_pairs={{0,3},{1,2},{2,1},{3,0},{4,7},{5,6},{6,5},{7,4},{8,11},{9,10},{10,... | collective-permute-start | bytes 786440 | tf_op jit(solution)/shard_map/ppermute | solution.py:299
  42.0 8.6 %collective-permute-start.11 = (bf16[256,512]{1,0:T(8,128)(2,1)S(1)}, bf16[256,512]{1,0:T(8,128)(2,1)S(1)}, u32[]{:S(2)}, u32[]{:S(2)}) collective-permute-start(bf16[256,512]{1,0:T(8,128)(2,1)S(1)} %get-tuple-element.47.own.after.head), channel_id=1, source_target_pairs={{0,1},{1,0},{2,3},{3,2},{4,5},{5,4},{6,7},{7,6},{8,9},{9,8},{10,11... | collective-permute-start | bytes 786440 | tf_op jit(solution)/shard_map/ppermute | solution.py:299
  42.0 13.8 %collective-permute-start.9 = (bf16[256,512]{1,0:T(8,128)(2,1)S(1)}, bf16[256,512]{1,0:T(8,128)(2,1)S(1)}, u32[]{:S(2)}, u32[]{:S(2)}) collective-permute-start(bf16[256,512]{1,0:T(8,128)(2,1)S(1)} %get-tuple-element.47.own.after.head), channel_id=1, source_target_pairs={{0,2},{1,3},{2,0},{3,1},{4,6},{5,7},{6,4},{7,5},{8,10},{9,11},{10,... | collective-permute-start | bytes 786440 | tf_op jit(solution)/shard_map/ppermute | solution.py:299
  43.8 16.6 %collective-permute-start.17 = (bf16[256,512]{1,0:T(8,128)(2,1)S(1)}, bf16[256,512]{1,0:T(8,128)(2,1)S(1)}, u32[]{:S(2)}, u32[]{:S(2)}) collective-permute-start(bf16[256,512]{1,0:T(8,128)(2,1)S(1)} %shard_map.128.own.last), channel_id=1, source_target_pairs={{0,3},{1,2},{2,1},{3,0},{4,7},{5,6},{6,5},{7,4},{8,11},{9,10},{10,... | collective-permute-start | bytes 786440 | tf_op jit(solution)/shard_map/ppermute | solution.py:299
  46.4 16.5 %collective-permute-start.18 = (bf16[256,512]{1,0:T(8,128)(2,1)S(1)}, bf16[256,512]{1,0:T(8,128)(2,1)S(1)}, u32[]{:S(2)}, u32[]{:S(2)}) collective-permute-start(bf16[256,512]{1,0:T(8,128)(2,1)S(1)} %shard_map.128.own.last), channel_id=1, source_target_pairs={{0,1},{1,0},{2,3},{3,2},{4,5},{5,4},{6,7},{7,6},{8,9},{9,8},{10,11... | collective-permute-start | bytes 786440 | tf_op jit(solution)/shard_map/ppermute | solution.py:299
  49.0 18.0 %collective-permute-start.16 = (bf16[256,512]{1,0:T(8,128)(2,1)S(1)}, bf16[256,512]{1,0:T(8,128)(2,1)S(1)}, u32[]{:S(2)}, u32[]{:S(2)}) collective-permute-start(bf16[256,512]{1,0:T(8,128)(2,1)S(1)} %shard_map.128.own.last), channel_id=1, source_target_pairs={{0,2},{1,3},{2,0},{3,1},{4,6},{5,7},{6,4},{7,5},{8,10},{9,11},{10,... | collective-permute-start | bytes 786440 | tf_op jit(solution)/shard_map/ppermute | solution.py:299
  57.1 14.5 %collective-permute-start.12 = (bf16[256,512]{1,0:T(8,128)(2,1)S(1)}, bf16[256,512]{1,0:T(8,128)(2,1)S(1)}, u32[]{:S(2)}, u32[]{:S(2)}) collective-permute-start(bf16[256,512]{1,0:T(8,128)(2,1)S(1)} %get-tuple-element.49), channel_id=1, source_target_pairs={{0,4},{4,0},{8,12},{12,8},{1,5},{5,1},{9,13},{13,9},{2,6},{6,2},{1... | collective-permute-start | bytes 786440 | tf_op jit(solution)/shard_map/ppermute | solution.py:299
  58.5 13.9 %collective-permute-start.13 = (bf16[256,512]{1,0:T(8,128)(2,1)S(1)}, bf16[256,512]{1,0:T(8,128)(2,1)S(1)}, u32[]{:S(2)}, u32[]{:S(2)}) collective-permute-start(bf16[256,512]{1,0:T(8,128)(2,1)S(1)} %get-tuple-element.50), channel_id=1, source_target_pairs={{0,12},{4,8},{8,4},{12,0},{1,13},{5,9},{9,5},{13,1},{2,14},{6,10},... | collective-permute-start | bytes 786440 | tf_op jit(solution)/shard_map/ppermute | solution.py:299
  60.4 12.1 %collective-permute-start.14 = (bf16[256,512]{1,0:T(8,128)(2,1)S(1)}, bf16[256,512]{1,0:T(8,128)(2,1)S(1)}, u32[]{:S(2)}, u32[]{:S(2)}) collective-permute-start(bf16[256,512]{1,0:T(8,128)(2,1)S(1)} %get-tuple-element.51), channel_id=1, source_target_pairs={{0,8},{4,12},{8,0},{12,4},{1,9},{5,13},{9,1},{13,5},{2,10},{6,14},... | collective-permute-start | bytes 786440 | tf_op jit(solution)/shard_map/ppermute | solution.py:299
  68.3 7.5 %collective-permute-start.19 = (bf16[256,512]{1,0:T(8,128)(2,1)S(1)}, bf16[256,512]{1,0:T(8,128)(2,1)S(1)}, u32[]{:S(2)}, u32[]{:S(2)}) collective-permute-start(bf16[256,512]{1,0:T(8,128)(2,1)S(1)} %get-tuple-element.55), channel_id=1, source_target_pairs={{0,4},{4,0},{8,12},{12,8},{1,5},{5,1},{9,13},{13,9},{2,6},{6,2},{1... | collective-permute-start | bytes 786440 | tf_op jit(solution)/shard_map/ppermute | solution.py:299
  69.7 12.2 %collective-permute-start.20 = (bf16[256,512]{1,0:T(8,128)(2,1)S(1)}, bf16[256,512]{1,0:T(8,128)(2,1)S(1)}, u32[]{:S(2)}, u32[]{:S(2)}) collective-permute-start(bf16[256,512]{1,0:T(8,128)(2,1)S(1)} %get-tuple-element.56), channel_id=1, source_target_pairs={{0,12},{4,8},{8,4},{12,0},{1,13},{5,9},{9,5},{13,1},{2,14},{6,10},... | collective-permute-start | bytes 786440 | tf_op jit(solution)/shard_map/ppermute | solution.py:299
  71.6 12.2 %collective-permute-start.21 = (bf16[256,512]{1,0:T(8,128)(2,1)S(1)}, bf16[256,512]{1,0:T(8,128)(2,1)S(1)}, u32[]{:S(2)}, u32[]{:S(2)}) collective-permute-start(bf16[256,512]{1,0:T(8,128)(2,1)S(1)} %get-tuple-element.57), channel_id=1, source_target_pairs={{0,8},{4,12},{8,0},{12,4},{1,9},{5,13},{9,1},{13,5},{2,10},{6,14},... | collective-permute-start | bytes 786440 | tf_op jit(solution)/shard_map/ppermute | solution.py:299

commit v4 on v3

--- a/solution.py
+++ b/solution.py
@@ -1,3 +1,5 @@
+import functools
+
 import jax
 import jax.numpy as jnp
 from jax import lax
@@ -192,7 +194,7 @@
 
 
 def carry_kernel(
-    where, sums, decays, one, two, three, far, near, middle, later, own, first, second, third,
+    where, sums, decays, one, two, three, middle, near, far, later, own, first, second, third,
     values, scales, carries,
 ):
     heads = decays.shape[0]
@@ -276,11 +278,11 @@
         total[:, spot] = sums
 
 
-def finish_kernel(where, across, weight, total, kept, near, far, over):
+def finish_kernel(flips, where, across, weight, total, *outs):
     row, column = where[2], where[3]
     width = across.shape[1]
     at = pl.ds(pl.multiple_of(jnp.bitwise_xor(column, 2) * width, width), width)
-    for flip, out in ((2, over), (1, near), (3, far), (0, kept)):
+    for flip, out in zip(flips, outs):
         target = jnp.bitwise_xor(row, flip)
         spot = pl.ds(pl.multiple_of(target * width, width), width)
         term = lax.dot_general(
@@ -357,7 +359,7 @@
     own, *out = call(
         carry_kernel,
         (piece,) * 4,
-        (where, sums, decays, *near, far, close, middle, quarter),
+        (where, sums, decays, *near, middle, close, far, quarter),
         specs=(SMEM,),
         scratch=quads + (pltpu.VMEM((QUAD, heads, part, states), BF16),),
     )
@@ -386,9 +388,15 @@
             (where, chunk, far, near, proj_weight, after),
             specs=(SMEM,),
         )
-        kept, near, far, over = call(
-            finish_kernel,
-            (held, block, block, block),
+        near, far = call(
+            functools.partial(finish_kernel, (1, 3)),
+            (block, block),
+            (where, across, proj_weight, partial),
+            specs=(SMEM,),
+        )
+        over, kept = call(
+            functools.partial(finish_kernel, (2, 0)),
+            (block, held),
             (where, across, proj_weight, partial),
             specs=(SMEM,),
         )

time: 85 us -> 83.6 us (0.984)
  starting transfers between devices: 33.7 us -> 29.9 us
  Pallas kernels: 16.7 us -> 18 us
  waiting for transfers between devices: 27.8 us -> 28.7 us
    ppermute x18, starting transfers between devices: 27.5 us -> 23.7 us  [swapped(): lax.ppermute(value, axis, [(place, place ^ flip) for place in range(count)])]
    pallas_call x11 -> x13, Pallas kernels: 16.7 us -> 18 us  [call(): pl.pallas_call(kernel, out_shape=outs, in_specs=list(specs) + [VMEM] * (l...]
  transfers between devices with their start and end apart: 22 -> 22, of which waited for: 13 -> 12; matrix products, arithmetic and copies ran while one was open for 2% -> 3% of each run, Pallas kernels for 14% -> 16%
where the time goes in v4:
time: 83.6 us; the launch traced here: 83.4 us
  starting transfers between devices  29.9 us (36%)
  waiting for transfers between devices  28.7 us (34%)
  Pallas kernels  18 us (22%)
  local copies, waits for them, and re-layouts  4.57 us (5%)
  other arithmetic  1.18 us (1%)
  between operations  0.95 us (1%)
    ppermute x18, starting transfers between devices, swapped(): lax.ppermute(value, axis, [(place, place ^ flip) for place in range(count)])  23.7 us
    ppermute x18, waiting for transfers between devices, swapped(): lax.ppermute(value, axis, [(place, place ^ flip) for place in range(count)])  23.6 us
    pallas_call x13, Pallas kernels, call(): pl.pallas_call(kernel, out_shape=outs, in_specs=list(specs) + [VMEM] * (l...  18 us
    ppermute x4, starting transfers between devices, earlier(): lax.ppermute(value, 'ctx', [(place, place - steps) for place in range(ste...  6.15 us
    ppermute x4, waiting for transfers between devices, earlier(): lax.ppermute(value, 'ctx', [(place, place - steps) for place in range(ste...  5.1 us
    unnamed x20, local copies, waits for them, and re-layouts  2.11 us
    dynamic_slice x1, local copies, waits for them, and re-layouts, on_device(): writes = lax.dynamic_index_in_dim(input_mix, group, 1, keepdims=False)  1.92 us
  transfers between devices with their start and end apart: 22, of which 12 were waited for; matrix products, arithmetic and copies ran while one was open for 3% of the time, Pallas kernels for 16%

profile of v4, /device:TPU:1, one launch (start us, length us, event | category | flops | bytes accessed | tf_op | source)
XLA Modules:
  0.0 83.4 jit_solution(14107812135226676290)
XLA Ops:
  0.6 0.0 copy-start
  0.7 1.2 %copy-done = bf16[512,4,256]{2,1,0:T(4,128)(2,1)S(1)} copy-done((bf16[512,4,256]{2,1,0:T(4,128)(2,1)S(1)}, bf16[512,4,256]{2,1,0:T(4,128)(2,1)}, u32[]{:S(2)}) %copy-start) | copy-done | bytes 1048600
  1.9 0.5 constant_dynamic-slice_fusion.1
  2.4 0.0 copy-start.3
  2.4 0.0 copy-start.4
  2.4 0.0 copy-start.6
  2.5 0.1 pad_add_fusion.where
  2.6 0.8 copy-done.7
  3.4 1.9 %shard_map.121 = (f32[512,256]{1,0:T(8,128)S(1)}, f32[8,512]{1,0:T(8,128)S(1)}, f32[8,256]{1,0:T(8,128)S(1)}, bf16[136,256]{1,0:T(8,128)(2,1)S(1)}, bf16[136,256...) custom-call(s32[4]{0:T(128)S(1)} %pad_add_fusion.where, bf16[512,512]{1,0:T(8,128)(2,1)S(1)} %copy-done.2, ...), custom_call_target="tpu_custom_call" | custom-call | tf_op jit(solution)/shard_map/pallas_call | solution.py:27
  5.3 3.3 %collective-permute-start = (bf16[136,256]{1,0:T(8,128)(2,1)S(1)}, bf16[136,256]{1,0:T(8,128)(2,1)S(1)}, u32[]{:S(2)}, u32[]{:S(2)}) collective-permute-start(bf16[136,256]{1,0:T(8,128)(2,1)S(1)} %get-tuple-element.36), channel_id=1, source_target_pairs={{0,16},{16,0},{32,48},{48,32},{64,80},{80,64},{96,112},{112,96},{1... | collective-permute-start | bytes 208904 | tf_op jit(solution)/shard_map/ppermute | solution.py:301
  8.6 0.0 collective-permute-start.1
  8.6 1.7 %collective-permute-start.2 = (bf16[136,256]{1,0:T(8,128)(2,1)S(1)}, bf16[136,256]{1,0:T(8,128)(2,1)S(1)}, u32[]{:S(2)}, u32[]{:S(2)}) collective-permute-start(bf16[136,256]{1,0:T(8,128)(2,1)S(1)} %get-tuple-element.38), channel_id=1, source_target_pairs={{0,48},{16,32},{32,16},{48,0},{64,112},{80,96},{96,80},{112,64},{1... | collective-permute-start | bytes 208904 | tf_op jit(solution)/shard_map/ppermute | solution.py:301
  10.3 1.9 %constant_dynamic-slice_fusion = bf16[512,1,256]{2,1,0:T(2,128)(2,1)S(1)} fusion(bf16[512,4,256]{2,1,0:T(4,128)(2,1)} %param.12, s32[]{:T(128)S(6)} %select_n.22), kind=kLoop, calls=%fused_computation.6 | loop fusion | bytes 524292 | tf_op jit(solution)/shard_map/jit(dynamic_index_in_dim)/dynamic_slice | solution.py:316
  12.3 0.0 collective-permute-done.one
  12.3 0.0 collective-permute-done.1.two
  12.4 1.7 %collective-permute-done.2.three = bf16[136,256]{1,0:T(8,128)(2,1)S(1)} collective-permute-done((bf16[136,256]{1,0:T(8,128)(2,1)S(1)}, bf16[136,256]{1,0:T(8,128)(2,1)S(1)}, u32[]{:S(2)}, u32[]{:S(2)}) %collective-permute-start.2) | collective-permute-done | bytes 69664 | tf_op jit(solution)/shard_map/ppermute | solution.py:301
  14.0 0.6 shard_map.122.after
  14.7 1.3 %collective-permute-start.3 = (bf16[136,256]{1,0:T(8,128)(2,1)S(1)}, bf16[136,256]{1,0:T(8,128)(2,1)S(1)}, u32[]{:S(2)}, u32[]{:S(2)}) collective-permute-start(bf16[136,256]{1,0:T(8,128)(2,1)S(1)} %shard_map.122.after), channel_id=1, source_target_pairs={{128,0},{144,16},{160,32},{176,48},{192,64},{208,80},{224,96},{240... | collective-permute-start | bytes 208904 | tf_op jit(solution)/shard_map/ppermute | solution.py:296
  16.0 1.3 %collective-permute-start.4 = (bf16[136,256]{1,0:T(8,128)(2,1)S(1)}, bf16[136,256]{1,0:T(8,128)(2,1)S(1)}, u32[]{:S(2)}, u32[]{:S(2)}) collective-permute-start(bf16[136,256]{1,0:T(8,128)(2,1)S(1)} %shard_map.122.after), channel_id=1, source_target_pairs={{64,0},{80,16},{96,32},{112,48},{128,64},{144,80},{160,96},{176,11... | collective-permute-start | bytes 208904 | tf_op jit(solution)/shard_map/ppermute | solution.py:296
  17.3 1.3 %collective-permute-start.5 = (bf16[136,256]{1,0:T(8,128)(2,1)S(1)}, bf16[136,256]{1,0:T(8,128)(2,1)S(1)}, u32[]{:S(2)}, u32[]{:S(2)}) collective-permute-start(bf16[136,256]{1,0:T(8,128)(2,1)S(1)} %shard_map.122.after), channel_id=1, source_target_pairs={{192,0},{208,16},{224,32},{240,48},{193,1},{209,17},{225,33},{241,... | collective-permute-start | bytes 208904 | tf_op jit(solution)/shard_map/ppermute | solution.py:296
  18.6 3.4 %shard_map.123 = (f32[512,512]{1,0:T(8,128)S(1)}, f32[512,512]{1,0:T(8,128)S(1)}, f32[8,16,256]{2,1,0:T(8,128)S(1)}) custom-call(s32[4]{0:T(128)S(1)} %pad_add_fusion.where, f32[8]{0:T(128)S(1)} %copy-done.8, bf16[512,512]{1,0:T(8,128)(2,1)S(1)} %copy-done.2, bf16[512,512]{1,0:T(8,128)(2,1)S(1)} %copy-done.3, f32[8,512]{1,0:T(8,128)S(1)} %copy-done.6, ...), custom_call_target="tpu_custom_call" | custom-call | tf_op jit(solution)/shard_map/pallas_call | solution.py:27
  22.0 2.0 %collective-permute-done.3.middle = bf16[136,256]{1,0:T(8,128)(2,1)S(1)} collective-permute-done((bf16[136,256]{1,0:T(8,128)(2,1)S(1)}, bf16[136,256]{1,0:T(8,128)(2,1)S(1)}, u32[]{:S(2)}, u32[]{:S(2)}) %collective-permute-start.3) | collective-permute-done | bytes 69664 | tf_op jit(solution)/shard_map/ppermute | solution.py:296
  24.0 1.6 %collective-permute-done.4.near = bf16[136,256]{1,0:T(8,128)(2,1)S(1)} collective-permute-done((bf16[136,256]{1,0:T(8,128)(2,1)S(1)}, bf16[136,256]{1,0:T(8,128)(2,1)S(1)}, u32[]{:S(2)}, u32[]{:S(2)}) %collective-permute-start.4) | collective-permute-done | bytes 69664 | tf_op jit(solution)/shard_map/ppermute | solution.py:296
  25.6 1.5 %collective-permute-done.5.far = bf16[136,256]{1,0:T(8,128)(2,1)S(1)} collective-permute-done((bf16[136,256]{1,0:T(8,128)(2,1)S(1)}, bf16[136,256]{1,0:T(8,128)(2,1)S(1)}, u32[]{:S(2)}, u32[]{:S(2)}) %collective-permute-start.5) | collective-permute-done | bytes 69664 | tf_op jit(solution)/shard_map/ppermute | solution.py:296
  27.1 0.7 shard_map.124
  27.8 1.7 %collective-permute-start.6 = (bf16[8,16,256]{2,1,0:T(8,128)(2,1)S(1)}, bf16[8,16,256]{2,1,0:T(8,128)(2,1)S(1)}, u32[]{:S(2)}, u32[]{:S(2)}) collective-permute-start(bf16[8,16,256]{2,1,0:T(8,128)(2,1)S(1)} %get-tuple-element.42), channel_id=1, source_target_pairs={{0,16},{16,0},{32,48},{48,32},{64,80},{80,64},{96,112},{112,96},{1... | collective-permute-start | bytes 196616 | tf_op jit(solution)/shard_map/ppermute | solution.py:301
  29.5 1.7 %collective-permute-start.7 = (bf16[8,16,256]{2,1,0:T(8,128)(2,1)S(1)}, bf16[8,16,256]{2,1,0:T(8,128)(2,1)S(1)}, u32[]{:S(2)}, u32[]{:S(2)}) collective-permute-start(bf16[8,16,256]{2,1,0:T(8,128)(2,1)S(1)} %get-tuple-element.43), channel_id=1, source_target_pairs={{0,32},{16,48},{32,0},{48,16},{64,96},{80,112},{96,64},{112,80},{1... | collective-permute-start | bytes 196616 | tf_op jit(solution)/shard_map/ppermute | solution.py:301
  31.3 0.1 collective-permute-start.8
  31.4 0.0 collective-permute-done.6.first
  31.4 2.3 %collective-permute-done.7.second = bf16[8,16,256]{2,1,0:T(8,128)(2,1)S(1)} collective-permute-done((bf16[8,16,256]{2,1,0:T(8,128)(2,1)S(1)}, bf16[8,16,256]{2,1,0:T(8,128)(2,1)S(1)}, u32[]{:S(2)}, u32[]{:S(2)}) %collective-permute-start.7) | collective-permute-done | bytes 65568 | tf_op jit(solution)/shard_map/ppermute | solution.py:301
  33.6 1.7 %collective-permute-done.8.third = bf16[8,16,256]{2,1,0:T(8,128)(2,1)S(1)} collective-permute-done((bf16[8,16,256]{2,1,0:T(8,128)(2,1)S(1)}, bf16[8,16,256]{2,1,0:T(8,128)(2,1)S(1)}, u32[]{:S(2)}, u32[]{:S(2)}) %collective-permute-start.8) | collective-permute-done | bytes 65568 | tf_op jit(solution)/shard_map/ppermute | solution.py:301
  35.4 1.2 %shard_map.125 = (bf16[256,512]{1,0:T(8,128)(2,1)S(1)}, bf16[16,512]{1,0:T(8,128)(2,1)S(1)}, bf16[256,512]{1,0:T(8,128)(2,1)S(1)}, bf16[512,256]{1,0:T(8,128)(2,1)S(1)}) custom-call(s32[4]{0:T(128)S(1)} %pad_add_fusion.where, bf16[8,16,256]{2,1,0:T(8,128)(2,1)S(1)} %get-tuple-element.41.own, bf16[8,16,256]{2,1,0:T(8,128)(2,1)S(1)} %collective-permute-done.6.first, ...), custom_call_target="tpu_custom_call" | custom-call | tf_op jit(solution)/shard_map/pallas_call | solution.py:27
  36.5 2.3 %collective-permute-start.15 = (bf16[16,512]{1,0:T(8,128)(2,1)S(1)}, bf16[16,512]{1,0:T(8,128)(2,1)S(1)}, u32[]{:S(2)}, u32[]{:S(2)}) collective-permute-start(bf16[16,512]{1,0:T(8,128)(2,1)S(1)} %get-tuple-element.53), channel_id=1, source_target_pairs={{16,0},{32,16},{48,32},{64,48},{80,64},{96,80},{112,96},{128,112},... | collective-permute-start | bytes 49160 | tf_op jit(solution)/shard_map/ppermute | solution.py:296
  38.8 2.1 %collective-permute-start.10 = (bf16[256,512]{1,0:T(8,128)(2,1)S(1)}, bf16[256,512]{1,0:T(8,128)(2,1)S(1)}, u32[]{:S(2)}, u32[]{:S(2)}) collective-permute-start(bf16[256,512]{1,0:T(8,128)(2,1)S(1)} %get-tuple-element.47.own.after.head), channel_id=1, source_target_pairs={{0,3},{1,2},{2,1},{3,0},{4,7},{5,6},{6,5},{7,4},{8,11},{9,10},{10,... | collective-permute-start | bytes 786440 | tf_op jit(solution)/shard_map/ppermute | solution.py:301
  40.9 0.0 collective-permute-start.11
  40.9 1.9 %collective-permute-start.9 = (bf16[256,512]{1,0:T(8,128)(2,1)S(1)}, bf16[256,512]{1,0:T(8,128)(2,1)S(1)}, u32[]{:S(2)}, u32[]{:S(2)}) collective-permute-start(bf16[256,512]{1,0:T(8,128)(2,1)S(1)} %get-tuple-element.47.own.after.head), channel_id=1, source_target_pairs={{0,2},{1,3},{2,0},{3,1},{4,6},{5,7},{6,4},{7,5},{8,10},{9,11},{10,... | collective-permute-start | bytes 786440 | tf_op jit(solution)/shard_map/ppermute | solution.py:301
  42.8 0.0 collective-permute-done.15.rim
  42.8 0.4 shard_map.129.own.last
  43.2 2.1 %collective-permute-start.17 = (bf16[256,512]{1,0:T(8,128)(2,1)S(1)}, bf16[256,512]{1,0:T(8,128)(2,1)S(1)}, u32[]{:S(2)}, u32[]{:S(2)}) collective-permute-start(bf16[256,512]{1,0:T(8,128)(2,1)S(1)} %shard_map.129.own.last), channel_id=1, source_target_pairs={{0,3},{1,2},{2,1},{3,0},{4,7},{5,6},{6,5},{7,4},{8,11},{9,10},{10,... | collective-permute-start | bytes 786440 | tf_op jit(solution)/shard_map/ppermute | solution.py:301
  45.2 0.0 collective-permute-start.18
  45.2 3.2 %collective-permute-done.10.far = bf16[256,512]{1,0:T(8,128)(2,1)S(1)} collective-permute-done((bf16[256,512]{1,0:T(8,128)(2,1)S(1)}, bf16[256,512]{1,0:T(8,128)(2,1)S(1)}, u32[]{:S(2)}, u32[]{:S(2)}) %collective-permute-start.10) | collective-permute-done | bytes 262176 | tf_op jit(solution)/shard_map/ppermute | solution.py:301
  48.4 1.0 %collective-permute-start.16 = (bf16[256,512]{1,0:T(8,128)(2,1)S(1)}, bf16[256,512]{1,0:T(8,128)(2,1)S(1)}, u32[]{:S(2)}, u32[]{:S(2)}) collective-permute-start(bf16[256,512]{1,0:T(8,128)(2,1)S(1)} %shard_map.129.own.last), channel_id=1, source_target_pairs={{0,2},{1,3},{2,0},{3,1},{4,6},{5,7},{6,4},{7,5},{8,10},{9,11},{10,... | collective-permute-start | bytes 786440 | tf_op jit(solution)/shard_map/ppermute | solution.py:301
  49.5 2.4 %shard_map.126.total = f32[256,2048]{1,0:T(8,128)S(1)} custom-call(s32[4]{0:T(128)S(1)} %pad_add_fusion.where, bf16[256,512]{1,0:T(8,128)(2,1)S(1)} %get-tuple-element.47.own.after.head, bf16[256,512]{1,0:T(8,128)(2,1)S(1)} %collective-permute-done.10.far, bf16[256,512]{1,0:T(8,128)(2,1)S(1)} %collective-permute-done.11.near, ...), custom_call_target="tpu_custom_call" | custom-call | tf_op jit(solution)/shard_map/pallas_call | solution.py:27
  51.8 3.3 %collective-permute-done.9.across = bf16[256,512]{1,0:T(8,128)(2,1)S(1)} collective-permute-done((bf16[256,512]{1,0:T(8,128)(2,1)S(1)}, bf16[256,512]{1,0:T(8,128)(2,1)S(1)}, u32[]{:S(2)}, u32[]{:S(2)}) %collective-permute-start.9) | collective-permute-done | bytes 262176 | tf_op jit(solution)/shard_map/ppermute | solution.py:301
  55.1 1.0 %shard_map.128 = (bf16[256,512]{1,0:T(8,128)(2,1)S(1)}, bf16[256,512]{1,0:T(8,128)(2,1)S(1)}) custom-call(s32[4]{0:T(128)S(1)} %pad_add_fusion.where, bf16[256,512]{1,0:T(8,128)(2,1)S(1)} %collective-permute-done.9.across, bf16[2048,2048]{1,0:T(8,128)(2,1)S(1)} %copy-done.1, f32[256,2048]{1,0:T(8,128)S(1)} %shard_map.126.total), custom_call_target="tpu_custom_call" | custom-call | tf_op jit(solution)/shard_map/pallas_call | solution.py:27
  56.2 0.9 %collective-permute-start.12 = (bf16[256,512]{1,0:T(8,128)(2,1)S(1)}, bf16[256,512]{1,0:T(8,128)(2,1)S(1)}, u32[]{:S(2)}, u32[]{:S(2)}) collective-permute-start(bf16[256,512]{1,0:T(8,128)(2,1)S(1)} %get-tuple-element.49), channel_id=1, source_target_pairs={{0,4},{4,0},{8,12},{12,8},{1,5},{5,1},{9,13},{13,9},{2,6},{6,2},{1... | collective-permute-start | bytes 786440 | tf_op jit(solution)/shard_map/ppermute | solution.py:301
  57.0 1.9 %collective-permute-start.13 = (bf16[256,512]{1,0:T(8,128)(2,1)S(1)}, bf16[256,512]{1,0:T(8,128)(2,1)S(1)}, u32[]{:S(2)}, u32[]{:S(2)}) collective-permute-start(bf16[256,512]{1,0:T(8,128)(2,1)S(1)} %get-tuple-element.50), channel_id=1, source_target_pairs={{0,12},{4,8},{8,4},{12,0},{1,13},{5,9},{9,5},{13,1},{2,14},{6,10},... | collective-permute-start | bytes 786440 | tf_op jit(solution)/shard_map/ppermute | solution.py:301
  58.9 1.0 %shard_map.127 = (bf16[256,512]{1,0:T(8,128)(2,1)S(1)}, f32[256,512]{1,0:T(8,128)S(1)}) custom-call(s32[4]{0:T(128)S(1)} %pad_add_fusion.where, bf16[256,512]{1,0:T(8,128)(2,1)S(1)} %collective-permute-done.9.across, bf16[2048,2048]{1,0:T(8,128)(2,1)S(1)} %copy-done.1, f32[256,2048]{1,0:T(8,128)S(1)} %shard_map.126.total), custom_call_target="tpu_custom_call" | custom-call | tf_op jit(solution)/shard_map/pallas_call | solution.py:27
  60.0 0.0 collective-permute-done.17.far
  60.0 1.8 %collective-permute-start.14 = (bf16[256,512]{1,0:T(8,128)(2,1)S(1)}, bf16[256,512]{1,0:T(8,128)(2,1)S(1)}, u32[]{:S(2)}, u32[]{:S(2)}) collective-permute-start(bf16[256,512]{1,0:T(8,128)(2,1)S(1)} %get-tuple-element.51), channel_id=1, source_target_pairs={{0,8},{4,12},{8,0},{12,4},{1,9},{5,13},{9,1},{13,5},{2,10},{6,14},... | collective-permute-start | bytes 786440 | tf_op jit(solution)/shard_map/ppermute | solution.py:301
  61.8 2.4 %shard_map.130.total = f32[256,2048]{1,0:T(8,128)S(1)} custom-call(s32[4]{0:T(128)S(1)} %pad_add_fusion.where, bf16[256,512]{1,0:T(8,128)(2,1)S(1)} %shard_map.129.own.last, bf16[256,512]{1,0:T(8,128)(2,1)S(1)} %collective-permute-done.17.far, bf16[256,512]{1,0:T(8,128)(2,1)S(1)} %collective-permute-done.18.near, bf16[2048,2048]{1,0:T(8,128)(2,1)S(1)} %copy-done.1, ...), custom_call_target="tpu_custom_call" | custom-call | tf_op jit(solution)/shard_map/pallas_call | solution.py:27
  64.1 2.3 %collective-permute-done.16.across = bf16[256,512]{1,0:T(8,128)(2,1)S(1)} collective-permute-done((bf16[256,512]{1,0:T(8,128)(2,1)S(1)}, bf16[256,512]{1,0:T(8,128)(2,1)S(1)}, u32[]{:S(2)}, u32[]{:S(2)}) %collective-permute-start.16) | collective-permute-done | bytes 262176 | tf_op jit(solution)/shard_map/ppermute | solution.py:301
  66.4 1.0 %shard_map.132 = (bf16[256,512]{1,0:T(8,128)(2,1)S(1)}, bf16[256,512]{1,0:T(8,128)(2,1)S(1)}) custom-call(s32[4]{0:T(128)S(1)} %pad_add_fusion.where, bf16[256,512]{1,0:T(8,128)(2,1)S(1)} %collective-permute-done.16.across, bf16[2048,2048]{1,0:T(8,128)(2,1)S(1)} %copy-done.1, f32[256,2048]{1,0:T(8,128)S(1)} %shard_map.130.total), custom_call_target="tpu_custom_call" | custom-call | tf_op jit(solution)/shard_map/pallas_call | solution.py:27
  67.4 0.9 %collective-permute-start.19 = (bf16[256,512]{1,0:T(8,128)(2,1)S(1)}, bf16[256,512]{1,0:T(8,128)(2,1)S(1)}, u32[]{:S(2)}, u32[]{:S(2)}) collective-permute-start(bf16[256,512]{1,0:T(8,128)(2,1)S(1)} %get-tuple-element.55), channel_id=1, source_target_pairs={{0,4},{4,0},{8,12},{12,8},{1,5},{5,1},{9,13},{13,9},{2,6},{6,2},{1... | collective-permute-start | bytes 786440 | tf_op jit(solution)/shard_map/ppermute | solution.py:301
  68.3 1.9 %collective-permute-start.20 = (bf16[256,512]{1,0:T(8,128)(2,1)S(1)}, bf16[256,512]{1,0:T(8,128)(2,1)S(1)}, u32[]{:S(2)}, u32[]{:S(2)}) collective-permute-start(bf16[256,512]{1,0:T(8,128)(2,1)S(1)} %get-tuple-element.56), channel_id=1, source_target_pairs={{0,12},{4,8},{8,4},{12,0},{1,13},{5,9},{9,5},{13,1},{2,14},{6,10},... | collective-permute-start | bytes 786440 | tf_op jit(solution)/shard_map/ppermute | solution.py:301
  70.2 1.0 %shard_map.131 = (bf16[256,512]{1,0:T(8,128)(2,1)S(1)}, f32[256,512]{1,0:T(8,128)S(1)}) custom-call(s32[4]{0:T(128)S(1)} %pad_add_fusion.where, bf16[256,512]{1,0:T(8,128)(2,1)S(1)} %collective-permute-done.16.across, bf16[2048,2048]{1,0:T(8,128)(2,1)S(1)} %copy-done.1, f32[256,2048]{1,0:T(8,128)S(1)} %shard_map.130.total), custom_call_target="tpu_custom_call" | custom-call | tf_op jit(solution)/shard_map/pallas_call | solution.py:27
  71.2 0.8 collective-permute-start.21
  72.0 0.1 add_convert_fusion.1
  72.2 2.8 %collective-permute-done.19.after = bf16[256,512]{1,0:T(8,128)(2,1)S(1)} collective-permute-done((bf16[256,512]{1,0:T(8,128)(2,1)S(1)}, bf16[256,512]{1,0:T(8,128)(2,1)S(1)}, u32[]{:S(2)}, u32[]{:S(2)}) %collective-permute-start.19) | collective-permute-done | bytes 262176 | tf_op jit(solution)/shard_map/ppermute | solution.py:301
  74.9 1.0 %shard_map.133 = (f32[512,256]{1,0:T(8,128)}, bf16[512,512]{1,0:T(8,128)(2,1)}) custom-call(f32[512,256]{1,0:T(8,128)S(1)} %get-tuple-element.34.sums, f32[8,256]{1,0:T(8,128)S(1)} %get-tuple-element.35.decays, bf16[512,256]{1,0:T(8,128)(2,1)S(1)} %get-tuple-element.58.carried, bf16[256,512]{1,0:T(8,128)(2,1)S(1)} %get-tuple-element.47.own.after.head, ...), custom_call_target="tpu_custom_call" | custom-call | tf_op jit(solution)/shard_map/pallas_call | solution.py:27
  76.0 0.5 collective-permute-done.20
  76.5 5.9 %collective-permute-done.21 = bf16[256,512]{1,0:T(8,128)(2,1)S(1)} collective-permute-done((bf16[256,512]{1,0:T(8,128)(2,1)S(1)}, bf16[256,512]{1,0:T(8,128)(2,1)S(1)}, u32[]{:S(2)}, u32[]{:S(2)}) %collective-permute-start.21) | collective-permute-done | bytes 262176 | tf_op jit(solution)/shard_map/ppermute | solution.py:301
  82.4 0.1 add_convert_fusion
  82.5 0.8 pad_maximum_fusion
  (19 shorter events, 0.1 us)
Async XLA Ops:
  0.6 1.2 %copy-start = (bf16[512,4,256]{2,1,0:T(4,128)(2,1)S(1)}, bf16[512,4,256]{2,1,0:T(4,128)(2,1)}, u32[]{:S(2)}) copy-start(bf16[512,4,256]{2,1,0:T(4,128)(2,1)} %param.13) | copy-start | bytes 3145732
  0.6 2.0 %copy-start.2 = (bf16[512,512]{1,0:T(8,128)(2,1)S(1)}, bf16[512,512]{1,0:T(8,128)(2,1)}, u32[]{:S(2)}) copy-start(bf16[512,512]{1,0:T(8,128)(2,1)} %grad_hbm.3) | copy-start | bytes 1572868
  1.9 16.7 %copy-start.8 = (f32[8]{0:T(128)S(1)}, f32[8]{0:T(128)}, u32[]{:S(2)}) copy-start(f32[8]{0:T(128)} %skips.1) | copy-start | bytes 100
  2.4 16.2 %copy-start.3 = (bf16[512,512]{1,0:T(8,128)(2,1)S(1)}, bf16[512,512]{1,0:T(8,128)(2,1)}, u32[]{:S(2)}) copy-start(bf16[512,512]{1,0:T(8,128)(2,1)} %conv_hbm.1) | copy-start | bytes 1572868
  2.4 16.2 %copy-start.4 = (f32[8,64,256]{2,1,0:T(8,128)S(1)}, f32[8,64,256]{2,1,0:T(8,128)}, u32[]{:S(2)}) copy-start(f32[8,64,256]{2,1,0:T(8,128)} %param.18) | copy-start | bytes 1572868
  2.4 16.2 %copy-start.6 = (f32[8,512]{1,0:T(8,128)S(1)}, f32[8,512]{1,0:T(8,128)}, u32[]{:S(2)}) copy-start(f32[8,512]{1,0:T(8,128)} %step_hbm.1) | copy-start | bytes 49156
  2.6 0.8 copy-start.7
  3.4 31.9 %copy-start.5 = (f32[4,512]{1,0:T(4,128)S(1)}, f32[4,512]{1,0:T(4,128)}, u32[]{:S(2)}) copy-start(f32[4,512]{1,0:T(4,128)} %taps.3) | copy-start | bytes 24580
  5.3 7.0 %collective-permute-start = (bf16[136,256]{1,0:T(8,128)(2,1)S(1)}, bf16[136,256]{1,0:T(8,128)(2,1)S(1)}, u32[]{:S(2)}, u32[]{:S(2)}) collective-permute-start(bf16[136,256]{1,0:T(8,128)(2,1)S(1)} %get-tuple-element.36), channel_id=1, source_target_pairs={{0,16},{16,0},{32,48},{48,32},{64,80},{80,64},{96,112},{112,96},{1... | collective-permute-start | bytes 208904 | tf_op jit(solution)/shard_map/ppermute | solution.py:301
  8.6 3.7 %collective-permute-start.1 = (bf16[136,256]{1,0:T(8,128)(2,1)S(1)}, bf16[136,256]{1,0:T(8,128)(2,1)S(1)}, u32[]{:S(2)}, u32[]{:S(2)}) collective-permute-start(bf16[136,256]{1,0:T(8,128)(2,1)S(1)} %get-tuple-element.37), channel_id=1, source_target_pairs={{0,32},{16,48},{32,0},{48,16},{64,96},{80,112},{96,64},{112,80},{1... | collective-permute-start | bytes 208904 | tf_op jit(solution)/shard_map/ppermute | solution.py:301
  8.6 5.4 %collective-permute-start.2 = (bf16[136,256]{1,0:T(8,128)(2,1)S(1)}, bf16[136,256]{1,0:T(8,128)(2,1)S(1)}, u32[]{:S(2)}, u32[]{:S(2)}) collective-permute-start(bf16[136,256]{1,0:T(8,128)(2,1)S(1)} %get-tuple-element.38), channel_id=1, source_target_pairs={{0,48},{16,32},{32,16},{48,0},{64,112},{80,96},{96,80},{112,64},{1... | collective-permute-start | bytes 208904 | tf_op jit(solution)/shard_map/ppermute | solution.py:301
  10.3 39.1 %copy-start.1 = (bf16[2048,2048]{1,0:T(8,128)(2,1)S(1)}, bf16[2048,2048]{1,0:T(8,128)(2,1)}, u32[]{:S(2)}) copy-start(bf16[2048,2048]{1,0:T(8,128)(2,1)} %weight.11) | copy-start | bytes 25165828
  14.7 9.4 %collective-permute-start.3 = (bf16[136,256]{1,0:T(8,128)(2,1)S(1)}, bf16[136,256]{1,0:T(8,128)(2,1)S(1)}, u32[]{:S(2)}, u32[]{:S(2)}) collective-permute-start(bf16[136,256]{1,0:T(8,128)(2,1)S(1)} %shard_map.122.after), channel_id=1, source_target_pairs={{128,0},{144,16},{160,32},{176,48},{192,64},{208,80},{224,96},{240... | collective-permute-start | bytes 208904 | tf_op jit(solution)/shard_map/ppermute | solution.py:296
  16.0 9.7 %collective-permute-start.4 = (bf16[136,256]{1,0:T(8,128)(2,1)S(1)}, bf16[136,256]{1,0:T(8,128)(2,1)S(1)}, u32[]{:S(2)}, u32[]{:S(2)}) collective-permute-start(bf16[136,256]{1,0:T(8,128)(2,1)S(1)} %shard_map.122.after), channel_id=1, source_target_pairs={{64,0},{80,16},{96,32},{112,48},{128,64},{144,80},{160,96},{176,11... | collective-permute-start | bytes 208904 | tf_op jit(solution)/shard_map/ppermute | solution.py:296
  17.3 9.9 %collective-permute-start.5 = (bf16[136,256]{1,0:T(8,128)(2,1)S(1)}, bf16[136,256]{1,0:T(8,128)(2,1)S(1)}, u32[]{:S(2)}, u32[]{:S(2)}) collective-permute-start(bf16[136,256]{1,0:T(8,128)(2,1)S(1)} %shard_map.122.after), channel_id=1, source_target_pairs={{192,0},{208,16},{224,32},{240,48},{193,1},{209,17},{225,33},{241,... | collective-permute-start | bytes 208904 | tf_op jit(solution)/shard_map/ppermute | solution.py:296
  27.8 3.5 %collective-permute-start.6 = (bf16[8,16,256]{2,1,0:T(8,128)(2,1)S(1)}, bf16[8,16,256]{2,1,0:T(8,128)(2,1)S(1)}, u32[]{:S(2)}, u32[]{:S(2)}) collective-permute-start(bf16[8,16,256]{2,1,0:T(8,128)(2,1)S(1)} %get-tuple-element.42), channel_id=1, source_target_pairs={{0,16},{16,0},{32,48},{48,32},{64,80},{80,64},{96,112},{112,96},{1... | collective-permute-start | bytes 196616 | tf_op jit(solution)/shard_map/ppermute | solution.py:301
  29.5 4.1 %collective-permute-start.7 = (bf16[8,16,256]{2,1,0:T(8,128)(2,1)S(1)}, bf16[8,16,256]{2,1,0:T(8,128)(2,1)S(1)}, u32[]{:S(2)}, u32[]{:S(2)}) collective-permute-start(bf16[8,16,256]{2,1,0:T(8,128)(2,1)S(1)} %get-tuple-element.43), channel_id=1, source_target_pairs={{0,32},{16,48},{32,0},{48,16},{64,96},{80,112},{96,64},{112,80},{1... | collective-permute-start | bytes 196616 | tf_op jit(solution)/shard_map/ppermute | solution.py:301
  31.3 4.1 %collective-permute-start.8 = (bf16[8,16,256]{2,1,0:T(8,128)(2,1)S(1)}, bf16[8,16,256]{2,1,0:T(8,128)(2,1)S(1)}, u32[]{:S(2)}, u32[]{:S(2)}) collective-permute-start(bf16[8,16,256]{2,1,0:T(8,128)(2,1)S(1)} %get-tuple-element.44), channel_id=1, source_target_pairs={{0,48},{16,32},{32,16},{48,0},{64,112},{80,96},{96,80},{112,64},{1... | collective-permute-start | bytes 196616 | tf_op jit(solution)/shard_map/ppermute | solution.py:301
  36.5 6.2 %collective-permute-start.15 = (bf16[16,512]{1,0:T(8,128)(2,1)S(1)}, bf16[16,512]{1,0:T(8,128)(2,1)S(1)}, u32[]{:S(2)}, u32[]{:S(2)}) collective-permute-start(bf16[16,512]{1,0:T(8,128)(2,1)S(1)} %get-tuple-element.53), channel_id=1, source_target_pairs={{16,0},{32,16},{48,32},{64,48},{80,64},{96,80},{112,96},{128,112},... | collective-permute-start | bytes 49160 | tf_op jit(solution)/shard_map/ppermute | solution.py:296
  38.8 9.6 %collective-permute-start.10 = (bf16[256,512]{1,0:T(8,128)(2,1)S(1)}, bf16[256,512]{1,0:T(8,128)(2,1)S(1)}, u32[]{:S(2)}, u32[]{:S(2)}) collective-permute-start(bf16[256,512]{1,0:T(8,128)(2,1)S(1)} %get-tuple-element.47.own.after.head), channel_id=1, source_target_pairs={{0,3},{1,2},{2,1},{3,0},{4,7},{5,6},{6,5},{7,4},{8,11},{9,10},{10,... | collective-permute-start | bytes 786440 | tf_op jit(solution)/shard_map/ppermute | solution.py:301
  40.9 8.6 %collective-permute-start.11 = (bf16[256,512]{1,0:T(8,128)(2,1)S(1)}, bf16[256,512]{1,0:T(8,128)(2,1)S(1)}, u32[]{:S(2)}, u32[]{:S(2)}) collective-permute-start(bf16[256,512]{1,0:T(8,128)(2,1)S(1)} %get-tuple-element.47.own.after.head), channel_id=1, source_target_pairs={{0,1},{1,0},{2,3},{3,2},{4,5},{5,4},{6,7},{7,6},{8,9},{9,8},{10,11... | collective-permute-start | bytes 786440 | tf_op jit(solution)/shard_map/ppermute | solution.py:301
  40.9 14.3 %collective-permute-start.9 = (bf16[256,512]{1,0:T(8,128)(2,1)S(1)}, bf16[256,512]{1,0:T(8,128)(2,1)S(1)}, u32[]{:S(2)}, u32[]{:S(2)}) collective-permute-start(bf16[256,512]{1,0:T(8,128)(2,1)S(1)} %get-tuple-element.47.own.after.head), channel_id=1, source_target_pairs={{0,2},{1,3},{2,0},{3,1},{4,6},{5,7},{6,4},{7,5},{8,10},{9,11},{10,... | collective-permute-start | bytes 786440 | tf_op jit(solution)/shard_map/ppermute | solution.py:301
  43.2 16.8 %collective-permute-start.17 = (bf16[256,512]{1,0:T(8,128)(2,1)S(1)}, bf16[256,512]{1,0:T(8,128)(2,1)S(1)}, u32[]{:S(2)}, u32[]{:S(2)}) collective-permute-start(bf16[256,512]{1,0:T(8,128)(2,1)S(1)} %shard_map.129.own.last), channel_id=1, source_target_pairs={{0,3},{1,2},{2,1},{3,0},{4,7},{5,6},{6,5},{7,4},{8,11},{9,10},{10,... | collective-permute-start | bytes 786440 | tf_op jit(solution)/shard_map/ppermute | solution.py:301
  45.2 16.5 %collective-permute-start.18 = (bf16[256,512]{1,0:T(8,128)(2,1)S(1)}, bf16[256,512]{1,0:T(8,128)(2,1)S(1)}, u32[]{:S(2)}, u32[]{:S(2)}) collective-permute-start(bf16[256,512]{1,0:T(8,128)(2,1)S(1)} %shard_map.129.own.last), channel_id=1, source_target_pairs={{0,1},{1,0},{2,3},{3,2},{4,5},{5,4},{6,7},{7,6},{8,9},{9,8},{10,11... | collective-permute-start | bytes 786440 | tf_op jit(solution)/shard_map/ppermute | solution.py:301
  48.4 18.0 %collective-permute-start.16 = (bf16[256,512]{1,0:T(8,128)(2,1)S(1)}, bf16[256,512]{1,0:T(8,128)(2,1)S(1)}, u32[]{:S(2)}, u32[]{:S(2)}) collective-permute-start(bf16[256,512]{1,0:T(8,128)(2,1)S(1)} %shard_map.129.own.last), channel_id=1, source_target_pairs={{0,2},{1,3},{2,0},{3,1},{4,6},{5,7},{6,4},{7,5},{8,10},{9,11},{10,... | collective-permute-start | bytes 786440 | tf_op jit(solution)/shard_map/ppermute | solution.py:301
  56.2 15.0 %collective-permute-start.12 = (bf16[256,512]{1,0:T(8,128)(2,1)S(1)}, bf16[256,512]{1,0:T(8,128)(2,1)S(1)}, u32[]{:S(2)}, u32[]{:S(2)}) collective-permute-start(bf16[256,512]{1,0:T(8,128)(2,1)S(1)} %get-tuple-element.49), channel_id=1, source_target_pairs={{0,4},{4,0},{8,12},{12,8},{1,5},{5,1},{9,13},{13,9},{2,6},{6,2},{1... | collective-permute-start | bytes 786440 | tf_op jit(solution)/shard_map/ppermute | solution.py:301
  57.0 15.0 %collective-permute-start.13 = (bf16[256,512]{1,0:T(8,128)(2,1)S(1)}, bf16[256,512]{1,0:T(8,128)(2,1)S(1)}, u32[]{:S(2)}, u32[]{:S(2)}) collective-permute-start(bf16[256,512]{1,0:T(8,128)(2,1)S(1)} %get-tuple-element.50), channel_id=1, source_target_pairs={{0,12},{4,8},{8,4},{12,0},{1,13},{5,9},{9,5},{13,1},{2,14},{6,10},... | collective-permute-start | bytes 786440 | tf_op jit(solution)/shard_map/ppermute | solution.py:301
  60.0 12.1 %collective-permute-start.14 = (bf16[256,512]{1,0:T(8,128)(2,1)S(1)}, bf16[256,512]{1,0:T(8,128)(2,1)S(1)}, u32[]{:S(2)}, u32[]{:S(2)}) collective-permute-start(bf16[256,512]{1,0:T(8,128)(2,1)S(1)} %get-tuple-element.51), channel_id=1, source_target_pairs={{0,8},{4,12},{8,0},{12,4},{1,9},{5,13},{9,1},{13,5},{2,10},{6,14},... | collective-permute-start | bytes 786440 | tf_op jit(solution)/shard_map/ppermute | solution.py:301
  67.4 7.5 %collective-permute-start.19 = (bf16[256,512]{1,0:T(8,128)(2,1)S(1)}, bf16[256,512]{1,0:T(8,128)(2,1)S(1)}, u32[]{:S(2)}, u32[]{:S(2)}) collective-permute-start(bf16[256,512]{1,0:T(8,128)(2,1)S(1)} %get-tuple-element.55), channel_id=1, source_target_pairs={{0,4},{4,0},{8,12},{12,8},{1,5},{5,1},{9,13},{13,9},{2,6},{6,2},{1... | collective-permute-start | bytes 786440 | tf_op jit(solution)/shard_map/ppermute | solution.py:301
  68.3 8.2 %collective-permute-start.20 = (bf16[256,512]{1,0:T(8,128)(2,1)S(1)}, bf16[256,512]{1,0:T(8,128)(2,1)S(1)}, u32[]{:S(2)}, u32[]{:S(2)}) collective-permute-start(bf16[256,512]{1,0:T(8,128)(2,1)S(1)} %get-tuple-element.56), channel_id=1, source_target_pairs={{0,12},{4,8},{8,4},{12,0},{1,13},{5,9},{9,5},{13,1},{2,14},{6,10},... | collective-permute-start | bytes 786440 | tf_op jit(solution)/shard_map/ppermute | solution.py:301
  71.2 11.2 %collective-permute-start.21 = (bf16[256,512]{1,0:T(8,128)(2,1)S(1)}, bf16[256,512]{1,0:T(8,128)(2,1)S(1)}, u32[]{:S(2)}, u32[]{:S(2)}) collective-permute-start(bf16[256,512]{1,0:T(8,128)(2,1)S(1)} %get-tuple-element.57), channel_id=1, source_target_pairs={{0,8},{4,12},{8,0},{12,4},{1,9},{5,13},{9,1},{13,5},{2,10},{6,14},... | collective-permute-start | bytes 786440 | tf_op jit(solution)/shard_map/ppermute | solution.py:301

commit v5 on v4

--- a/solution.py
+++ b/solution.py
@@ -400,7 +400,7 @@
             (where, across, proj_weight, partial),
             specs=(SMEM,),
         )
-        came = [swapped(value, "row", flip) for value, flip in ((near, 1), (far, 3), (over, 2))]
+        came = [swapped(value, "row", flip) for value, flip in ((far, 3), (near, 1), (over, 2))]
         sums_of.append((kept, *came))
         after = kept
     state, x_grad = call(

time: 83.6 us -> 83.7 us (level)
  transfers between devices with their start and end apart: 22 -> 22, of which waited for: 12 -> 11; matrix products, arithmetic and copies ran while one was open for 3% -> 3% of each run, Pallas kernels for 16% -> 16%
where the time goes in v5:
time: 83.7 us; the launch traced here: 83.5 us
  starting transfers between devices  30.3 us (36%)
  waiting for transfers between devices  28.4 us (34%)
  Pallas kernels  18 us (22%)
  local copies, waits for them, and re-layouts  4.57 us (5%)
  other arithmetic  1.18 us (1%)
  between operations  0.95 us (1%)
    ppermute x18, starting transfers between devices, swapped(): lax.ppermute(value, axis, [(place, place ^ flip) for place in range(count)])  24.2 us
    ppermute x18, waiting for transfers between devices, swapped(): lax.ppermute(value, axis, [(place, place ^ flip) for place in range(count)])  23.3 us
    pallas_call x13, Pallas kernels, call(): pl.pallas_call(kernel, out_shape=outs, in_specs=list(specs) + [VMEM] * (l...  18 us
    ppermute x4, starting transfers between devices, earlier(): lax.ppermute(value, 'ctx', [(place, place - steps) for place in range(ste...  6.15 us
    ppermute x4, waiting for transfers between devices, earlier(): lax.ppermute(value, 'ctx', [(place, place - steps) for place in range(ste...  5.1 us
    unnamed x20, local copies, waits for them, and re-layouts  2.11 us
    dynamic_slice x1, local copies, waits for them, and re-layouts, on_device(): writes = lax.dynamic_index_in_dim(input_mix, group, 1, keepdims=False)  1.92 us
  transfers between devices with their start and end apart: 22, of which 11 were waited for; matrix products, arithmetic and copies ran while one was open for 3% of the time, Pallas kernels for 16%

profile of v5, /device:TPU:1, one launch (start us, length us, event | category | flops | bytes accessed | tf_op | source)
XLA Modules:
  0.0 83.5 jit_solution(18340765966166542593)
XLA Ops:
  0.6 0.0 copy-start
  0.7 1.2 %copy-done = bf16[512,4,256]{2,1,0:T(4,128)(2,1)S(1)} copy-done((bf16[512,4,256]{2,1,0:T(4,128)(2,1)S(1)}, bf16[512,4,256]{2,1,0:T(4,128)(2,1)}, u32[]{:S(2)}) %copy-start) | copy-done | bytes 1048600
  1.9 0.5 constant_dynamic-slice_fusion.1
  2.4 0.0 copy-start.3
  2.4 0.0 copy-start.4
  2.4 0.0 copy-start.6
  2.5 0.1 pad_add_fusion.where
  2.6 0.8 copy-done.7
  3.4 1.9 %shard_map.121 = (f32[512,256]{1,0:T(8,128)S(1)}, f32[8,512]{1,0:T(8,128)S(1)}, f32[8,256]{1,0:T(8,128)S(1)}, bf16[136,256]{1,0:T(8,128)(2,1)S(1)}, bf16[136,256...) custom-call(s32[4]{0:T(128)S(1)} %pad_add_fusion.where, bf16[512,512]{1,0:T(8,128)(2,1)S(1)} %copy-done.2, ...), custom_call_target="tpu_custom_call" | custom-call | tf_op jit(solution)/shard_map/pallas_call | solution.py:27
  5.3 3.3 %collective-permute-start = (bf16[136,256]{1,0:T(8,128)(2,1)S(1)}, bf16[136,256]{1,0:T(8,128)(2,1)S(1)}, u32[]{:S(2)}, u32[]{:S(2)}) collective-permute-start(bf16[136,256]{1,0:T(8,128)(2,1)S(1)} %get-tuple-element.36), channel_id=1, source_target_pairs={{0,16},{16,0},{32,48},{48,32},{64,80},{80,64},{96,112},{112,96},{1... | collective-permute-start | bytes 208904 | tf_op jit(solution)/shard_map/ppermute | solution.py:301
  8.6 0.0 collective-permute-start.1
  8.6 1.7 %collective-permute-start.2 = (bf16[136,256]{1,0:T(8,128)(2,1)S(1)}, bf16[136,256]{1,0:T(8,128)(2,1)S(1)}, u32[]{:S(2)}, u32[]{:S(2)}) collective-permute-start(bf16[136,256]{1,0:T(8,128)(2,1)S(1)} %get-tuple-element.38), channel_id=1, source_target_pairs={{0,48},{16,32},{32,16},{48,0},{64,112},{80,96},{96,80},{112,64},{1... | collective-permute-start | bytes 208904 | tf_op jit(solution)/shard_map/ppermute | solution.py:301
  10.3 1.9 %constant_dynamic-slice_fusion = bf16[512,1,256]{2,1,0:T(2,128)(2,1)S(1)} fusion(bf16[512,4,256]{2,1,0:T(4,128)(2,1)} %param.12, s32[]{:T(128)S(6)} %select_n.22), kind=kLoop, calls=%fused_computation.6 | loop fusion | bytes 524292 | tf_op jit(solution)/shard_map/jit(dynamic_index_in_dim)/dynamic_slice | solution.py:316
  12.3 0.0 collective-permute-done.one
  12.3 0.0 collective-permute-done.1.two
  12.4 1.7 %collective-permute-done.2.three = bf16[136,256]{1,0:T(8,128)(2,1)S(1)} collective-permute-done((bf16[136,256]{1,0:T(8,128)(2,1)S(1)}, bf16[136,256]{1,0:T(8,128)(2,1)S(1)}, u32[]{:S(2)}, u32[]{:S(2)}) %collective-permute-start.2) | collective-permute-done | bytes 69664 | tf_op jit(solution)/shard_map/ppermute | solution.py:301
  14.0 0.6 shard_map.122.after
  14.7 1.3 %collective-permute-start.3 = (bf16[136,256]{1,0:T(8,128)(2,1)S(1)}, bf16[136,256]{1,0:T(8,128)(2,1)S(1)}, u32[]{:S(2)}, u32[]{:S(2)}) collective-permute-start(bf16[136,256]{1,0:T(8,128)(2,1)S(1)} %shard_map.122.after), channel_id=1, source_target_pairs={{128,0},{144,16},{160,32},{176,48},{192,64},{208,80},{224,96},{240... | collective-permute-start | bytes 208904 | tf_op jit(solution)/shard_map/ppermute | solution.py:296
  16.0 1.3 %collective-permute-start.4 = (bf16[136,256]{1,0:T(8,128)(2,1)S(1)}, bf16[136,256]{1,0:T(8,128)(2,1)S(1)}, u32[]{:S(2)}, u32[]{:S(2)}) collective-permute-start(bf16[136,256]{1,0:T(8,128)(2,1)S(1)} %shard_map.122.after), channel_id=1, source_target_pairs={{64,0},{80,16},{96,32},{112,48},{128,64},{144,80},{160,96},{176,11... | collective-permute-start | bytes 208904 | tf_op jit(solution)/shard_map/ppermute | solution.py:296
  17.3 1.3 %collective-permute-start.5 = (bf16[136,256]{1,0:T(8,128)(2,1)S(1)}, bf16[136,256]{1,0:T(8,128)(2,1)S(1)}, u32[]{:S(2)}, u32[]{:S(2)}) collective-permute-start(bf16[136,256]{1,0:T(8,128)(2,1)S(1)} %shard_map.122.after), channel_id=1, source_target_pairs={{192,0},{208,16},{224,32},{240,48},{193,1},{209,17},{225,33},{241,... | collective-permute-start | bytes 208904 | tf_op jit(solution)/shard_map/ppermute | solution.py:296
  18.6 3.4 %shard_map.123 = (f32[512,512]{1,0:T(8,128)S(1)}, f32[512,512]{1,0:T(8,128)S(1)}, f32[8,16,256]{2,1,0:T(8,128)S(1)}) custom-call(s32[4]{0:T(128)S(1)} %pad_add_fusion.where, f32[8]{0:T(128)S(1)} %copy-done.8, bf16[512,512]{1,0:T(8,128)(2,1)S(1)} %copy-done.2, bf16[512,512]{1,0:T(8,128)(2,1)S(1)} %copy-done.3, f32[8,512]{1,0:T(8,128)S(1)} %copy-done.6, ...), custom_call_target="tpu_custom_call" | custom-call | tf_op jit(solution)/shard_map/pallas_call | solution.py:27
  22.0 2.0 %collective-permute-done.3.middle = bf16[136,256]{1,0:T(8,128)(2,1)S(1)} collective-permute-done((bf16[136,256]{1,0:T(8,128)(2,1)S(1)}, bf16[136,256]{1,0:T(8,128)(2,1)S(1)}, u32[]{:S(2)}, u32[]{:S(2)}) %collective-permute-start.3) | collective-permute-done | bytes 69664 | tf_op jit(solution)/shard_map/ppermute | solution.py:296
  24.0 1.6 %collective-permute-done.4.near = bf16[136,256]{1,0:T(8,128)(2,1)S(1)} collective-permute-done((bf16[136,256]{1,0:T(8,128)(2,1)S(1)}, bf16[136,256]{1,0:T(8,128)(2,1)S(1)}, u32[]{:S(2)}, u32[]{:S(2)}) %collective-permute-start.4) | collective-permute-done | bytes 69664 | tf_op jit(solution)/shard_map/ppermute | solution.py:296
  25.6 1.5 %collective-permute-done.5.far = bf16[136,256]{1,0:T(8,128)(2,1)S(1)} collective-permute-done((bf16[136,256]{1,0:T(8,128)(2,1)S(1)}, bf16[136,256]{1,0:T(8,128)(2,1)S(1)}, u32[]{:S(2)}, u32[]{:S(2)}) %collective-permute-start.5) | collective-permute-done | bytes 69664 | tf_op jit(solution)/shard_map/ppermute | solution.py:296
  27.1 0.7 shard_map.124
  27.8 1.7 %collective-permute-start.6 = (bf16[8,16,256]{2,1,0:T(8,128)(2,1)S(1)}, bf16[8,16,256]{2,1,0:T(8,128)(2,1)S(1)}, u32[]{:S(2)}, u32[]{:S(2)}) collective-permute-start(bf16[8,16,256]{2,1,0:T(8,128)(2,1)S(1)} %get-tuple-element.42), channel_id=1, source_target_pairs={{0,16},{16,0},{32,48},{48,32},{64,80},{80,64},{96,112},{112,96},{1... | collective-permute-start | bytes 196616 | tf_op jit(solution)/shard_map/ppermute | solution.py:301
  29.5 1.7 %collective-permute-start.7 = (bf16[8,16,256]{2,1,0:T(8,128)(2,1)S(1)}, bf16[8,16,256]{2,1,0:T(8,128)(2,1)S(1)}, u32[]{:S(2)}, u32[]{:S(2)}) collective-permute-start(bf16[8,16,256]{2,1,0:T(8,128)(2,1)S(1)} %get-tuple-element.43), channel_id=1, source_target_pairs={{0,32},{16,48},{32,0},{48,16},{64,96},{80,112},{96,64},{112,80},{1... | collective-permute-start | bytes 196616 | tf_op jit(solution)/shard_map/ppermute | solution.py:301
  31.3 0.1 collective-permute-start.8
  31.4 0.0 collective-permute-done.6.first
  31.4 2.3 %collective-permute-done.7.second = bf16[8,16,256]{2,1,0:T(8,128)(2,1)S(1)} collective-permute-done((bf16[8,16,256]{2,1,0:T(8,128)(2,1)S(1)}, bf16[8,16,256]{2,1,0:T(8,128)(2,1)S(1)}, u32[]{:S(2)}, u32[]{:S(2)}) %collective-permute-start.7) | collective-permute-done | bytes 65568 | tf_op jit(solution)/shard_map/ppermute | solution.py:301
  33.6 1.7 %collective-permute-done.8.third = bf16[8,16,256]{2,1,0:T(8,128)(2,1)S(1)} collective-permute-done((bf16[8,16,256]{2,1,0:T(8,128)(2,1)S(1)}, bf16[8,16,256]{2,1,0:T(8,128)(2,1)S(1)}, u32[]{:S(2)}, u32[]{:S(2)}) %collective-permute-start.8) | collective-permute-done | bytes 65568 | tf_op jit(solution)/shard_map/ppermute | solution.py:301
  35.4 1.2 %shard_map.125 = (bf16[256,512]{1,0:T(8,128)(2,1)S(1)}, bf16[16,512]{1,0:T(8,128)(2,1)S(1)}, bf16[256,512]{1,0:T(8,128)(2,1)S(1)}, bf16[512,256]{1,0:T(8,128)(2,1)S(1)}) custom-call(s32[4]{0:T(128)S(1)} %pad_add_fusion.where, bf16[8,16,256]{2,1,0:T(8,128)(2,1)S(1)} %get-tuple-element.41.own, bf16[8,16,256]{2,1,0:T(8,128)(2,1)S(1)} %collective-permute-done.6.first, ...), custom_call_target="tpu_custom_call" | custom-call | tf_op jit(solution)/shard_map/pallas_call | solution.py:27
  36.5 2.3 %collective-permute-start.15 = (bf16[16,512]{1,0:T(8,128)(2,1)S(1)}, bf16[16,512]{1,0:T(8,128)(2,1)S(1)}, u32[]{:S(2)}, u32[]{:S(2)}) collective-permute-start(bf16[16,512]{1,0:T(8,128)(2,1)S(1)} %get-tuple-element.53), channel_id=1, source_target_pairs={{16,0},{32,16},{48,32},{64,48},{80,64},{96,80},{112,96},{128,112},... | collective-permute-start | bytes 49160 | tf_op jit(solution)/shard_map/ppermute | solution.py:296
  38.8 2.1 %collective-permute-start.10 = (bf16[256,512]{1,0:T(8,128)(2,1)S(1)}, bf16[256,512]{1,0:T(8,128)(2,1)S(1)}, u32[]{:S(2)}, u32[]{:S(2)}) collective-permute-start(bf16[256,512]{1,0:T(8,128)(2,1)S(1)} %get-tuple-element.47.own.after.head), channel_id=1, source_target_pairs={{0,3},{1,2},{2,1},{3,0},{4,7},{5,6},{6,5},{7,4},{8,11},{9,10},{10,... | collective-permute-start | bytes 786440 | tf_op jit(solution)/shard_map/ppermute | solution.py:301
  40.9 0.0 collective-permute-start.11
  40.9 1.9 %collective-permute-start.9 = (bf16[256,512]{1,0:T(8,128)(2,1)S(1)}, bf16[256,512]{1,0:T(8,128)(2,1)S(1)}, u32[]{:S(2)}, u32[]{:S(2)}) collective-permute-start(bf16[256,512]{1,0:T(8,128)(2,1)S(1)} %get-tuple-element.47.own.after.head), channel_id=1, source_target_pairs={{0,2},{1,3},{2,0},{3,1},{4,6},{5,7},{6,4},{7,5},{8,10},{9,11},{10,... | collective-permute-start | bytes 786440 | tf_op jit(solution)/shard_map/ppermute | solution.py:301
  42.8 0.4 shard_map.129.own.last
  43.2 2.1 %collective-permute-start.17 = (bf16[256,512]{1,0:T(8,128)(2,1)S(1)}, bf16[256,512]{1,0:T(8,128)(2,1)S(1)}, u32[]{:S(2)}, u32[]{:S(2)}) collective-permute-start(bf16[256,512]{1,0:T(8,128)(2,1)S(1)} %shard_map.129.own.last), channel_id=1, source_target_pairs={{0,3},{1,2},{2,1},{3,0},{4,7},{5,6},{6,5},{7,4},{8,11},{9,10},{10,... | collective-permute-start | bytes 786440 | tf_op jit(solution)/shard_map/ppermute | solution.py:301
  45.2 0.0 collective-permute-start.18
  45.2 3.2 %collective-permute-done.10.far = bf16[256,512]{1,0:T(8,128)(2,1)S(1)} collective-permute-done((bf16[256,512]{1,0:T(8,128)(2,1)S(1)}, bf16[256,512]{1,0:T(8,128)(2,1)S(1)}, u32[]{:S(2)}, u32[]{:S(2)}) %collective-permute-start.10) | collective-permute-done | bytes 262176 | tf_op jit(solution)/shard_map/ppermute | solution.py:301
  48.4 1.0 %collective-permute-start.16 = (bf16[256,512]{1,0:T(8,128)(2,1)S(1)}, bf16[256,512]{1,0:T(8,128)(2,1)S(1)}, u32[]{:S(2)}, u32[]{:S(2)}) collective-permute-start(bf16[256,512]{1,0:T(8,128)(2,1)S(1)} %shard_map.129.own.last), channel_id=1, source_target_pairs={{0,2},{1,3},{2,0},{3,1},{4,6},{5,7},{6,4},{7,5},{8,10},{9,11},{10,... | collective-permute-start | bytes 786440 | tf_op jit(solution)/shard_map/ppermute | solution.py:301
  49.5 0.0 collective-permute-done.11.near
  49.5 2.4 %shard_map.126.total = f32[256,2048]{1,0:T(8,128)S(1)} custom-call(s32[4]{0:T(128)S(1)} %pad_add_fusion.where, bf16[256,512]{1,0:T(8,128)(2,1)S(1)} %get-tuple-element.47.own.after.head, bf16[256,512]{1,0:T(8,128)(2,1)S(1)} %collective-permute-done.10.far, bf16[256,512]{1,0:T(8,128)(2,1)S(1)} %collective-permute-done.11.near, ...), custom_call_target="tpu_custom_call" | custom-call | tf_op jit(solution)/shard_map/pallas_call | solution.py:27
  51.8 3.3 %collective-permute-done.9.across = bf16[256,512]{1,0:T(8,128)(2,1)S(1)} collective-permute-done((bf16[256,512]{1,0:T(8,128)(2,1)S(1)}, bf16[256,512]{1,0:T(8,128)(2,1)S(1)}, u32[]{:S(2)}, u32[]{:S(2)}) %collective-permute-start.9) | collective-permute-done | bytes 262176 | tf_op jit(solution)/shard_map/ppermute | solution.py:301
  55.1 1.0 %shard_map.128 = (bf16[256,512]{1,0:T(8,128)(2,1)S(1)}, bf16[256,512]{1,0:T(8,128)(2,1)S(1)}) custom-call(s32[4]{0:T(128)S(1)} %pad_add_fusion.where, bf16[256,512]{1,0:T(8,128)(2,1)S(1)} %collective-permute-done.9.across, bf16[2048,2048]{1,0:T(8,128)(2,1)S(1)} %copy-done.1, f32[256,2048]{1,0:T(8,128)S(1)} %shard_map.126.total), custom_call_target="tpu_custom_call" | custom-call | tf_op jit(solution)/shard_map/pallas_call | solution.py:27
  56.2 2.3 %collective-permute-start.12 = (bf16[256,512]{1,0:T(8,128)(2,1)S(1)}, bf16[256,512]{1,0:T(8,128)(2,1)S(1)}, u32[]{:S(2)}, u32[]{:S(2)}) collective-permute-start(bf16[256,512]{1,0:T(8,128)(2,1)S(1)} %get-tuple-element.49), channel_id=1, source_target_pairs={{0,12},{4,8},{8,4},{12,0},{1,13},{5,9},{9,5},{13,1},{2,14},{6,10},... | collective-permute-start | bytes 786440 | tf_op jit(solution)/shard_map/ppermute | solution.py:301
  58.5 0.0 collective-permute-start.13
  58.5 1.0 %shard_map.127 = (bf16[256,512]{1,0:T(8,128)(2,1)S(1)}, f32[256,512]{1,0:T(8,128)S(1)}) custom-call(s32[4]{0:T(128)S(1)} %pad_add_fusion.where, bf16[256,512]{1,0:T(8,128)(2,1)S(1)} %collective-permute-done.9.across, bf16[2048,2048]{1,0:T(8,128)(2,1)S(1)} %copy-done.1, f32[256,2048]{1,0:T(8,128)S(1)} %shard_map.126.total), custom_call_target="tpu_custom_call" | custom-call | tf_op jit(solution)/shard_map/pallas_call | solution.py:27
  59.5 2.2 %collective-permute-start.14 = (bf16[256,512]{1,0:T(8,128)(2,1)S(1)}, bf16[256,512]{1,0:T(8,128)(2,1)S(1)}, u32[]{:S(2)}, u32[]{:S(2)}) collective-permute-start(bf16[256,512]{1,0:T(8,128)(2,1)S(1)} %get-tuple-element.51), channel_id=1, source_target_pairs={{0,8},{4,12},{8,0},{12,4},{1,9},{5,13},{9,1},{13,5},{2,10},{6,14},... | collective-permute-start | bytes 786440 | tf_op jit(solution)/shard_map/ppermute | solution.py:301
  61.7 0.0 collective-permute-done.18.near
  61.8 2.4 %shard_map.130.total = f32[256,2048]{1,0:T(8,128)S(1)} custom-call(s32[4]{0:T(128)S(1)} %pad_add_fusion.where, bf16[256,512]{1,0:T(8,128)(2,1)S(1)} %shard_map.129.own.last, bf16[256,512]{1,0:T(8,128)(2,1)S(1)} %collective-permute-done.17.far, bf16[256,512]{1,0:T(8,128)(2,1)S(1)} %collective-permute-done.18.near, bf16[2048,2048]{1,0:T(8,128)(2,1)S(1)} %copy-done.1, ...), custom_call_target="tpu_custom_call" | custom-call | tf_op jit(solution)/shard_map/pallas_call | solution.py:27
  64.1 2.3 %collective-permute-done.16.across = bf16[256,512]{1,0:T(8,128)(2,1)S(1)} collective-permute-done((bf16[256,512]{1,0:T(8,128)(2,1)S(1)}, bf16[256,512]{1,0:T(8,128)(2,1)S(1)}, u32[]{:S(2)}, u32[]{:S(2)}) %collective-permute-start.16) | collective-permute-done | bytes 262176 | tf_op jit(solution)/shard_map/ppermute | solution.py:301
  66.4 1.0 %shard_map.132 = (bf16[256,512]{1,0:T(8,128)(2,1)S(1)}, bf16[256,512]{1,0:T(8,128)(2,1)S(1)}) custom-call(s32[4]{0:T(128)S(1)} %pad_add_fusion.where, bf16[256,512]{1,0:T(8,128)(2,1)S(1)} %collective-permute-done.16.across, bf16[2048,2048]{1,0:T(8,128)(2,1)S(1)} %copy-done.1, f32[256,2048]{1,0:T(8,128)S(1)} %shard_map.130.total), custom_call_target="tpu_custom_call" | custom-call | tf_op jit(solution)/shard_map/pallas_call | solution.py:27
  67.4 2.3 %collective-permute-start.19 = (bf16[256,512]{1,0:T(8,128)(2,1)S(1)}, bf16[256,512]{1,0:T(8,128)(2,1)S(1)}, u32[]{:S(2)}, u32[]{:S(2)}) collective-permute-start(bf16[256,512]{1,0:T(8,128)(2,1)S(1)} %get-tuple-element.55), channel_id=1, source_target_pairs={{0,12},{4,8},{8,4},{12,0},{1,13},{5,9},{9,5},{13,1},{2,14},{6,10},... | collective-permute-start | bytes 786440 | tf_op jit(solution)/shard_map/ppermute | solution.py:301
  69.7 0.0 collective-permute-start.20
  69.7 1.0 %shard_map.131 = (bf16[256,512]{1,0:T(8,128)(2,1)S(1)}, f32[256,512]{1,0:T(8,128)S(1)}) custom-call(s32[4]{0:T(128)S(1)} %pad_add_fusion.where, bf16[256,512]{1,0:T(8,128)(2,1)S(1)} %collective-permute-done.16.across, bf16[2048,2048]{1,0:T(8,128)(2,1)S(1)} %copy-done.1, f32[256,2048]{1,0:T(8,128)S(1)} %shard_map.130.total), custom_call_target="tpu_custom_call" | custom-call | tf_op jit(solution)/shard_map/pallas_call | solution.py:27
  70.8 1.7 %collective-permute-start.21 = (bf16[256,512]{1,0:T(8,128)(2,1)S(1)}, bf16[256,512]{1,0:T(8,128)(2,1)S(1)}, u32[]{:S(2)}, u32[]{:S(2)}) collective-permute-start(bf16[256,512]{1,0:T(8,128)(2,1)S(1)} %get-tuple-element.57), channel_id=1, source_target_pairs={{0,8},{4,12},{8,0},{12,4},{1,9},{5,13},{9,1},{13,5},{2,10},{6,14},... | collective-permute-start | bytes 786440 | tf_op jit(solution)/shard_map/ppermute | solution.py:301
  72.5 0.0 collective-permute-done.14
  72.5 0.1 add_convert_fusion.1
  72.6 6.7 %collective-permute-done.19.after = bf16[256,512]{1,0:T(8,128)(2,1)S(1)} collective-permute-done((bf16[256,512]{1,0:T(8,128)(2,1)S(1)}, bf16[256,512]{1,0:T(8,128)(2,1)S(1)}, u32[]{:S(2)}, u32[]{:S(2)}) %collective-permute-start.19) | collective-permute-done | bytes 262176 | tf_op jit(solution)/shard_map/ppermute | solution.py:301
  79.3 1.0 %shard_map.133 = (f32[512,256]{1,0:T(8,128)}, bf16[512,512]{1,0:T(8,128)(2,1)}) custom-call(f32[512,256]{1,0:T(8,128)S(1)} %get-tuple-element.34.sums, f32[8,256]{1,0:T(8,128)S(1)} %get-tuple-element.35.decays, bf16[512,256]{1,0:T(8,128)(2,1)S(1)} %get-tuple-element.58.carried, bf16[256,512]{1,0:T(8,128)(2,1)S(1)} %get-tuple-element.47.own.after.head, ...), custom_call_target="tpu_custom_call" | custom-call | tf_op jit(solution)/shard_map/pallas_call | solution.py:27
  80.4 2.2 %collective-permute-done.21 = bf16[256,512]{1,0:T(8,128)(2,1)S(1)} collective-permute-done((bf16[256,512]{1,0:T(8,128)(2,1)S(1)}, bf16[256,512]{1,0:T(8,128)(2,1)S(1)}, u32[]{:S(2)}, u32[]{:S(2)}) %collective-permute-start.21) | collective-permute-done | bytes 262176 | tf_op jit(solution)/shard_map/ppermute | solution.py:301
  82.5 0.1 add_convert_fusion
  82.7 0.8 pad_maximum_fusion
  (19 shorter events, 0.1 us)
Async XLA Ops:
  0.6 1.2 %copy-start = (bf16[512,4,256]{2,1,0:T(4,128)(2,1)S(1)}, bf16[512,4,256]{2,1,0:T(4,128)(2,1)}, u32[]{:S(2)}) copy-start(bf16[512,4,256]{2,1,0:T(4,128)(2,1)} %param.13) | copy-start | bytes 3145732
  0.6 2.0 %copy-start.2 = (bf16[512,512]{1,0:T(8,128)(2,1)S(1)}, bf16[512,512]{1,0:T(8,128)(2,1)}, u32[]{:S(2)}) copy-start(bf16[512,512]{1,0:T(8,128)(2,1)} %grad_hbm.3) | copy-start | bytes 1572868
  1.9 16.7 %copy-start.8 = (f32[8]{0:T(128)S(1)}, f32[8]{0:T(128)}, u32[]{:S(2)}) copy-start(f32[8]{0:T(128)} %skips.1) | copy-start | bytes 100
  2.4 16.2 %copy-start.3 = (bf16[512,512]{1,0:T(8,128)(2,1)S(1)}, bf16[512,512]{1,0:T(8,128)(2,1)}, u32[]{:S(2)}) copy-start(bf16[512,512]{1,0:T(8,128)(2,1)} %conv_hbm.1) | copy-start | bytes 1572868
  2.4 16.2 %copy-start.4 = (f32[8,64,256]{2,1,0:T(8,128)S(1)}, f32[8,64,256]{2,1,0:T(8,128)}, u32[]{:S(2)}) copy-start(f32[8,64,256]{2,1,0:T(8,128)} %param.18) | copy-start | bytes 1572868
  2.4 16.2 %copy-start.6 = (f32[8,512]{1,0:T(8,128)S(1)}, f32[8,512]{1,0:T(8,128)}, u32[]{:S(2)}) copy-start(f32[8,512]{1,0:T(8,128)} %step_hbm.1) | copy-start | bytes 49156
  2.6 0.8 copy-start.7
  3.4 31.9 %copy-start.5 = (f32[4,512]{1,0:T(4,128)S(1)}, f32[4,512]{1,0:T(4,128)}, u32[]{:S(2)}) copy-start(f32[4,512]{1,0:T(4,128)} %taps.3) | copy-start | bytes 24580
  5.3 7.0 %collective-permute-start = (bf16[136,256]{1,0:T(8,128)(2,1)S(1)}, bf16[136,256]{1,0:T(8,128)(2,1)S(1)}, u32[]{:S(2)}, u32[]{:S(2)}) collective-permute-start(bf16[136,256]{1,0:T(8,128)(2,1)S(1)} %get-tuple-element.36), channel_id=1, source_target_pairs={{0,16},{16,0},{32,48},{48,32},{64,80},{80,64},{96,112},{112,96},{1... | collective-permute-start | bytes 208904 | tf_op jit(solution)/shard_map/ppermute | solution.py:301
  8.6 3.7 %collective-permute-start.1 = (bf16[136,256]{1,0:T(8,128)(2,1)S(1)}, bf16[136,256]{1,0:T(8,128)(2,1)S(1)}, u32[]{:S(2)}, u32[]{:S(2)}) collective-permute-start(bf16[136,256]{1,0:T(8,128)(2,1)S(1)} %get-tuple-element.37), channel_id=1, source_target_pairs={{0,32},{16,48},{32,0},{48,16},{64,96},{80,112},{96,64},{112,80},{1... | collective-permute-start | bytes 208904 | tf_op jit(solution)/shard_map/ppermute | solution.py:301
  8.6 5.4 %collective-permute-start.2 = (bf16[136,256]{1,0:T(8,128)(2,1)S(1)}, bf16[136,256]{1,0:T(8,128)(2,1)S(1)}, u32[]{:S(2)}, u32[]{:S(2)}) collective-permute-start(bf16[136,256]{1,0:T(8,128)(2,1)S(1)} %get-tuple-element.38), channel_id=1, source_target_pairs={{0,48},{16,32},{32,16},{48,0},{64,112},{80,96},{96,80},{112,64},{1... | collective-permute-start | bytes 208904 | tf_op jit(solution)/shard_map/ppermute | solution.py:301
  10.3 39.1 %copy-start.1 = (bf16[2048,2048]{1,0:T(8,128)(2,1)S(1)}, bf16[2048,2048]{1,0:T(8,128)(2,1)}, u32[]{:S(2)}) copy-start(bf16[2048,2048]{1,0:T(8,128)(2,1)} %weight.11) | copy-start | bytes 25165828
  14.7 9.4 %collective-permute-start.3 = (bf16[136,256]{1,0:T(8,128)(2,1)S(1)}, bf16[136,256]{1,0:T(8,128)(2,1)S(1)}, u32[]{:S(2)}, u32[]{:S(2)}) collective-permute-start(bf16[136,256]{1,0:T(8,128)(2,1)S(1)} %shard_map.122.after), channel_id=1, source_target_pairs={{128,0},{144,16},{160,32},{176,48},{192,64},{208,80},{224,96},{240... | collective-permute-start | bytes 208904 | tf_op jit(solution)/shard_map/ppermute | solution.py:296
  16.0 9.7 %collective-permute-start.4 = (bf16[136,256]{1,0:T(8,128)(2,1)S(1)}, bf16[136,256]{1,0:T(8,128)(2,1)S(1)}, u32[]{:S(2)}, u32[]{:S(2)}) collective-permute-start(bf16[136,256]{1,0:T(8,128)(2,1)S(1)} %shard_map.122.after), channel_id=1, source_target_pairs={{64,0},{80,16},{96,32},{112,48},{128,64},{144,80},{160,96},{176,11... | collective-permute-start | bytes 208904 | tf_op jit(solution)/shard_map/ppermute | solution.py:296
  17.3 9.9 %collective-permute-start.5 = (bf16[136,256]{1,0:T(8,128)(2,1)S(1)}, bf16[136,256]{1,0:T(8,128)(2,1)S(1)}, u32[]{:S(2)}, u32[]{:S(2)}) collective-permute-start(bf16[136,256]{1,0:T(8,128)(2,1)S(1)} %shard_map.122.after), channel_id=1, source_target_pairs={{192,0},{208,16},{224,32},{240,48},{193,1},{209,17},{225,33},{241,... | collective-permute-start | bytes 208904 | tf_op jit(solution)/shard_map/ppermute | solution.py:296
  27.8 3.5 %collective-permute-start.6 = (bf16[8,16,256]{2,1,0:T(8,128)(2,1)S(1)}, bf16[8,16,256]{2,1,0:T(8,128)(2,1)S(1)}, u32[]{:S(2)}, u32[]{:S(2)}) collective-permute-start(bf16[8,16,256]{2,1,0:T(8,128)(2,1)S(1)} %get-tuple-element.42), channel_id=1, source_target_pairs={{0,16},{16,0},{32,48},{48,32},{64,80},{80,64},{96,112},{112,96},{1... | collective-permute-start | bytes 196616 | tf_op jit(solution)/shard_map/ppermute | solution.py:301
  29.5 4.1 %collective-permute-start.7 = (bf16[8,16,256]{2,1,0:T(8,128)(2,1)S(1)}, bf16[8,16,256]{2,1,0:T(8,128)(2,1)S(1)}, u32[]{:S(2)}, u32[]{:S(2)}) collective-permute-start(bf16[8,16,256]{2,1,0:T(8,128)(2,1)S(1)} %get-tuple-element.43), channel_id=1, source_target_pairs={{0,32},{16,48},{32,0},{48,16},{64,96},{80,112},{96,64},{112,80},{1... | collective-permute-start | bytes 196616 | tf_op jit(solution)/shard_map/ppermute | solution.py:301
  31.3 4.1 %collective-permute-start.8 = (bf16[8,16,256]{2,1,0:T(8,128)(2,1)S(1)}, bf16[8,16,256]{2,1,0:T(8,128)(2,1)S(1)}, u32[]{:S(2)}, u32[]{:S(2)}) collective-permute-start(bf16[8,16,256]{2,1,0:T(8,128)(2,1)S(1)} %get-tuple-element.44), channel_id=1, source_target_pairs={{0,48},{16,32},{32,16},{48,0},{64,112},{80,96},{96,80},{112,64},{1... | collective-permute-start | bytes 196616 | tf_op jit(solution)/shard_map/ppermute | solution.py:301
  36.5 6.2 %collective-permute-start.15 = (bf16[16,512]{1,0:T(8,128)(2,1)S(1)}, bf16[16,512]{1,0:T(8,128)(2,1)S(1)}, u32[]{:S(2)}, u32[]{:S(2)}) collective-permute-start(bf16[16,512]{1,0:T(8,128)(2,1)S(1)} %get-tuple-element.53), channel_id=1, source_target_pairs={{16,0},{32,16},{48,32},{64,48},{80,64},{96,80},{112,96},{128,112},... | collective-permute-start | bytes 49160 | tf_op jit(solution)/shard_map/ppermute | solution.py:296
  38.8 9.6 %collective-permute-start.10 = (bf16[256,512]{1,0:T(8,128)(2,1)S(1)}, bf16[256,512]{1,0:T(8,128)(2,1)S(1)}, u32[]{:S(2)}, u32[]{:S(2)}) collective-permute-start(bf16[256,512]{1,0:T(8,128)(2,1)S(1)} %get-tuple-element.47.own.after.head), channel_id=1, source_target_pairs={{0,3},{1,2},{2,1},{3,0},{4,7},{5,6},{6,5},{7,4},{8,11},{9,10},{10,... | collective-permute-start | bytes 786440 | tf_op jit(solution)/shard_map/ppermute | solution.py:301
  40.9 8.6 %collective-permute-start.11 = (bf16[256,512]{1,0:T(8,128)(2,1)S(1)}, bf16[256,512]{1,0:T(8,128)(2,1)S(1)}, u32[]{:S(2)}, u32[]{:S(2)}) collective-permute-start(bf16[256,512]{1,0:T(8,128)(2,1)S(1)} %get-tuple-element.47.own.after.head), channel_id=1, source_target_pairs={{0,1},{1,0},{2,3},{3,2},{4,5},{5,4},{6,7},{7,6},{8,9},{9,8},{10,11... | collective-permute-start | bytes 786440 | tf_op jit(solution)/shard_map/ppermute | solution.py:301
  40.9 14.3 %collective-permute-start.9 = (bf16[256,512]{1,0:T(8,128)(2,1)S(1)}, bf16[256,512]{1,0:T(8,128)(2,1)S(1)}, u32[]{:S(2)}, u32[]{:S(2)}) collective-permute-start(bf16[256,512]{1,0:T(8,128)(2,1)S(1)} %get-tuple-element.47.own.after.head), channel_id=1, source_target_pairs={{0,2},{1,3},{2,0},{3,1},{4,6},{5,7},{6,4},{7,5},{8,10},{9,11},{10,... | collective-permute-start | bytes 786440 | tf_op jit(solution)/shard_map/ppermute | solution.py:301
  43.2 16.3 %collective-permute-start.17 = (bf16[256,512]{1,0:T(8,128)(2,1)S(1)}, bf16[256,512]{1,0:T(8,128)(2,1)S(1)}, u32[]{:S(2)}, u32[]{:S(2)}) collective-permute-start(bf16[256,512]{1,0:T(8,128)(2,1)S(1)} %shard_map.129.own.last), channel_id=1, source_target_pairs={{0,3},{1,2},{2,1},{3,0},{4,7},{5,6},{6,5},{7,4},{8,11},{9,10},{10,... | collective-permute-start | bytes 786440 | tf_op jit(solution)/shard_map/ppermute | solution.py:301
  45.2 16.5 %collective-permute-start.18 = (bf16[256,512]{1,0:T(8,128)(2,1)S(1)}, bf16[256,512]{1,0:T(8,128)(2,1)S(1)}, u32[]{:S(2)}, u32[]{:S(2)}) collective-permute-start(bf16[256,512]{1,0:T(8,128)(2,1)S(1)} %shard_map.129.own.last), channel_id=1, source_target_pairs={{0,1},{1,0},{2,3},{3,2},{4,5},{5,4},{6,7},{7,6},{8,9},{9,8},{10,11... | collective-permute-start | bytes 786440 | tf_op jit(solution)/shard_map/ppermute | solution.py:301
  48.4 18.0 %collective-permute-start.16 = (bf16[256,512]{1,0:T(8,128)(2,1)S(1)}, bf16[256,512]{1,0:T(8,128)(2,1)S(1)}, u32[]{:S(2)}, u32[]{:S(2)}) collective-permute-start(bf16[256,512]{1,0:T(8,128)(2,1)S(1)} %shard_map.129.own.last), channel_id=1, source_target_pairs={{0,2},{1,3},{2,0},{3,1},{4,6},{5,7},{6,4},{7,5},{8,10},{9,11},{10,... | collective-permute-start | bytes 786440 | tf_op jit(solution)/shard_map/ppermute | solution.py:301
  56.2 14.6 %collective-permute-start.12 = (bf16[256,512]{1,0:T(8,128)(2,1)S(1)}, bf16[256,512]{1,0:T(8,128)(2,1)S(1)}, u32[]{:S(2)}, u32[]{:S(2)}) collective-permute-start(bf16[256,512]{1,0:T(8,128)(2,1)S(1)} %get-tuple-element.49), channel_id=1, source_target_pairs={{0,12},{4,8},{8,4},{12,0},{1,13},{5,9},{9,5},{13,1},{2,14},{6,10},... | collective-permute-start | bytes 786440 | tf_op jit(solution)/shard_map/ppermute | solution.py:301
  58.5 14.0 %collective-permute-start.13 = (bf16[256,512]{1,0:T(8,128)(2,1)S(1)}, bf16[256,512]{1,0:T(8,128)(2,1)S(1)}, u32[]{:S(2)}, u32[]{:S(2)}) collective-permute-start(bf16[256,512]{1,0:T(8,128)(2,1)S(1)} %get-tuple-element.50), channel_id=1, source_target_pairs={{0,4},{4,0},{8,12},{12,8},{1,5},{5,1},{9,13},{13,9},{2,6},{6,2},{1... | collective-permute-start | bytes 786440 | tf_op jit(solution)/shard_map/ppermute | solution.py:301
  59.5 13.0 %collective-permute-start.14 = (bf16[256,512]{1,0:T(8,128)(2,1)S(1)}, bf16[256,512]{1,0:T(8,128)(2,1)S(1)}, u32[]{:S(2)}, u32[]{:S(2)}) collective-permute-start(bf16[256,512]{1,0:T(8,128)(2,1)S(1)} %get-tuple-element.51), channel_id=1, source_target_pairs={{0,8},{4,12},{8,0},{12,4},{1,9},{5,13},{9,1},{13,5},{2,10},{6,14},... | collective-permute-start | bytes 786440 | tf_op jit(solution)/shard_map/ppermute | solution.py:301
  67.4 11.9 %collective-permute-start.19 = (bf16[256,512]{1,0:T(8,128)(2,1)S(1)}, bf16[256,512]{1,0:T(8,128)(2,1)S(1)}, u32[]{:S(2)}, u32[]{:S(2)}) collective-permute-start(bf16[256,512]{1,0:T(8,128)(2,1)S(1)} %get-tuple-element.55), channel_id=1, source_target_pairs={{0,12},{4,8},{8,4},{12,0},{1,13},{5,9},{9,5},{13,1},{2,14},{6,10},... | collective-permute-start | bytes 786440 | tf_op jit(solution)/shard_map/ppermute | solution.py:301
  69.7 10.7 %collective-permute-start.20 = (bf16[256,512]{1,0:T(8,128)(2,1)S(1)}, bf16[256,512]{1,0:T(8,128)(2,1)S(1)}, u32[]{:S(2)}, u32[]{:S(2)}) collective-permute-start(bf16[256,512]{1,0:T(8,128)(2,1)S(1)} %get-tuple-element.56), channel_id=1, source_target_pairs={{0,4},{4,0},{8,12},{12,8},{1,5},{5,1},{9,13},{13,9},{2,6},{6,2},{1... | collective-permute-start | bytes 786440 | tf_op jit(solution)/shard_map/ppermute | solution.py:301
  70.8 11.8 %collective-permute-start.21 = (bf16[256,512]{1,0:T(8,128)(2,1)S(1)}, bf16[256,512]{1,0:T(8,128)(2,1)S(1)}, u32[]{:S(2)}, u32[]{:S(2)}) collective-permute-start(bf16[256,512]{1,0:T(8,128)(2,1)S(1)} %get-tuple-element.57), channel_id=1, source_target_pairs={{0,8},{4,12},{8,0},{12,4},{1,9},{5,13},{9,1},{13,5},{2,10},{6,14},... | collective-permute-start | bytes 786440 | tf_op jit(solution)/shard_map/ppermute | solution.py:301

commit v6 on v5

--- a/solution.py
+++ b/solution.py
@@ -241,7 +241,7 @@
         writes[...], carried[...], (((1,), (1,)), ((), ())), preferred_element_type=F32
     )
     rounded = (fixed[...] + slope[...] * inter).astype(BF16)
-    rim[...] = rounded[:16]
+    rim[...] = rounded[:8]
     rest[...] = rounded[count:]
     pre[...] = rounded[: count + 16].astype(F32)
     chunk[...] = taps_sum(pre, taps, 0, count)
@@ -367,7 +367,7 @@
     blocks = [struct((count, width), BF16) for count in (FIRST, tokens - FIRST)]
     head, rim, rest, carried = call(
         join_kernel,
-        (blocks[0], struct((16, width), BF16), blocks[1], struct((width, states), BF16)),
+        (blocks[0], struct((8, width), BF16), blocks[1], struct((width, states), BF16)),
         (where, own, *parts, writes, fixed, slope, conv_weight),
         specs=(SMEM,),
         scratch=(pltpu.VMEM((FIRST + 16, width), F32),),
@@ -376,7 +376,7 @@
         tail_kernel,
         blocks[1],
         (rest, earlier(rim, 1), conv_weight),
-        scratch=(pltpu.VMEM((tokens - FIRST + 16, width), F32),),
+        scratch=(pltpu.VMEM((tokens - FIRST + 8, width), F32),),
     )
     sums_of, after = [], head
     for chunk in (head, last):

time: 83.7 us -> 83.7 us (level)
  no operation moved by 1% of the time
where the time goes in v6:
time: 83.7 us; the launch traced here: 83.5 us
  starting transfers between devices  30.3 us (36%)
  waiting for transfers between devices  28.4 us (34%)
  Pallas kernels  18.1 us (22%)
  local copies, waits for them, and re-layouts  4.57 us (5%)
  other arithmetic  1.18 us (1%)
  between operations  0.95 us (1%)
    ppermute x18, starting transfers between devices, swapped(): lax.ppermute(value, axis, [(place, place ^ flip) for place in range(count)])  24.2 us
    ppermute x18, waiting for transfers between devices, swapped(): lax.ppermute(value, axis, [(place, place ^ flip) for place in range(count)])  23.3 us
    pallas_call x13, Pallas kernels, call(): pl.pallas_call(kernel, out_shape=outs, in_specs=list(specs) + [VMEM] * (l...  18.1 us
    ppermute x4, starting transfers between devices, earlier(): lax.ppermute(value, 'ctx', [(place, place - steps) for place in range(ste...  6.15 us
    ppermute x4, waiting for transfers between devices, earlier(): lax.ppermute(value, 'ctx', [(place, place - steps) for place in range(ste...  5.1 us
    unnamed x20, local copies, waits for them, and re-layouts  2.11 us
    dynamic_slice x1, local copies, waits for them, and re-layouts, on_device(): writes = lax.dynamic_index_in_dim(input_mix, group, 1, keepdims=False)  1.92 us
  transfers between devices with their start and end apart: 22, of which 11 were waited for; matrix products, arithmetic and copies ran while one was open for 3% of the time, Pallas kernels for 16%

profile of v6, /device:TPU:1, one launch (start us, length us, event | category | flops | bytes accessed | tf_op | source)
XLA Modules:
  0.0 83.5 jit_solution(9729257640797333058)
XLA Ops:
  0.6 0.0 copy-start
  0.7 1.2 %copy-done = bf16[512,4,256]{2,1,0:T(4,128)(2,1)S(1)} copy-done((bf16[512,4,256]{2,1,0:T(4,128)(2,1)S(1)}, bf16[512,4,256]{2,1,0:T(4,128)(2,1)}, u32[]{:S(2)}) %copy-start) | copy-done | bytes 1048600
  1.9 0.5 constant_dynamic-slice_fusion.1
  2.4 0.0 copy-start.3
  2.4 0.0 copy-start.4
  2.4 0.0 copy-start.6
  2.5 0.1 pad_add_fusion.where
  2.6 0.8 copy-done.7
  3.4 1.9 %shard_map.121 = (f32[512,256]{1,0:T(8,128)S(1)}, f32[8,512]{1,0:T(8,128)S(1)}, f32[8,256]{1,0:T(8,128)S(1)}, bf16[136,256]{1,0:T(8,128)(2,1)S(1)}, bf16[136,256...) custom-call(s32[4]{0:T(128)S(1)} %pad_add_fusion.where, bf16[512,512]{1,0:T(8,128)(2,1)S(1)} %copy-done.2, ...), custom_call_target="tpu_custom_call" | custom-call | tf_op jit(solution)/shard_map/pallas_call | solution.py:27
  5.3 3.3 %collective-permute-start = (bf16[136,256]{1,0:T(8,128)(2,1)S(1)}, bf16[136,256]{1,0:T(8,128)(2,1)S(1)}, u32[]{:S(2)}, u32[]{:S(2)}) collective-permute-start(bf16[136,256]{1,0:T(8,128)(2,1)S(1)} %get-tuple-element.36), channel_id=1, source_target_pairs={{0,16},{16,0},{32,48},{48,32},{64,80},{80,64},{96,112},{112,96},{1... | collective-permute-start | bytes 208904 | tf_op jit(solution)/shard_map/ppermute | solution.py:301
  8.6 0.0 collective-permute-start.1
  8.6 1.7 %collective-permute-start.2 = (bf16[136,256]{1,0:T(8,128)(2,1)S(1)}, bf16[136,256]{1,0:T(8,128)(2,1)S(1)}, u32[]{:S(2)}, u32[]{:S(2)}) collective-permute-start(bf16[136,256]{1,0:T(8,128)(2,1)S(1)} %get-tuple-element.38), channel_id=1, source_target_pairs={{0,48},{16,32},{32,16},{48,0},{64,112},{80,96},{96,80},{112,64},{1... | collective-permute-start | bytes 208904 | tf_op jit(solution)/shard_map/ppermute | solution.py:301
  10.3 1.9 %constant_dynamic-slice_fusion = bf16[512,1,256]{2,1,0:T(2,128)(2,1)S(1)} fusion(bf16[512,4,256]{2,1,0:T(4,128)(2,1)} %param.12, s32[]{:T(128)S(6)} %select_n.22), kind=kLoop, calls=%fused_computation.6 | loop fusion | bytes 524292 | tf_op jit(solution)/shard_map/jit(dynamic_index_in_dim)/dynamic_slice | solution.py:316
  12.3 0.0 collective-permute-done.one
  12.3 0.0 collective-permute-done.1.two
  12.4 1.7 %collective-permute-done.2.three = bf16[136,256]{1,0:T(8,128)(2,1)S(1)} collective-permute-done((bf16[136,256]{1,0:T(8,128)(2,1)S(1)}, bf16[136,256]{1,0:T(8,128)(2,1)S(1)}, u32[]{:S(2)}, u32[]{:S(2)}) %collective-permute-start.2) | collective-permute-done | bytes 69664 | tf_op jit(solution)/shard_map/ppermute | solution.py:301
  14.0 0.6 shard_map.122.after
  14.7 1.3 %collective-permute-start.3 = (bf16[136,256]{1,0:T(8,128)(2,1)S(1)}, bf16[136,256]{1,0:T(8,128)(2,1)S(1)}, u32[]{:S(2)}, u32[]{:S(2)}) collective-permute-start(bf16[136,256]{1,0:T(8,128)(2,1)S(1)} %shard_map.122.after), channel_id=1, source_target_pairs={{128,0},{144,16},{160,32},{176,48},{192,64},{208,80},{224,96},{240... | collective-permute-start | bytes 208904 | tf_op jit(solution)/shard_map/ppermute | solution.py:296
  16.0 1.3 %collective-permute-start.4 = (bf16[136,256]{1,0:T(8,128)(2,1)S(1)}, bf16[136,256]{1,0:T(8,128)(2,1)S(1)}, u32[]{:S(2)}, u32[]{:S(2)}) collective-permute-start(bf16[136,256]{1,0:T(8,128)(2,1)S(1)} %shard_map.122.after), channel_id=1, source_target_pairs={{64,0},{80,16},{96,32},{112,48},{128,64},{144,80},{160,96},{176,11... | collective-permute-start | bytes 208904 | tf_op jit(solution)/shard_map/ppermute | solution.py:296
  17.3 1.3 %collective-permute-start.5 = (bf16[136,256]{1,0:T(8,128)(2,1)S(1)}, bf16[136,256]{1,0:T(8,128)(2,1)S(1)}, u32[]{:S(2)}, u32[]{:S(2)}) collective-permute-start(bf16[136,256]{1,0:T(8,128)(2,1)S(1)} %shard_map.122.after), channel_id=1, source_target_pairs={{192,0},{208,16},{224,32},{240,48},{193,1},{209,17},{225,33},{241,... | collective-permute-start | bytes 208904 | tf_op jit(solution)/shard_map/ppermute | solution.py:296
  18.6 3.4 %shard_map.123 = (f32[512,512]{1,0:T(8,128)S(1)}, f32[512,512]{1,0:T(8,128)S(1)}, f32[8,16,256]{2,1,0:T(8,128)S(1)}) custom-call(s32[4]{0:T(128)S(1)} %pad_add_fusion.where, f32[8]{0:T(128)S(1)} %copy-done.8, bf16[512,512]{1,0:T(8,128)(2,1)S(1)} %copy-done.2, bf16[512,512]{1,0:T(8,128)(2,1)S(1)} %copy-done.3, f32[8,512]{1,0:T(8,128)S(1)} %copy-done.6, ...), custom_call_target="tpu_custom_call" | custom-call | tf_op jit(solution)/shard_map/pallas_call | solution.py:27
  22.0 2.0 %collective-permute-done.3.middle = bf16[136,256]{1,0:T(8,128)(2,1)S(1)} collective-permute-done((bf16[136,256]{1,0:T(8,128)(2,1)S(1)}, bf16[136,256]{1,0:T(8,128)(2,1)S(1)}, u32[]{:S(2)}, u32[]{:S(2)}) %collective-permute-start.3) | collective-permute-done | bytes 69664 | tf_op jit(solution)/shard_map/ppermute | solution.py:296
  24.0 1.6 %collective-permute-done.4.near = bf16[136,256]{1,0:T(8,128)(2,1)S(1)} collective-permute-done((bf16[136,256]{1,0:T(8,128)(2,1)S(1)}, bf16[136,256]{1,0:T(8,128)(2,1)S(1)}, u32[]{:S(2)}, u32[]{:S(2)}) %collective-permute-start.4) | collective-permute-done | bytes 69664 | tf_op jit(solution)/shard_map/ppermute | solution.py:296
  25.6 1.5 %collective-permute-done.5.far = bf16[136,256]{1,0:T(8,128)(2,1)S(1)} collective-permute-done((bf16[136,256]{1,0:T(8,128)(2,1)S(1)}, bf16[136,256]{1,0:T(8,128)(2,1)S(1)}, u32[]{:S(2)}, u32[]{:S(2)}) %collective-permute-start.5) | collective-permute-done | bytes 69664 | tf_op jit(solution)/shard_map/ppermute | solution.py:296
  27.1 0.7 shard_map.124
  27.8 1.7 %collective-permute-start.6 = (bf16[8,16,256]{2,1,0:T(8,128)(2,1)S(1)}, bf16[8,16,256]{2,1,0:T(8,128)(2,1)S(1)}, u32[]{:S(2)}, u32[]{:S(2)}) collective-permute-start(bf16[8,16,256]{2,1,0:T(8,128)(2,1)S(1)} %get-tuple-element.42), channel_id=1, source_target_pairs={{0,16},{16,0},{32,48},{48,32},{64,80},{80,64},{96,112},{112,96},{1... | collective-permute-start | bytes 196616 | tf_op jit(solution)/shard_map/ppermute | solution.py:301
  29.5 1.7 %collective-permute-start.7 = (bf16[8,16,256]{2,1,0:T(8,128)(2,1)S(1)}, bf16[8,16,256]{2,1,0:T(8,128)(2,1)S(1)}, u32[]{:S(2)}, u32[]{:S(2)}) collective-permute-start(bf16[8,16,256]{2,1,0:T(8,128)(2,1)S(1)} %get-tuple-element.43), channel_id=1, source_target_pairs={{0,32},{16,48},{32,0},{48,16},{64,96},{80,112},{96,64},{112,80},{1... | collective-permute-start | bytes 196616 | tf_op jit(solution)/shard_map/ppermute | solution.py:301
  31.3 0.1 collective-permute-start.8
  31.4 0.0 collective-permute-done.6.first
  31.4 2.3 %collective-permute-done.7.second = bf16[8,16,256]{2,1,0:T(8,128)(2,1)S(1)} collective-permute-done((bf16[8,16,256]{2,1,0:T(8,128)(2,1)S(1)}, bf16[8,16,256]{2,1,0:T(8,128)(2,1)S(1)}, u32[]{:S(2)}, u32[]{:S(2)}) %collective-permute-start.7) | collective-permute-done | bytes 65568 | tf_op jit(solution)/shard_map/ppermute | solution.py:301
  33.6 1.7 %collective-permute-done.8.third = bf16[8,16,256]{2,1,0:T(8,128)(2,1)S(1)} collective-permute-done((bf16[8,16,256]{2,1,0:T(8,128)(2,1)S(1)}, bf16[8,16,256]{2,1,0:T(8,128)(2,1)S(1)}, u32[]{:S(2)}, u32[]{:S(2)}) %collective-permute-start.8) | collective-permute-done | bytes 65568 | tf_op jit(solution)/shard_map/ppermute | solution.py:301
  35.4 1.2 %shard_map.125 = (bf16[256,512]{1,0:T(8,128)(2,1)S(1)}, bf16[8,512]{1,0:T(8,128)(2,1)S(1)}, bf16[256,512]{1,0:T(8,128)(2,1)S(1)}, bf16[512,256]{1,0:T(8,128)(2,1)S(1)}) custom-call(s32[4]{0:T(128)S(1)} %pad_add_fusion.where, bf16[8,16,256]{2,1,0:T(8,128)(2,1)S(1)} %get-tuple-element.41.own, bf16[8,16,256]{2,1,0:T(8,128)(2,1)S(1)} %collective-permute-done.6.first, ...), custom_call_target="tpu_custom_call" | custom-call | tf_op jit(solution)/shard_map/pallas_call | solution.py:27
  36.5 2.3 %collective-permute-start.15 = (bf16[8,512]{1,0:T(8,128)(2,1)S(1)}, bf16[8,512]{1,0:T(8,128)(2,1)S(1)}, u32[]{:S(2)}, u32[]{:S(2)}) collective-permute-start(bf16[8,512]{1,0:T(8,128)(2,1)S(1)} %get-tuple-element.53), channel_id=1, source_target_pairs={{16,0},{32,16},{48,32},{64,48},{80,64},{96,80},{112,96},{128,112},... | collective-permute-start | bytes 24584 | tf_op jit(solution)/shard_map/ppermute | solution.py:296
  38.8 2.1 %collective-permute-start.10 = (bf16[256,512]{1,0:T(8,128)(2,1)S(1)}, bf16[256,512]{1,0:T(8,128)(2,1)S(1)}, u32[]{:S(2)}, u32[]{:S(2)}) collective-permute-start(bf16[256,512]{1,0:T(8,128)(2,1)S(1)} %get-tuple-element.47.own.after.head), channel_id=1, source_target_pairs={{0,3},{1,2},{2,1},{3,0},{4,7},{5,6},{6,5},{7,4},{8,11},{9,10},{10,... | collective-permute-start | bytes 786440 | tf_op jit(solution)/shard_map/ppermute | solution.py:301
  40.9 0.0 collective-permute-start.11
  40.9 1.9 %collective-permute-start.9 = (bf16[256,512]{1,0:T(8,128)(2,1)S(1)}, bf16[256,512]{1,0:T(8,128)(2,1)S(1)}, u32[]{:S(2)}, u32[]{:S(2)}) collective-permute-start(bf16[256,512]{1,0:T(8,128)(2,1)S(1)} %get-tuple-element.47.own.after.head), channel_id=1, source_target_pairs={{0,2},{1,3},{2,0},{3,1},{4,6},{5,7},{6,4},{7,5},{8,10},{9,11},{10,... | collective-permute-start | bytes 786440 | tf_op jit(solution)/shard_map/ppermute | solution.py:301
  42.7 0.0 collective-permute-done.15.rim
  42.8 0.4 shard_map.129.own.last
  43.2 2.1 %collective-permute-start.17 = (bf16[256,512]{1,0:T(8,128)(2,1)S(1)}, bf16[256,512]{1,0:T(8,128)(2,1)S(1)}, u32[]{:S(2)}, u32[]{:S(2)}) collective-permute-start(bf16[256,512]{1,0:T(8,128)(2,1)S(1)} %shard_map.129.own.last), channel_id=1, source_target_pairs={{0,3},{1,2},{2,1},{3,0},{4,7},{5,6},{6,5},{7,4},{8,11},{9,10},{10,... | collective-permute-start | bytes 786440 | tf_op jit(solution)/shard_map/ppermute | solution.py:301
  45.2 0.0 collective-permute-start.18
  45.2 3.2 %collective-permute-done.10.far = bf16[256,512]{1,0:T(8,128)(2,1)S(1)} collective-permute-done((bf16[256,512]{1,0:T(8,128)(2,1)S(1)}, bf16[256,512]{1,0:T(8,128)(2,1)S(1)}, u32[]{:S(2)}, u32[]{:S(2)}) %collective-permute-start.10) | collective-permute-done | bytes 262176 | tf_op jit(solution)/shard_map/ppermute | solution.py:301
  48.4 1.0 %collective-permute-start.16 = (bf16[256,512]{1,0:T(8,128)(2,1)S(1)}, bf16[256,512]{1,0:T(8,128)(2,1)S(1)}, u32[]{:S(2)}, u32[]{:S(2)}) collective-permute-start(bf16[256,512]{1,0:T(8,128)(2,1)S(1)} %shard_map.129.own.last), channel_id=1, source_target_pairs={{0,2},{1,3},{2,0},{3,1},{4,6},{5,7},{6,4},{7,5},{8,10},{9,11},{10,... | collective-permute-start | bytes 786440 | tf_op jit(solution)/shard_map/ppermute | solution.py:301
  49.5 0.0 collective-permute-done.11.near
  49.5 2.4 %shard_map.126.total = f32[256,2048]{1,0:T(8,128)S(1)} custom-call(s32[4]{0:T(128)S(1)} %pad_add_fusion.where, bf16[256,512]{1,0:T(8,128)(2,1)S(1)} %get-tuple-element.47.own.after.head, bf16[256,512]{1,0:T(8,128)(2,1)S(1)} %collective-permute-done.10.far, bf16[256,512]{1,0:T(8,128)(2,1)S(1)} %collective-permute-done.11.near, ...), custom_call_target="tpu_custom_call" | custom-call | tf_op jit(solution)/shard_map/pallas_call | solution.py:27
  51.8 3.3 %collective-permute-done.9.across = bf16[256,512]{1,0:T(8,128)(2,1)S(1)} collective-permute-done((bf16[256,512]{1,0:T(8,128)(2,1)S(1)}, bf16[256,512]{1,0:T(8,128)(2,1)S(1)}, u32[]{:S(2)}, u32[]{:S(2)}) %collective-permute-start.9) | collective-permute-done | bytes 262176 | tf_op jit(solution)/shard_map/ppermute | solution.py:301
  55.1 1.0 %shard_map.128 = (bf16[256,512]{1,0:T(8,128)(2,1)S(1)}, bf16[256,512]{1,0:T(8,128)(2,1)S(1)}) custom-call(s32[4]{0:T(128)S(1)} %pad_add_fusion.where, bf16[256,512]{1,0:T(8,128)(2,1)S(1)} %collective-permute-done.9.across, bf16[2048,2048]{1,0:T(8,128)(2,1)S(1)} %copy-done.1, f32[256,2048]{1,0:T(8,128)S(1)} %shard_map.126.total), custom_call_target="tpu_custom_call" | custom-call | tf_op jit(solution)/shard_map/pallas_call | solution.py:27
  56.2 2.3 %collective-permute-start.12 = (bf16[256,512]{1,0:T(8,128)(2,1)S(1)}, bf16[256,512]{1,0:T(8,128)(2,1)S(1)}, u32[]{:S(2)}, u32[]{:S(2)}) collective-permute-start(bf16[256,512]{1,0:T(8,128)(2,1)S(1)} %get-tuple-element.49), channel_id=1, source_target_pairs={{0,12},{4,8},{8,4},{12,0},{1,13},{5,9},{9,5},{13,1},{2,14},{6,10},... | collective-permute-start | bytes 786440 | tf_op jit(solution)/shard_map/ppermute | solution.py:301
  58.5 0.0 collective-permute-start.13
  58.5 1.0 %shard_map.127 = (bf16[256,512]{1,0:T(8,128)(2,1)S(1)}, f32[256,512]{1,0:T(8,128)S(1)}) custom-call(s32[4]{0:T(128)S(1)} %pad_add_fusion.where, bf16[256,512]{1,0:T(8,128)(2,1)S(1)} %collective-permute-done.9.across, bf16[2048,2048]{1,0:T(8,128)(2,1)S(1)} %copy-done.1, f32[256,2048]{1,0:T(8,128)S(1)} %shard_map.126.total), custom_call_target="tpu_custom_call" | custom-call | tf_op jit(solution)/shard_map/pallas_call | solution.py:27
  59.5 0.0 collective-permute-done.17.far
  59.5 2.2 %collective-permute-start.14 = (bf16[256,512]{1,0:T(8,128)(2,1)S(1)}, bf16[256,512]{1,0:T(8,128)(2,1)S(1)}, u32[]{:S(2)}, u32[]{:S(2)}) collective-permute-start(bf16[256,512]{1,0:T(8,128)(2,1)S(1)} %get-tuple-element.51), channel_id=1, source_target_pairs={{0,8},{4,12},{8,0},{12,4},{1,9},{5,13},{9,1},{13,5},{2,10},{6,14},... | collective-permute-start | bytes 786440 | tf_op jit(solution)/shard_map/ppermute | solution.py:301
  61.8 2.4 %shard_map.130.total = f32[256,2048]{1,0:T(8,128)S(1)} custom-call(s32[4]{0:T(128)S(1)} %pad_add_fusion.where, bf16[256,512]{1,0:T(8,128)(2,1)S(1)} %shard_map.129.own.last, bf16[256,512]{1,0:T(8,128)(2,1)S(1)} %collective-permute-done.17.far, bf16[256,512]{1,0:T(8,128)(2,1)S(1)} %collective-permute-done.18.near, bf16[2048,2048]{1,0:T(8,128)(2,1)S(1)} %copy-done.1, ...), custom_call_target="tpu_custom_call" | custom-call | tf_op jit(solution)/shard_map/pallas_call | solution.py:27
  64.1 2.3 %collective-permute-done.16.across = bf16[256,512]{1,0:T(8,128)(2,1)S(1)} collective-permute-done((bf16[256,512]{1,0:T(8,128)(2,1)S(1)}, bf16[256,512]{1,0:T(8,128)(2,1)S(1)}, u32[]{:S(2)}, u32[]{:S(2)}) %collective-permute-start.16) | collective-permute-done | bytes 262176 | tf_op jit(solution)/shard_map/ppermute | solution.py:301
  66.4 1.0 %shard_map.132 = (bf16[256,512]{1,0:T(8,128)(2,1)S(1)}, bf16[256,512]{1,0:T(8,128)(2,1)S(1)}) custom-call(s32[4]{0:T(128)S(1)} %pad_add_fusion.where, bf16[256,512]{1,0:T(8,128)(2,1)S(1)} %collective-permute-done.16.across, bf16[2048,2048]{1,0:T(8,128)(2,1)S(1)} %copy-done.1, f32[256,2048]{1,0:T(8,128)S(1)} %shard_map.130.total), custom_call_target="tpu_custom_call" | custom-call | tf_op jit(solution)/shard_map/pallas_call | solution.py:27
  67.4 2.3 %collective-permute-start.19 = (bf16[256,512]{1,0:T(8,128)(2,1)S(1)}, bf16[256,512]{1,0:T(8,128)(2,1)S(1)}, u32[]{:S(2)}, u32[]{:S(2)}) collective-permute-start(bf16[256,512]{1,0:T(8,128)(2,1)S(1)} %get-tuple-element.55), channel_id=1, source_target_pairs={{0,12},{4,8},{8,4},{12,0},{1,13},{5,9},{9,5},{13,1},{2,14},{6,10},... | collective-permute-start | bytes 786440 | tf_op jit(solution)/shard_map/ppermute | solution.py:301
  69.7 0.0 collective-permute-start.20
  69.7 1.0 %shard_map.131 = (bf16[256,512]{1,0:T(8,128)(2,1)S(1)}, f32[256,512]{1,0:T(8,128)S(1)}) custom-call(s32[4]{0:T(128)S(1)} %pad_add_fusion.where, bf16[256,512]{1,0:T(8,128)(2,1)S(1)} %collective-permute-done.16.across, bf16[2048,2048]{1,0:T(8,128)(2,1)S(1)} %copy-done.1, f32[256,2048]{1,0:T(8,128)S(1)} %shard_map.130.total), custom_call_target="tpu_custom_call" | custom-call | tf_op jit(solution)/shard_map/pallas_call | solution.py:27
  70.8 1.7 %collective-permute-start.21 = (bf16[256,512]{1,0:T(8,128)(2,1)S(1)}, bf16[256,512]{1,0:T(8,128)(2,1)S(1)}, u32[]{:S(2)}, u32[]{:S(2)}) collective-permute-start(bf16[256,512]{1,0:T(8,128)(2,1)S(1)} %get-tuple-element.57), channel_id=1, source_target_pairs={{0,8},{4,12},{8,0},{12,4},{1,9},{5,13},{9,1},{13,5},{2,10},{6,14},... | collective-permute-start | bytes 786440 | tf_op jit(solution)/shard_map/ppermute | solution.py:301
  72.5 0.1 add_convert_fusion.1
  72.6 6.7 %collective-permute-done.19.after = bf16[256,512]{1,0:T(8,128)(2,1)S(1)} collective-permute-done((bf16[256,512]{1,0:T(8,128)(2,1)S(1)}, bf16[256,512]{1,0:T(8,128)(2,1)S(1)}, u32[]{:S(2)}, u32[]{:S(2)}) %collective-permute-start.19) | collective-permute-done | bytes 262176 | tf_op jit(solution)/shard_map/ppermute | solution.py:301
  79.3 1.0 %shard_map.133 = (f32[512,256]{1,0:T(8,128)}, bf16[512,512]{1,0:T(8,128)(2,1)}) custom-call(f32[512,256]{1,0:T(8,128)S(1)} %get-tuple-element.34.sums, f32[8,256]{1,0:T(8,128)S(1)} %get-tuple-element.35.decays, bf16[512,256]{1,0:T(8,128)(2,1)S(1)} %get-tuple-element.58.carried, bf16[256,512]{1,0:T(8,128)(2,1)S(1)} %get-tuple-element.47.own.after.head, ...), custom_call_target="tpu_custom_call" | custom-call | tf_op jit(solution)/shard_map/pallas_call | solution.py:27
  80.4 2.2 %collective-permute-done.21 = bf16[256,512]{1,0:T(8,128)(2,1)S(1)} collective-permute-done((bf16[256,512]{1,0:T(8,128)(2,1)S(1)}, bf16[256,512]{1,0:T(8,128)(2,1)S(1)}, u32[]{:S(2)}, u32[]{:S(2)}) %collective-permute-start.21) | collective-permute-done | bytes 262176 | tf_op jit(solution)/shard_map/ppermute | solution.py:301
  82.5 0.1 add_convert_fusion
  82.7 0.8 pad_maximum_fusion
  (19 shorter events, 0.1 us)
Async XLA Ops:
  0.6 1.2 %copy-start = (bf16[512,4,256]{2,1,0:T(4,128)(2,1)S(1)}, bf16[512,4,256]{2,1,0:T(4,128)(2,1)}, u32[]{:S(2)}) copy-start(bf16[512,4,256]{2,1,0:T(4,128)(2,1)} %param.13) | copy-start | bytes 3145732
  0.6 2.0 %copy-start.2 = (bf16[512,512]{1,0:T(8,128)(2,1)S(1)}, bf16[512,512]{1,0:T(8,128)(2,1)}, u32[]{:S(2)}) copy-start(bf16[512,512]{1,0:T(8,128)(2,1)} %grad_hbm.3) | copy-start | bytes 1572868
  1.9 16.7 %copy-start.8 = (f32[8]{0:T(128)S(1)}, f32[8]{0:T(128)}, u32[]{:S(2)}) copy-start(f32[8]{0:T(128)} %skips.1) | copy-start | bytes 100
  2.4 16.2 %copy-start.3 = (bf16[512,512]{1,0:T(8,128)(2,1)S(1)}, bf16[512,512]{1,0:T(8,128)(2,1)}, u32[]{:S(2)}) copy-start(bf16[512,512]{1,0:T(8,128)(2,1)} %conv_hbm.1) | copy-start | bytes 1572868
  2.4 16.2 %copy-start.4 = (f32[8,64,256]{2,1,0:T(8,128)S(1)}, f32[8,64,256]{2,1,0:T(8,128)}, u32[]{:S(2)}) copy-start(f32[8,64,256]{2,1,0:T(8,128)} %param.18) | copy-start | bytes 1572868
  2.4 16.2 %copy-start.6 = (f32[8,512]{1,0:T(8,128)S(1)}, f32[8,512]{1,0:T(8,128)}, u32[]{:S(2)}) copy-start(f32[8,512]{1,0:T(8,128)} %step_hbm.1) | copy-start | bytes 49156
  2.6 0.8 copy-start.7
  3.4 31.9 %copy-start.5 = (f32[4,512]{1,0:T(4,128)S(1)}, f32[4,512]{1,0:T(4,128)}, u32[]{:S(2)}) copy-start(f32[4,512]{1,0:T(4,128)} %taps.3) | copy-start | bytes 24580
  5.3 7.0 %collective-permute-start = (bf16[136,256]{1,0:T(8,128)(2,1)S(1)}, bf16[136,256]{1,0:T(8,128)(2,1)S(1)}, u32[]{:S(2)}, u32[]{:S(2)}) collective-permute-start(bf16[136,256]{1,0:T(8,128)(2,1)S(1)} %get-tuple-element.36), channel_id=1, source_target_pairs={{0,16},{16,0},{32,48},{48,32},{64,80},{80,64},{96,112},{112,96},{1... | collective-permute-start | bytes 208904 | tf_op jit(solution)/shard_map/ppermute | solution.py:301
  8.6 3.7 %collective-permute-start.1 = (bf16[136,256]{1,0:T(8,128)(2,1)S(1)}, bf16[136,256]{1,0:T(8,128)(2,1)S(1)}, u32[]{:S(2)}, u32[]{:S(2)}) collective-permute-start(bf16[136,256]{1,0:T(8,128)(2,1)S(1)} %get-tuple-element.37), channel_id=1, source_target_pairs={{0,32},{16,48},{32,0},{48,16},{64,96},{80,112},{96,64},{112,80},{1... | collective-permute-start | bytes 208904 | tf_op jit(solution)/shard_map/ppermute | solution.py:301
  8.6 5.4 %collective-permute-start.2 = (bf16[136,256]{1,0:T(8,128)(2,1)S(1)}, bf16[136,256]{1,0:T(8,128)(2,1)S(1)}, u32[]{:S(2)}, u32[]{:S(2)}) collective-permute-start(bf16[136,256]{1,0:T(8,128)(2,1)S(1)} %get-tuple-element.38), channel_id=1, source_target_pairs={{0,48},{16,32},{32,16},{48,0},{64,112},{80,96},{96,80},{112,64},{1... | collective-permute-start | bytes 208904 | tf_op jit(solution)/shard_map/ppermute | solution.py:301
  10.3 39.1 %copy-start.1 = (bf16[2048,2048]{1,0:T(8,128)(2,1)S(1)}, bf16[2048,2048]{1,0:T(8,128)(2,1)}, u32[]{:S(2)}) copy-start(bf16[2048,2048]{1,0:T(8,128)(2,1)} %weight.11) | copy-start | bytes 25165828
  14.7 9.4 %collective-permute-start.3 = (bf16[136,256]{1,0:T(8,128)(2,1)S(1)}, bf16[136,256]{1,0:T(8,128)(2,1)S(1)}, u32[]{:S(2)}, u32[]{:S(2)}) collective-permute-start(bf16[136,256]{1,0:T(8,128)(2,1)S(1)} %shard_map.122.after), channel_id=1, source_target_pairs={{128,0},{144,16},{160,32},{176,48},{192,64},{208,80},{224,96},{240... | collective-permute-start | bytes 208904 | tf_op jit(solution)/shard_map/ppermute | solution.py:296
  16.0 9.7 %collective-permute-start.4 = (bf16[136,256]{1,0:T(8,128)(2,1)S(1)}, bf16[136,256]{1,0:T(8,128)(2,1)S(1)}, u32[]{:S(2)}, u32[]{:S(2)}) collective-permute-start(bf16[136,256]{1,0:T(8,128)(2,1)S(1)} %shard_map.122.after), channel_id=1, source_target_pairs={{64,0},{80,16},{96,32},{112,48},{128,64},{144,80},{160,96},{176,11... | collective-permute-start | bytes 208904 | tf_op jit(solution)/shard_map/ppermute | solution.py:296
  17.3 9.9 %collective-permute-start.5 = (bf16[136,256]{1,0:T(8,128)(2,1)S(1)}, bf16[136,256]{1,0:T(8,128)(2,1)S(1)}, u32[]{:S(2)}, u32[]{:S(2)}) collective-permute-start(bf16[136,256]{1,0:T(8,128)(2,1)S(1)} %shard_map.122.after), channel_id=1, source_target_pairs={{192,0},{208,16},{224,32},{240,48},{193,1},{209,17},{225,33},{241,... | collective-permute-start | bytes 208904 | tf_op jit(solution)/shard_map/ppermute | solution.py:296
  27.8 3.5 %collective-permute-start.6 = (bf16[8,16,256]{2,1,0:T(8,128)(2,1)S(1)}, bf16[8,16,256]{2,1,0:T(8,128)(2,1)S(1)}, u32[]{:S(2)}, u32[]{:S(2)}) collective-permute-start(bf16[8,16,256]{2,1,0:T(8,128)(2,1)S(1)} %get-tuple-element.42), channel_id=1, source_target_pairs={{0,16},{16,0},{32,48},{48,32},{64,80},{80,64},{96,112},{112,96},{1... | collective-permute-start | bytes 196616 | tf_op jit(solution)/shard_map/ppermute | solution.py:301
  29.5 4.1 %collective-permute-start.7 = (bf16[8,16,256]{2,1,0:T(8,128)(2,1)S(1)}, bf16[8,16,256]{2,1,0:T(8,128)(2,1)S(1)}, u32[]{:S(2)}, u32[]{:S(2)}) collective-permute-start(bf16[8,16,256]{2,1,0:T(8,128)(2,1)S(1)} %get-tuple-element.43), channel_id=1, source_target_pairs={{0,32},{16,48},{32,0},{48,16},{64,96},{80,112},{96,64},{112,80},{1... | collective-permute-start | bytes 196616 | tf_op jit(solution)/shard_map/ppermute | solution.py:301
  31.3 4.1 %collective-permute-start.8 = (bf16[8,16,256]{2,1,0:T(8,128)(2,1)S(1)}, bf16[8,16,256]{2,1,0:T(8,128)(2,1)S(1)}, u32[]{:S(2)}, u32[]{:S(2)}) collective-permute-start(bf16[8,16,256]{2,1,0:T(8,128)(2,1)S(1)} %get-tuple-element.44), channel_id=1, source_target_pairs={{0,48},{16,32},{32,16},{48,0},{64,112},{80,96},{96,80},{112,64},{1... | collective-permute-start | bytes 196616 | tf_op jit(solution)/shard_map/ppermute | solution.py:301
  36.5 6.2 %collective-permute-start.15 = (bf16[8,512]{1,0:T(8,128)(2,1)S(1)}, bf16[8,512]{1,0:T(8,128)(2,1)S(1)}, u32[]{:S(2)}, u32[]{:S(2)}) collective-permute-start(bf16[8,512]{1,0:T(8,128)(2,1)S(1)} %get-tuple-element.53), channel_id=1, source_target_pairs={{16,0},{32,16},{48,32},{64,48},{80,64},{96,80},{112,96},{128,112},... | collective-permute-start | bytes 24584 | tf_op jit(solution)/shard_map/ppermute | solution.py:296
  38.8 9.6 %collective-permute-start.10 = (bf16[256,512]{1,0:T(8,128)(2,1)S(1)}, bf16[256,512]{1,0:T(8,128)(2,1)S(1)}, u32[]{:S(2)}, u32[]{:S(2)}) collective-permute-start(bf16[256,512]{1,0:T(8,128)(2,1)S(1)} %get-tuple-element.47.own.after.head), channel_id=1, source_target_pairs={{0,3},{1,2},{2,1},{3,0},{4,7},{5,6},{6,5},{7,4},{8,11},{9,10},{10,... | collective-permute-start | bytes 786440 | tf_op jit(solution)/shard_map/ppermute | solution.py:301
  40.9 8.6 %collective-permute-start.11 = (bf16[256,512]{1,0:T(8,128)(2,1)S(1)}, bf16[256,512]{1,0:T(8,128)(2,1)S(1)}, u32[]{:S(2)}, u32[]{:S(2)}) collective-permute-start(bf16[256,512]{1,0:T(8,128)(2,1)S(1)} %get-tuple-element.47.own.after.head), channel_id=1, source_target_pairs={{0,1},{1,0},{2,3},{3,2},{4,5},{5,4},{6,7},{7,6},{8,9},{9,8},{10,11... | collective-permute-start | bytes 786440 | tf_op jit(solution)/shard_map/ppermute | solution.py:301
  40.9 14.3 %collective-permute-start.9 = (bf16[256,512]{1,0:T(8,128)(2,1)S(1)}, bf16[256,512]{1,0:T(8,128)(2,1)S(1)}, u32[]{:S(2)}, u32[]{:S(2)}) collective-permute-start(bf16[256,512]{1,0:T(8,128)(2,1)S(1)} %get-tuple-element.47.own.after.head), channel_id=1, source_target_pairs={{0,2},{1,3},{2,0},{3,1},{4,6},{5,7},{6,4},{7,5},{8,10},{9,11},{10,... | collective-permute-start | bytes 786440 | tf_op jit(solution)/shard_map/ppermute | solution.py:301
  43.2 16.3 %collective-permute-start.17 = (bf16[256,512]{1,0:T(8,128)(2,1)S(1)}, bf16[256,512]{1,0:T(8,128)(2,1)S(1)}, u32[]{:S(2)}, u32[]{:S(2)}) collective-permute-start(bf16[256,512]{1,0:T(8,128)(2,1)S(1)} %shard_map.129.own.last), channel_id=1, source_target_pairs={{0,3},{1,2},{2,1},{3,0},{4,7},{5,6},{6,5},{7,4},{8,11},{9,10},{10,... | collective-permute-start | bytes 786440 | tf_op jit(solution)/shard_map/ppermute | solution.py:301
  45.2 16.5 %collective-permute-start.18 = (bf16[256,512]{1,0:T(8,128)(2,1)S(1)}, bf16[256,512]{1,0:T(8,128)(2,1)S(1)}, u32[]{:S(2)}, u32[]{:S(2)}) collective-permute-start(bf16[256,512]{1,0:T(8,128)(2,1)S(1)} %shard_map.129.own.last), channel_id=1, source_target_pairs={{0,1},{1,0},{2,3},{3,2},{4,5},{5,4},{6,7},{7,6},{8,9},{9,8},{10,11... | collective-permute-start | bytes 786440 | tf_op jit(solution)/shard_map/ppermute | solution.py:301
  48.4 18.0 %collective-permute-start.16 = (bf16[256,512]{1,0:T(8,128)(2,1)S(1)}, bf16[256,512]{1,0:T(8,128)(2,1)S(1)}, u32[]{:S(2)}, u32[]{:S(2)}) collective-permute-start(bf16[256,512]{1,0:T(8,128)(2,1)S(1)} %shard_map.129.own.last), channel_id=1, source_target_pairs={{0,2},{1,3},{2,0},{3,1},{4,6},{5,7},{6,4},{7,5},{8,10},{9,11},{10,... | collective-permute-start | bytes 786440 | tf_op jit(solution)/shard_map/ppermute | solution.py:301
  56.2 14.6 %collective-permute-start.12 = (bf16[256,512]{1,0:T(8,128)(2,1)S(1)}, bf16[256,512]{1,0:T(8,128)(2,1)S(1)}, u32[]{:S(2)}, u32[]{:S(2)}) collective-permute-start(bf16[256,512]{1,0:T(8,128)(2,1)S(1)} %get-tuple-element.49), channel_id=1, source_target_pairs={{0,12},{4,8},{8,4},{12,0},{1,13},{5,9},{9,5},{13,1},{2,14},{6,10},... | collective-permute-start | bytes 786440 | tf_op jit(solution)/shard_map/ppermute | solution.py:301
  58.5 14.0 %collective-permute-start.13 = (bf16[256,512]{1,0:T(8,128)(2,1)S(1)}, bf16[256,512]{1,0:T(8,128)(2,1)S(1)}, u32[]{:S(2)}, u32[]{:S(2)}) collective-permute-start(bf16[256,512]{1,0:T(8,128)(2,1)S(1)} %get-tuple-element.50), channel_id=1, source_target_pairs={{0,4},{4,0},{8,12},{12,8},{1,5},{5,1},{9,13},{13,9},{2,6},{6,2},{1... | collective-permute-start | bytes 786440 | tf_op jit(solution)/shard_map/ppermute | solution.py:301
  59.5 13.0 %collective-permute-start.14 = (bf16[256,512]{1,0:T(8,128)(2,1)S(1)}, bf16[256,512]{1,0:T(8,128)(2,1)S(1)}, u32[]{:S(2)}, u32[]{:S(2)}) collective-permute-start(bf16[256,512]{1,0:T(8,128)(2,1)S(1)} %get-tuple-element.51), channel_id=1, source_target_pairs={{0,8},{4,12},{8,0},{12,4},{1,9},{5,13},{9,1},{13,5},{2,10},{6,14},... | collective-permute-start | bytes 786440 | tf_op jit(solution)/shard_map/ppermute | solution.py:301
  67.4 11.9 %collective-permute-start.19 = (bf16[256,512]{1,0:T(8,128)(2,1)S(1)}, bf16[256,512]{1,0:T(8,128)(2,1)S(1)}, u32[]{:S(2)}, u32[]{:S(2)}) collective-permute-start(bf16[256,512]{1,0:T(8,128)(2,1)S(1)} %get-tuple-element.55), channel_id=1, source_target_pairs={{0,12},{4,8},{8,4},{12,0},{1,13},{5,9},{9,5},{13,1},{2,14},{6,10},... | collective-permute-start | bytes 786440 | tf_op jit(solution)/shard_map/ppermute | solution.py:301
  69.7 10.7 %collective-permute-start.20 = (bf16[256,512]{1,0:T(8,128)(2,1)S(1)}, bf16[256,512]{1,0:T(8,128)(2,1)S(1)}, u32[]{:S(2)}, u32[]{:S(2)}) collective-permute-start(bf16[256,512]{1,0:T(8,128)(2,1)S(1)} %get-tuple-element.56), channel_id=1, source_target_pairs={{0,4},{4,0},{8,12},{12,8},{1,5},{5,1},{9,13},{13,9},{2,6},{6,2},{1... | collective-permute-start | bytes 786440 | tf_op jit(solution)/shard_map/ppermute | solution.py:301
  70.8 11.8 %collective-permute-start.21 = (bf16[256,512]{1,0:T(8,128)(2,1)S(1)}, bf16[256,512]{1,0:T(8,128)(2,1)S(1)}, u32[]{:S(2)}, u32[]{:S(2)}) collective-permute-start(bf16[256,512]{1,0:T(8,128)(2,1)S(1)} %get-tuple-element.57), channel_id=1, source_target_pairs={{0,8},{4,12},{8,0},{12,4},{1,9},{5,13},{9,1},{13,5},{2,10},{6,14},... | collective-permute-start | bytes 786440 | tf_op jit(solution)/shard_map/ppermute | solution.py:301
